TPU v7x, 32 devices: a whole 2x2x4 slice. The times are simulated.
32 devices in a mesh: row: 8 (over z, y), col: 4 (over x, core).
Axes of the slice: x: 2, y: 2, z: 4, core: 2. Of those that a mesh axis runs over, the one named last changes fastest.
Arguments:
- atmo_states: float32 [10, 12, 128, 128], P(None, None, 'row'), may hold values from -6 to 6
- remap_weights: float32 [128, 16, 128, 128], P('row', 'col'), may hold values from -0.25 to 0.25
- intersection_tiles: int32 [128, 16], P('row', 'col'), may hold values from 0 to 47, as said below
- land_mask: int32 [128, 512], P('row', 'col'), may hold values 0 or 1
- ocean_state: float32 [3, 128, 512], P(None, 'row', 'col'), may hold values from -6 to 6
Outputs:
- flux_mean: float32 [10, 128, 512], P(None, 'row', 'col')
- final_state: float32 [3, 128, 512], P(None, 'row', 'col')
Inputs may be any that keep to these rules, and one draw needn't show every extreme that they name: `intersection_tiles`: for every ocean row and block column, the first of its 4 slots names a tile of the previous row device (values below 16), the last one of the next row device (values from 32), the others of the own row device; row indices wrap around.
All inputs are finite; a program needn't handle non-finite values. No bound on the sum of `land_mask` on one device may be relied on, other than what follows from the above.
Results may differ from a plain program's by a relative error of at most 0.00017.
Values sent between devices are 32-bit elements; how exact they have to be, the bound alone decides.
No kernel may reach another device: no remote copies, remote signals or barrier semaphores. Data moves between devices by JAX's collectives and lax.ppermute only.
A program may use at most 64 MiB of HBM per device.

v0:
```python
import math

import jax
import jax.numpy as jnp
import numpy as np
from jax import lax
from jax.sharding import PartitionSpec as P

K = 12
SUB = 6


def padded_2(cells, sides, width):
    for axis, dim in sides:
        count = lax.axis_size(axis)
        head = lax.slice_in_dim(cells, 0, width, axis=dim)
        tail = lax.slice_in_dim(cells, cells.shape[dim] - width, cells.shape[dim], axis=dim)
        cells = jnp.concatenate(
            [
                lax.ppermute(tail, axis, [(i, (i + 1) % count) for i in range(count)]),
                cells,
                lax.ppermute(head, axis, [((i + 1) % count, i) for i in range(count)]),
            ],
            axis=dim,
        )
    return cells


def hermite_table(count_sub, count_levels):
    table = np.zeros((count_sub, count_levels))

    def add_slope(position_row, level, factor):
        if level == 0:
            table[position_row, 1] += factor
            table[position_row, 0] -= factor
        elif level == count_levels - 1:
            table[position_row, level] += factor
            table[position_row, level - 1] -= factor
        else:
            table[position_row, level + 1] += 0.5 * factor
            table[position_row, level - 1] -= 0.5 * factor

    for substep in range(count_sub):
        position = (substep + 0.5) * (count_levels - 1) / count_sub
        lower = min(int(math.floor(position)), count_levels - 2)
        fraction = position - lower
        table[substep, lower] += 2 * fraction**3 - 3 * fraction**2 + 1
        table[substep, lower + 1] += -2 * fraction**3 + 3 * fraction**2
        add_slope(substep, lower, fraction**3 - 2 * fraction**2 + fraction)
        add_slope(substep, lower + 1, fraction**3 - fraction**2)
    return table


def per_device(atmo_states, remap_weights, intersection_tiles, land_mask, ocean_state):
    highest = lax.Precision.HIGHEST
    table = jnp.asarray(hermite_table(SUB, K), jnp.float32)
    tiles_own = atmo_states.shape[2]
    own_flux = jnp.einsum("sk,fkta->fsta", table, atmo_states, precision=highest)
    window = padded_2(own_flux, (("row", 2),), tiles_own)
    picked = window[:, :, intersection_tiles, :]
    forcing = jnp.einsum("fsrqa,rqao->sfro", picked, remap_weights, precision=highest)
    flux_mean = jnp.mean(forcing, axis=0)
    ocean = land_mask.astype(jnp.float32)
    height, zonal, merid = (ocean_state[0], ocean_state[1], ocean_state[2])
    for substep in range(SUB):
        padded = padded_2(height, (("row", 0), ("col", 1)), 1)
        grad_x = (padded[2:, 1:-1] - padded[:-2, 1:-1]) * 0.5
        grad_y = (padded[1:-1, 2:] - padded[1:-1, :-2]) * 0.5
        zonal = ocean * (zonal - grad_x + 0.2 * merid + 0.5 * forcing[substep, 0])
        merid = ocean * (merid - grad_y - 0.2 * zonal + 0.5 * forcing[substep, 1])
        currents = padded_2(jnp.stack([zonal, merid]), (("row", 1), ("col", 2)), 1)
        spread = (currents[0, 2:, 1:-1] - currents[0, :-2, 1:-1]) * 0.5
        spread = spread + (currents[1, 1:-1, 2:] - currents[1, 1:-1, :-2]) * 0.5
        height = height - spread + 0.5 * forcing[substep, 2]
    return (flux_mean, jnp.stack([height, zonal, merid]))


def solution(mesh):
    placed = (
        P(None, None, "row", None),
        P("row", "col", None, None),
        P("row", "col"),
        P("row", "col"),
        P(None, "row", "col"),
    )
    return jax.shard_map(
        per_device,
        mesh=mesh,
        in_specs=placed,
        out_specs=(P(None, "row", "col"), P(None, "row", "col")),
        check_vma=False,
    )
```

profile of v0, /device:TPU:0, one launch (start us, length us, event | category | flops | bytes accessed | tf_op | source)
XLA Modules:
  0.0 153.4 jit_solution(10322030954611344846)
XLA Ops:
  4.5 3.0 %collective-permute-start = (f32[10,6,16,128]{3,2,1,0:T(8,128)S(1)}, f32[10,6,16,128]{3,2,1,0:T(8,128)S(1)}, u32[]{:S(2)}, u32[]{:S(2)}) collective-permute-start(f32[10,6,16,128]{3,2,1,0:T(8,128)S(1)} %copy.51), channel_id=1, source_target_pairs={{0,4},{4,8},{8,12},{12,16},{16,20},{20,24},{24,28},{28,0},{1,5},{5... | collective-permute-start | bytes 1474568 | tf_op jit(solution)/shard_map/ppermute | solution.py:20
  7.5 3.1 %collective-permute-start.1 = (f32[10,6,16,128]{3,2,1,0:T(8,128)S(1)}, f32[10,6,16,128]{3,2,1,0:T(8,128)S(1)}, u32[]{:S(2)}, u32[]{:S(2)}) collective-permute-start(f32[10,6,16,128]{3,2,1,0:T(8,128)S(1)} %copy.51), channel_id=1, source_target_pairs={{4,0},{8,4},{12,8},{16,12},{20,16},{24,20},{28,24},{0,28},{5,1},{9... | collective-permute-start | bytes 1474568 | tf_op jit(solution)/shard_map/ppermute | solution.py:22
  10.6 2.0 %collective-permute-start.2 = (f32[1,128]{1,0:T(1,128)S(1)}, f32[1,128]{1,0:T(1,128)S(1)}, u32[]{:S(2)}, u32[]{:S(2)}) collective-permute-start(f32[1,128]{1,0:T(1,128)S(1)} %get-tuple-element.55), channel_id=1, source_target_pairs={{4,0},{8,4},{12,8},{16,12},{20,16},{24,20},{28,24},{0,28},{5,1},{9... | collective-permute-start | bytes 1544 | tf_op jit(solution)/shard_map/ppermute | solution.py:22
  12.8 17.9 %collective-permute-done.2 = f32[1,128]{1,0:T(1,128)S(1)} collective-permute-done((f32[1,128]{1,0:T(1,128)S(1)}, f32[1,128]{1,0:T(1,128)S(1)}, u32[]{:S(2)}, u32[]{:S(2)}) %collective-permute-start.2) | collective-permute-done | bytes 544 | tf_op jit(solution)/shard_map/ppermute | solution.py:22
  31.9 2.4 %gather_fusion = f32[64,10,6,128]{3,2,1,0:T(8,128)} fusion(f32[10,6,48,128]{3,1,2,0:T(8,128)S(1)} %pad_maximum_fusion, s32[1024]{0:T(1024)S(1)} %pad_clamp_fusion), kind=kCustom, calls=%fused_computation | custom fusion | bytes 3932416 | tf_op jit(solution)/shard_map/gather | solution.py:60
  34.3 6.8 %fusion.145 = (f32[10,16,128]{2,0,1:T(8,128)S(1)}, f32[6,10,16,128]{3,0,1,2:T(8,128)S(1)}) fusion(f32[16,4,128,128]{3,2,1,0:T(8,128)} %param.7, f32[16,4,10,6,128]{4,3,2,1,0:T(8,128)} %bitcast.169), kind=kOutput, calls=%fused_computation.299 | convolution fusion | flops 755077120 | bytes 6733824 | tf_op jit(solution)/shard_map/fsrqa,rqao->sfro/dot_general | solution.py:61
  41.4 3.4 %collective-permute-start.6 = (f32[2,1,128]{2,1,0:T(1,128)S(1)}, f32[2,1,128]{2,1,0:T(1,128)S(1)}, u32[]{:S(2)}, u32[]{:S(2)}) collective-permute-start(f32[2,1,128]{2,1,0:T(1,128)S(1)} %get-tuple-element.67), channel_id=1, source_target_pairs={{4,0},{8,4},{12,8},{16,12},{20,16},{24,20},{28,24},{0,28},{5,1},{9... | collective-permute-start | bytes 3080 | tf_op jit(solution)/shard_map/ppermute | solution.py:22
  46.0 5.0 %collective-permute-done.7 = f32[2,1,128]{2,1,0:T(1,128)S(1)} collective-permute-done((f32[2,1,128]{2,1,0:T(1,128)S(1)}, f32[2,1,128]{2,1,0:T(1,128)S(1)}, u32[]{:S(2)}, u32[]{:S(2)}) %collective-permute-start.7) | collective-permute-done | bytes 1056 | tf_op jit(solution)/shard_map/ppermute | solution.py:20
  52.6 2.0 %collective-permute-done.9 = f32[2,18,1]{2,1,0:T(8,128)S(1)} collective-permute-done((f32[2,18,1]{2,1,0:T(8,128)S(1)}, f32[2,18,1]{2,1,0:T(8,128)S(1)}, u32[]{:S(2)}, u32[]{:S(2)}) %collective-permute-start.9) | collective-permute-done | bytes 176 | tf_op jit(solution)/shard_map/ppermute | solution.py:20
  54.8 2.0 %collective-permute-start.11 = (f32[1,128]{1,0:T(1,128)S(1)}, f32[1,128]{1,0:T(1,128)S(1)}, u32[]{:S(2)}, u32[]{:S(2)}) collective-permute-start(f32[1,128]{1,0:T(1,128)S(1)} %get-tuple-element.88), channel_id=1, source_target_pairs={{0,4},{4,8},{8,12},{12,16},{16,20},{20,24},{24,28},{28,0},{1,5},{5... | collective-permute-start | bytes 1544 | tf_op jit(solution)/shard_map/ppermute | solution.py:20
  58.3 2.8 %collective-permute-done.11 = f32[1,128]{1,0:T(1,128)S(1)} collective-permute-done((f32[1,128]{1,0:T(1,128)S(1)}, f32[1,128]{1,0:T(1,128)S(1)}, u32[]{:S(2)}, u32[]{:S(2)}) %collective-permute-start.11) | collective-permute-done | bytes 544 | tf_op jit(solution)/shard_map/ppermute | solution.py:20
  64.5 2.0 %collective-permute-start.15 = (f32[2,1,128]{2,1,0:T(1,128)S(1)}, f32[2,1,128]{2,1,0:T(1,128)S(1)}, u32[]{:S(2)}, u32[]{:S(2)}) collective-permute-start(f32[2,1,128]{2,1,0:T(1,128)S(1)} %get-tuple-element.64), channel_id=1, source_target_pairs={{0,4},{4,8},{8,12},{12,16},{16,20},{20,24},{24,28},{28,0},{1,5},{5... | collective-permute-start | bytes 3080 | tf_op jit(solution)/shard_map/ppermute | solution.py:20
  68.1 2.8 %collective-permute-done.15 = f32[2,1,128]{2,1,0:T(1,128)S(1)} collective-permute-done((f32[2,1,128]{2,1,0:T(1,128)S(1)}, f32[2,1,128]{2,1,0:T(1,128)S(1)}, u32[]{:S(2)}, u32[]{:S(2)}) %collective-permute-start.15) | collective-permute-done | bytes 1056 | tf_op jit(solution)/shard_map/ppermute | solution.py:20
  72.5 1.9 %collective-permute-done.17 = f32[2,18,1]{2,1,0:T(8,128)S(1)} collective-permute-done((f32[2,18,1]{2,1,0:T(8,128)S(1)}, f32[2,18,1]{2,1,0:T(8,128)S(1)}, u32[]{:S(2)}, u32[]{:S(2)}) %collective-permute-start.17) | collective-permute-done | bytes 176 | tf_op jit(solution)/shard_map/ppermute | solution.py:20
  74.5 2.0 %collective-permute-start.19 = (f32[1,128]{1,0:T(1,128)S(1)}, f32[1,128]{1,0:T(1,128)S(1)}, u32[]{:S(2)}, u32[]{:S(2)}) collective-permute-start(f32[1,128]{1,0:T(1,128)S(1)} %get-tuple-element.86), channel_id=1, source_target_pairs={{0,4},{4,8},{8,12},{12,16},{16,20},{20,24},{24,28},{28,0},{1,5},{5... | collective-permute-start | bytes 1544 | tf_op jit(solution)/shard_map/ppermute | solution.py:20
  78.1 2.8 %collective-permute-done.19 = f32[1,128]{1,0:T(1,128)S(1)} collective-permute-done((f32[1,128]{1,0:T(1,128)S(1)}, f32[1,128]{1,0:T(1,128)S(1)}, u32[]{:S(2)}, u32[]{:S(2)}) %collective-permute-start.19) | collective-permute-done | bytes 544 | tf_op jit(solution)/shard_map/ppermute | solution.py:20
  84.2 2.0 %collective-permute-start.23 = (f32[2,1,128]{2,1,0:T(1,128)S(1)}, f32[2,1,128]{2,1,0:T(1,128)S(1)}, u32[]{:S(2)}, u32[]{:S(2)}) collective-permute-start(f32[2,1,128]{2,1,0:T(1,128)S(1)} %get-tuple-element.62), channel_id=1, source_target_pairs={{0,4},{4,8},{8,12},{12,16},{16,20},{20,24},{24,28},{28,0},{1,5},{5... | collective-permute-start | bytes 3080 | tf_op jit(solution)/shard_map/ppermute | solution.py:20
  87.8 2.8 %collective-permute-done.23 = f32[2,1,128]{2,1,0:T(1,128)S(1)} collective-permute-done((f32[2,1,128]{2,1,0:T(1,128)S(1)}, f32[2,1,128]{2,1,0:T(1,128)S(1)}, u32[]{:S(2)}, u32[]{:S(2)}) %collective-permute-start.23) | collective-permute-done | bytes 1056 | tf_op jit(solution)/shard_map/ppermute | solution.py:20
  92.2 1.8 %collective-permute-done.25 = f32[2,18,1]{2,1,0:T(8,128)S(1)} collective-permute-done((f32[2,18,1]{2,1,0:T(8,128)S(1)}, f32[2,18,1]{2,1,0:T(8,128)S(1)}, u32[]{:S(2)}, u32[]{:S(2)}) %collective-permute-start.25) | collective-permute-done | bytes 176 | tf_op jit(solution)/shard_map/ppermute | solution.py:20
  94.1 2.0 %collective-permute-start.27 = (f32[1,128]{1,0:T(1,128)S(1)}, f32[1,128]{1,0:T(1,128)S(1)}, u32[]{:S(2)}, u32[]{:S(2)}) collective-permute-start(f32[1,128]{1,0:T(1,128)S(1)} %get-tuple-element.84), channel_id=1, source_target_pairs={{0,4},{4,8},{8,12},{12,16},{16,20},{20,24},{24,28},{28,0},{1,5},{5... | collective-permute-start | bytes 1544 | tf_op jit(solution)/shard_map/ppermute | solution.py:20
  97.6 2.8 %collective-permute-done.27 = f32[1,128]{1,0:T(1,128)S(1)} collective-permute-done((f32[1,128]{1,0:T(1,128)S(1)}, f32[1,128]{1,0:T(1,128)S(1)}, u32[]{:S(2)}, u32[]{:S(2)}) %collective-permute-start.27) | collective-permute-done | bytes 544 | tf_op jit(solution)/shard_map/ppermute | solution.py:20
  103.8 2.0 %collective-permute-start.31 = (f32[2,1,128]{2,1,0:T(1,128)S(1)}, f32[2,1,128]{2,1,0:T(1,128)S(1)}, u32[]{:S(2)}, u32[]{:S(2)}) collective-permute-start(f32[2,1,128]{2,1,0:T(1,128)S(1)} %get-tuple-element.60), channel_id=1, source_target_pairs={{0,4},{4,8},{8,12},{12,16},{16,20},{20,24},{24,28},{28,0},{1,5},{5... | collective-permute-start | bytes 3080 | tf_op jit(solution)/shard_map/ppermute | solution.py:20
  107.4 2.8 %collective-permute-done.31 = f32[2,1,128]{2,1,0:T(1,128)S(1)} collective-permute-done((f32[2,1,128]{2,1,0:T(1,128)S(1)}, f32[2,1,128]{2,1,0:T(1,128)S(1)}, u32[]{:S(2)}, u32[]{:S(2)}) %collective-permute-start.31) | collective-permute-done | bytes 1056 | tf_op jit(solution)/shard_map/ppermute | solution.py:20
  113.7 2.0 %collective-permute-start.35 = (f32[1,128]{1,0:T(1,128)S(1)}, f32[1,128]{1,0:T(1,128)S(1)}, u32[]{:S(2)}, u32[]{:S(2)}) collective-permute-start(f32[1,128]{1,0:T(1,128)S(1)} %get-tuple-element.82), channel_id=1, source_target_pairs={{0,4},{4,8},{8,12},{12,16},{16,20},{20,24},{24,28},{28,0},{1,5},{5... | collective-permute-start | bytes 1544 | tf_op jit(solution)/shard_map/ppermute | solution.py:20
  117.2 2.8 %collective-permute-done.35 = f32[1,128]{1,0:T(1,128)S(1)} collective-permute-done((f32[1,128]{1,0:T(1,128)S(1)}, f32[1,128]{1,0:T(1,128)S(1)}, u32[]{:S(2)}, u32[]{:S(2)}) %collective-permute-start.35) | collective-permute-done | bytes 544 | tf_op jit(solution)/shard_map/ppermute | solution.py:20
  123.4 2.0 %collective-permute-start.39 = (f32[2,1,128]{2,1,0:T(1,128)S(1)}, f32[2,1,128]{2,1,0:T(1,128)S(1)}, u32[]{:S(2)}, u32[]{:S(2)}) collective-permute-start(f32[2,1,128]{2,1,0:T(1,128)S(1)} %get-tuple-element.58), channel_id=1, source_target_pairs={{0,4},{4,8},{8,12},{12,16},{16,20},{20,24},{24,28},{28,0},{1,5},{5... | collective-permute-start | bytes 3080 | tf_op jit(solution)/shard_map/ppermute | solution.py:20
  127.0 2.8 %collective-permute-done.39 = f32[2,1,128]{2,1,0:T(1,128)S(1)} collective-permute-done((f32[2,1,128]{2,1,0:T(1,128)S(1)}, f32[2,1,128]{2,1,0:T(1,128)S(1)}, u32[]{:S(2)}, u32[]{:S(2)}) %collective-permute-start.39) | collective-permute-done | bytes 1056 | tf_op jit(solution)/shard_map/ppermute | solution.py:20
  131.3 1.8 %collective-permute-done.41 = f32[2,18,1]{2,1,0:T(8,128)S(1)} collective-permute-done((f32[2,18,1]{2,1,0:T(8,128)S(1)}, f32[2,18,1]{2,1,0:T(8,128)S(1)}, u32[]{:S(2)}, u32[]{:S(2)}) %collective-permute-start.41) | collective-permute-done | bytes 176 | tf_op jit(solution)/shard_map/ppermute | solution.py:20
  133.3 2.0 %collective-permute-start.43 = (f32[1,128]{1,0:T(1,128)S(1)}, f32[1,128]{1,0:T(1,128)S(1)}, u32[]{:S(2)}, u32[]{:S(2)}) collective-permute-start(f32[1,128]{1,0:T(1,128)S(1)} %get-tuple-element.80), channel_id=1, source_target_pairs={{0,4},{4,8},{8,12},{12,16},{16,20},{20,24},{24,28},{28,0},{1,5},{5... | collective-permute-start | bytes 1544 | tf_op jit(solution)/shard_map/ppermute | solution.py:20
  136.8 2.8 %collective-permute-done.43 = f32[1,128]{1,0:T(1,128)S(1)} collective-permute-done((f32[1,128]{1,0:T(1,128)S(1)}, f32[1,128]{1,0:T(1,128)S(1)}, u32[]{:S(2)}, u32[]{:S(2)}) %collective-permute-start.43) | collective-permute-done | bytes 544 | tf_op jit(solution)/shard_map/ppermute | solution.py:20
  143.0 2.0 %collective-permute-start.47 = (f32[2,1,128]{2,1,0:T(1,128)S(1)}, f32[2,1,128]{2,1,0:T(1,128)S(1)}, u32[]{:S(2)}, u32[]{:S(2)}) collective-permute-start(f32[2,1,128]{2,1,0:T(1,128)S(1)} %get-tuple-element.56), channel_id=1, source_target_pairs={{0,4},{4,8},{8,12},{12,16},{16,20},{20,24},{24,28},{28,0},{1,5},{5... | collective-permute-start | bytes 3080 | tf_op jit(solution)/shard_map/ppermute | solution.py:20
  146.6 2.8 %collective-permute-done.47 = f32[2,1,128]{2,1,0:T(1,128)S(1)} collective-permute-done((f32[2,1,128]{2,1,0:T(1,128)S(1)}, f32[2,1,128]{2,1,0:T(1,128)S(1)}, u32[]{:S(2)}, u32[]{:S(2)}) %collective-permute-start.47) | collective-permute-done | bytes 1056 | tf_op jit(solution)/shard_map/ppermute | solution.py:20
  (146 shorter events, 53.6 us)
Async XLA Ops:
  4.5 26.9 %collective-permute-start = (f32[10,6,16,128]{3,2,1,0:T(8,128)S(1)}, f32[10,6,16,128]{3,2,1,0:T(8,128)S(1)}, u32[]{:S(2)}, u32[]{:S(2)}) collective-permute-start(f32[10,6,16,128]{3,2,1,0:T(8,128)S(1)} %copy.51), channel_id=1, source_target_pairs={{0,4},{4,8},{8,12},{12,16},{16,20},{20,24},{24,28},{28,0},{1,5},{5... | collective-permute-start | bytes 1474568 | tf_op jit(solution)/shard_map/ppermute | solution.py:20
  7.5 24.1 %collective-permute-start.1 = (f32[10,6,16,128]{3,2,1,0:T(8,128)S(1)}, f32[10,6,16,128]{3,2,1,0:T(8,128)S(1)}, u32[]{:S(2)}, u32[]{:S(2)}) collective-permute-start(f32[10,6,16,128]{3,2,1,0:T(8,128)S(1)} %copy.51), channel_id=1, source_target_pairs={{4,0},{8,4},{12,8},{16,12},{20,16},{24,20},{28,24},{0,28},{5,1},{9... | collective-permute-start | bytes 1474568 | tf_op jit(solution)/shard_map/ppermute | solution.py:22
  10.6 20.2 %collective-permute-start.2 = (f32[1,128]{1,0:T(1,128)S(1)}, f32[1,128]{1,0:T(1,128)S(1)}, u32[]{:S(2)}, u32[]{:S(2)}) collective-permute-start(f32[1,128]{1,0:T(1,128)S(1)} %get-tuple-element.55), channel_id=1, source_target_pairs={{4,0},{8,4},{12,8},{16,12},{20,16},{24,20},{28,24},{0,28},{5,1},{9... | collective-permute-start | bytes 1544 | tf_op jit(solution)/shard_map/ppermute | solution.py:22
  12.6 18.2 %collective-permute-start.3 = (f32[1,128]{1,0:T(1,128)S(1)}, f32[1,128]{1,0:T(1,128)S(1)}, u32[]{:S(2)}, u32[]{:S(2)}) collective-permute-start(f32[1,128]{1,0:T(1,128)S(1)} %get-tuple-element.54), channel_id=1, source_target_pairs={{0,4},{4,8},{8,12},{12,16},{16,20},{20,24},{24,28},{28,0},{1,5},{5... | collective-permute-start | bytes 1544 | tf_op jit(solution)/shard_map/ppermute | solution.py:20
  30.9 10.4 %collective-permute-start.4 = (f32[18,1]{1,0:T(8,128)S(1)}, f32[18,1]{1,0:T(8,128)S(1)}, u32[]{:S(2)}, u32[]{:S(2)}) collective-permute-start(f32[18,1]{1,0:T(8,128)S(1)} %get-tuple-element.78), channel_id=1, source_target_pairs={{1,0},{2,1},{3,2},{0,3},{5,4},{6,5},{7,6},{4,7},{9,8},{10,9},{11,1... | collective-permute-start | bytes 224 | tf_op jit(solution)/shard_map/ppermute | solution.py:22
  30.9 10.4 %collective-permute-start.5 = (f32[18,1]{1,0:T(8,128)S(1)}, f32[18,1]{1,0:T(8,128)S(1)}, u32[]{:S(2)}, u32[]{:S(2)}) collective-permute-start(f32[18,1]{1,0:T(8,128)S(1)} %get-tuple-element.79), channel_id=1, source_target_pairs={{0,1},{1,2},{2,3},{3,0},{4,5},{5,6},{6,7},{7,4},{8,9},{9,10},{10,1... | collective-permute-start | bytes 224 | tf_op jit(solution)/shard_map/ppermute | solution.py:20
  41.4 4.7 %collective-permute-start.6 = (f32[2,1,128]{2,1,0:T(1,128)S(1)}, f32[2,1,128]{2,1,0:T(1,128)S(1)}, u32[]{:S(2)}, u32[]{:S(2)}) collective-permute-start(f32[2,1,128]{2,1,0:T(1,128)S(1)} %get-tuple-element.67), channel_id=1, source_target_pairs={{4,0},{8,4},{12,8},{16,12},{20,16},{24,20},{28,24},{0,28},{5,1},{9... | collective-permute-start | bytes 3080 | tf_op jit(solution)/shard_map/ppermute | solution.py:22
  44.7 6.3 %collective-permute-start.7 = (f32[2,1,128]{2,1,0:T(1,128)S(1)}, f32[2,1,128]{2,1,0:T(1,128)S(1)}, u32[]{:S(2)}, u32[]{:S(2)}) collective-permute-start(f32[2,1,128]{2,1,0:T(1,128)S(1)} %get-tuple-element.66), channel_id=1, source_target_pairs={{0,4},{4,8},{8,12},{12,16},{16,20},{20,24},{24,28},{28,0},{1,5},{5... | collective-permute-start | bytes 3080 | tf_op jit(solution)/shard_map/ppermute | solution.py:20
  51.1 3.6 %collective-permute-start.9 = (f32[2,18,1]{2,1,0:T(8,128)S(1)}, f32[2,18,1]{2,1,0:T(8,128)S(1)}, u32[]{:S(2)}, u32[]{:S(2)}) collective-permute-start(f32[2,18,1]{2,1,0:T(8,128)S(1)} %get-tuple-element.53), channel_id=1, source_target_pairs={{0,1},{1,2},{2,3},{3,0},{4,5},{5,6},{6,7},{7,4},{8,9},{9,10},{10,1... | collective-permute-start | bytes 440 | tf_op jit(solution)/shard_map/ppermute | solution.py:20
  54.7 3.6 %collective-permute-start.10 = (f32[1,128]{1,0:T(1,128)S(1)}, f32[1,128]{1,0:T(1,128)S(1)}, u32[]{:S(2)}, u32[]{:S(2)}) collective-permute-start(f32[1,128]{1,0:T(1,128)S(1)} %get-tuple-element.89), channel_id=1, source_target_pairs={{4,0},{8,4},{12,8},{16,12},{20,16},{24,20},{28,24},{0,28},{5,1},{9... | collective-permute-start | bytes 1544 | tf_op jit(solution)/shard_map/ppermute | solution.py:22
  54.8 6.3 %collective-permute-start.11 = (f32[1,128]{1,0:T(1,128)S(1)}, f32[1,128]{1,0:T(1,128)S(1)}, u32[]{:S(2)}, u32[]{:S(2)}) collective-permute-start(f32[1,128]{1,0:T(1,128)S(1)} %get-tuple-element.88), channel_id=1, source_target_pairs={{0,4},{4,8},{8,12},{12,16},{16,20},{20,24},{24,28},{28,0},{1,5},{5... | collective-permute-start | bytes 1544 | tf_op jit(solution)/shard_map/ppermute | solution.py:20
  64.5 3.6 %collective-permute-start.14 = (f32[2,1,128]{2,1,0:T(1,128)S(1)}, f32[2,1,128]{2,1,0:T(1,128)S(1)}, u32[]{:S(2)}, u32[]{:S(2)}) collective-permute-start(f32[2,1,128]{2,1,0:T(1,128)S(1)} %get-tuple-element.65), channel_id=1, source_target_pairs={{4,0},{8,4},{12,8},{16,12},{20,16},{24,20},{28,24},{0,28},{5,1},{9... | collective-permute-start | bytes 3080 | tf_op jit(solution)/shard_map/ppermute | solution.py:22
  64.5 6.3 %collective-permute-start.15 = (f32[2,1,128]{2,1,0:T(1,128)S(1)}, f32[2,1,128]{2,1,0:T(1,128)S(1)}, u32[]{:S(2)}, u32[]{:S(2)}) collective-permute-start(f32[2,1,128]{2,1,0:T(1,128)S(1)} %get-tuple-element.64), channel_id=1, source_target_pairs={{0,4},{4,8},{8,12},{12,16},{16,20},{20,24},{24,28},{28,0},{1,5},{5... | collective-permute-start | bytes 3080 | tf_op jit(solution)/shard_map/ppermute | solution.py:20
  70.9 3.4 %collective-permute-start.17 = (f32[2,18,1]{2,1,0:T(8,128)S(1)}, f32[2,18,1]{2,1,0:T(8,128)S(1)}, u32[]{:S(2)}, u32[]{:S(2)}) collective-permute-start(f32[2,18,1]{2,1,0:T(8,128)S(1)} %get-tuple-element.51), channel_id=1, source_target_pairs={{0,1},{1,2},{2,3},{3,0},{4,5},{5,6},{6,7},{7,4},{8,9},{9,10},{10,1... | collective-permute-start | bytes 440 | tf_op jit(solution)/shard_map/ppermute | solution.py:20
  74.5 3.6 %collective-permute-start.18 = (f32[1,128]{1,0:T(1,128)S(1)}, f32[1,128]{1,0:T(1,128)S(1)}, u32[]{:S(2)}, u32[]{:S(2)}) collective-permute-start(f32[1,128]{1,0:T(1,128)S(1)} %get-tuple-element.87), channel_id=1, source_target_pairs={{4,0},{8,4},{12,8},{16,12},{20,16},{24,20},{28,24},{0,28},{5,1},{9... | collective-permute-start | bytes 1544 | tf_op jit(solution)/shard_map/ppermute | solution.py:22
  74.5 6.3 %collective-permute-start.19 = (f32[1,128]{1,0:T(1,128)S(1)}, f32[1,128]{1,0:T(1,128)S(1)}, u32[]{:S(2)}, u32[]{:S(2)}) collective-permute-start(f32[1,128]{1,0:T(1,128)S(1)} %get-tuple-element.86), channel_id=1, source_target_pairs={{0,4},{4,8},{8,12},{12,16},{16,20},{20,24},{24,28},{28,0},{1,5},{5... | collective-permute-start | bytes 1544 | tf_op jit(solution)/shard_map/ppermute | solution.py:20
  84.2 3.6 %collective-permute-start.22 = (f32[2,1,128]{2,1,0:T(1,128)S(1)}, f32[2,1,128]{2,1,0:T(1,128)S(1)}, u32[]{:S(2)}, u32[]{:S(2)}) collective-permute-start(f32[2,1,128]{2,1,0:T(1,128)S(1)} %get-tuple-element.63), channel_id=1, source_target_pairs={{4,0},{8,4},{12,8},{16,12},{20,16},{24,20},{28,24},{0,28},{5,1},{9... | collective-permute-start | bytes 3080 | tf_op jit(solution)/shard_map/ppermute | solution.py:22
  84.2 6.3 %collective-permute-start.23 = (f32[2,1,128]{2,1,0:T(1,128)S(1)}, f32[2,1,128]{2,1,0:T(1,128)S(1)}, u32[]{:S(2)}, u32[]{:S(2)}) collective-permute-start(f32[2,1,128]{2,1,0:T(1,128)S(1)} %get-tuple-element.62), channel_id=1, source_target_pairs={{0,4},{4,8},{8,12},{12,16},{16,20},{20,24},{24,28},{28,0},{1,5},{5... | collective-permute-start | bytes 3080 | tf_op jit(solution)/shard_map/ppermute | solution.py:20
  90.6 3.3 %collective-permute-start.25 = (f32[2,18,1]{2,1,0:T(8,128)S(1)}, f32[2,18,1]{2,1,0:T(8,128)S(1)}, u32[]{:S(2)}, u32[]{:S(2)}) collective-permute-start(f32[2,18,1]{2,1,0:T(8,128)S(1)} %get-tuple-element.49), channel_id=1, source_target_pairs={{0,1},{1,2},{2,3},{3,0},{4,5},{5,6},{6,7},{7,4},{8,9},{9,10},{10,1... | collective-permute-start | bytes 440 | tf_op jit(solution)/shard_map/ppermute | solution.py:20
  94.1 3.6 %collective-permute-start.26 = (f32[1,128]{1,0:T(1,128)S(1)}, f32[1,128]{1,0:T(1,128)S(1)}, u32[]{:S(2)}, u32[]{:S(2)}) collective-permute-start(f32[1,128]{1,0:T(1,128)S(1)} %get-tuple-element.85), channel_id=1, source_target_pairs={{4,0},{8,4},{12,8},{16,12},{20,16},{24,20},{28,24},{0,28},{5,1},{9... | collective-permute-start | bytes 1544 | tf_op jit(solution)/shard_map/ppermute | solution.py:22
  94.1 6.3 %collective-permute-start.27 = (f32[1,128]{1,0:T(1,128)S(1)}, f32[1,128]{1,0:T(1,128)S(1)}, u32[]{:S(2)}, u32[]{:S(2)}) collective-permute-start(f32[1,128]{1,0:T(1,128)S(1)} %get-tuple-element.84), channel_id=1, source_target_pairs={{0,4},{4,8},{8,12},{12,16},{16,20},{20,24},{24,28},{28,0},{1,5},{5... | collective-permute-start | bytes 1544 | tf_op jit(solution)/shard_map/ppermute | solution.py:20
  103.8 3.6 %collective-permute-start.30 = (f32[2,1,128]{2,1,0:T(1,128)S(1)}, f32[2,1,128]{2,1,0:T(1,128)S(1)}, u32[]{:S(2)}, u32[]{:S(2)}) collective-permute-start(f32[2,1,128]{2,1,0:T(1,128)S(1)} %get-tuple-element.61), channel_id=1, source_target_pairs={{4,0},{8,4},{12,8},{16,12},{20,16},{24,20},{28,24},{0,28},{5,1},{9... | collective-permute-start | bytes 3080 | tf_op jit(solution)/shard_map/ppermute | solution.py:22
  103.8 6.3 %collective-permute-start.31 = (f32[2,1,128]{2,1,0:T(1,128)S(1)}, f32[2,1,128]{2,1,0:T(1,128)S(1)}, u32[]{:S(2)}, u32[]{:S(2)}) collective-permute-start(f32[2,1,128]{2,1,0:T(1,128)S(1)} %get-tuple-element.60), channel_id=1, source_target_pairs={{0,4},{4,8},{8,12},{12,16},{16,20},{20,24},{24,28},{28,0},{1,5},{5... | collective-permute-start | bytes 3080 | tf_op jit(solution)/shard_map/ppermute | solution.py:20
  110.2 3.3 %collective-permute-start.33 = (f32[2,18,1]{2,1,0:T(8,128)S(1)}, f32[2,18,1]{2,1,0:T(8,128)S(1)}, u32[]{:S(2)}, u32[]{:S(2)}) collective-permute-start(f32[2,18,1]{2,1,0:T(8,128)S(1)} %get-tuple-element.47), channel_id=1, source_target_pairs={{0,1},{1,2},{2,3},{3,0},{4,5},{5,6},{6,7},{7,4},{8,9},{9,10},{10,1... | collective-permute-start | bytes 440 | tf_op jit(solution)/shard_map/ppermute | solution.py:20
  113.6 3.6 %collective-permute-start.34 = (f32[1,128]{1,0:T(1,128)S(1)}, f32[1,128]{1,0:T(1,128)S(1)}, u32[]{:S(2)}, u32[]{:S(2)}) collective-permute-start(f32[1,128]{1,0:T(1,128)S(1)} %get-tuple-element.83), channel_id=1, source_target_pairs={{4,0},{8,4},{12,8},{16,12},{20,16},{24,20},{28,24},{0,28},{5,1},{9... | collective-permute-start | bytes 1544 | tf_op jit(solution)/shard_map/ppermute | solution.py:22
  113.7 6.3 %collective-permute-start.35 = (f32[1,128]{1,0:T(1,128)S(1)}, f32[1,128]{1,0:T(1,128)S(1)}, u32[]{:S(2)}, u32[]{:S(2)}) collective-permute-start(f32[1,128]{1,0:T(1,128)S(1)} %get-tuple-element.82), channel_id=1, source_target_pairs={{0,4},{4,8},{8,12},{12,16},{16,20},{20,24},{24,28},{28,0},{1,5},{5... | collective-permute-start | bytes 1544 | tf_op jit(solution)/shard_map/ppermute | solution.py:20
  123.3 3.6 %collective-permute-start.38 = (f32[2,1,128]{2,1,0:T(1,128)S(1)}, f32[2,1,128]{2,1,0:T(1,128)S(1)}, u32[]{:S(2)}, u32[]{:S(2)}) collective-permute-start(f32[2,1,128]{2,1,0:T(1,128)S(1)} %get-tuple-element.59), channel_id=1, source_target_pairs={{4,0},{8,4},{12,8},{16,12},{20,16},{24,20},{28,24},{0,28},{5,1},{9... | collective-permute-start | bytes 3080 | tf_op jit(solution)/shard_map/ppermute | solution.py:22
  123.4 6.3 %collective-permute-start.39 = (f32[2,1,128]{2,1,0:T(1,128)S(1)}, f32[2,1,128]{2,1,0:T(1,128)S(1)}, u32[]{:S(2)}, u32[]{:S(2)}) collective-permute-start(f32[2,1,128]{2,1,0:T(1,128)S(1)} %get-tuple-element.58), channel_id=1, source_target_pairs={{0,4},{4,8},{8,12},{12,16},{16,20},{20,24},{24,28},{28,0},{1,5},{5... | collective-permute-start | bytes 3080 | tf_op jit(solution)/shard_map/ppermute | solution.py:20
  133.2 3.6 %collective-permute-start.42 = (f32[1,128]{1,0:T(1,128)S(1)}, f32[1,128]{1,0:T(1,128)S(1)}, u32[]{:S(2)}, u32[]{:S(2)}) collective-permute-start(f32[1,128]{1,0:T(1,128)S(1)} %get-tuple-element.81), channel_id=1, source_target_pairs={{4,0},{8,4},{12,8},{16,12},{20,16},{24,20},{28,24},{0,28},{5,1},{9... | collective-permute-start | bytes 1544 | tf_op jit(solution)/shard_map/ppermute | solution.py:22
  133.3 6.3 %collective-permute-start.43 = (f32[1,128]{1,0:T(1,128)S(1)}, f32[1,128]{1,0:T(1,128)S(1)}, u32[]{:S(2)}, u32[]{:S(2)}) collective-permute-start(f32[1,128]{1,0:T(1,128)S(1)} %get-tuple-element.80), channel_id=1, source_target_pairs={{0,4},{4,8},{8,12},{12,16},{16,20},{20,24},{24,28},{28,0},{1,5},{5... | collective-permute-start | bytes 1544 | tf_op jit(solution)/shard_map/ppermute | solution.py:20
  142.9 3.6 %collective-permute-start.46 = (f32[2,1,128]{2,1,0:T(1,128)S(1)}, f32[2,1,128]{2,1,0:T(1,128)S(1)}, u32[]{:S(2)}, u32[]{:S(2)}) collective-permute-start(f32[2,1,128]{2,1,0:T(1,128)S(1)} %get-tuple-element.57), channel_id=1, source_target_pairs={{4,0},{8,4},{12,8},{16,12},{20,16},{24,20},{28,24},{0,28},{5,1},{9... | collective-permute-start | bytes 3080 | tf_op jit(solution)/shard_map/ppermute | solution.py:22
  143.0 6.3 %collective-permute-start.47 = (f32[2,1,128]{2,1,0:T(1,128)S(1)}, f32[2,1,128]{2,1,0:T(1,128)S(1)}, u32[]{:S(2)}, u32[]{:S(2)}) collective-permute-start(f32[2,1,128]{2,1,0:T(1,128)S(1)} %get-tuple-element.56), channel_id=1, source_target_pairs={{0,4},{4,8},{8,12},{12,16},{16,20},{20,24},{24,28},{28,0},{1,5},{5... | collective-permute-start | bytes 3080 | tf_op jit(solution)/shard_map/ppermute | solution.py:20
  (24 other events, 88.6 us)
where the time goes:
time: 154 us; the launch traced here: 153 us
  waiting for transfers between devices  96.9 us (63%)
  starting transfers between devices  38.3 us (25%)
  matrix products  8.5 us (6%)
  local copies, waits for them, and re-layouts  6.57 us (4%)
  other arithmetic  2.09 us (1%)
    ppermute x25, waiting for transfers between devices, padded_2(): lax.ppermute(tail, axis, [(i, (i + 1) % count) for i in range(count)])  52.5 us
    ppermute x25, waiting for transfers between devices, padded_2(): lax.ppermute(head, axis, [((i + 1) % count, i) for i in range(count)])  44.4 us
    ppermute x25, starting transfers between devices, padded_2(): lax.ppermute(tail, axis, [(i, (i + 1) % count) for i in range(count)])  29.3 us
    ppermute x25, starting transfers between devices, padded_2(): lax.ppermute(head, axis, [((i + 1) % count, i) for i in range(count)])  9.04 us
    dot_general x1, matrix products, per_device(): jnp.einsum('fsrqa,rqao->sfro', picked, remap_weights, precision=highest)  6.83 us
  transfers between devices with their start and end apart: 50, of which 45 were waited for; matrix products, arithmetic and copies ran while one was open for 7% of the time, Pallas kernels for 0%

commit v1 on v0

v1 whole, which is shorter than its diff:
```python
import functools
import math

import jax
import jax.numpy as jnp
import numpy as np
from jax import lax
from jax.experimental import pallas as pl
from jax.experimental.pallas import tpu as pltpu
from jax.sharding import PartitionSpec as P

SUB = 6
DYN = 3


def hermite_table(count_sub, count_levels):
    table = np.zeros((count_sub, count_levels))

    def add_slope(position_row, level, factor):
        if level == 0:
            table[position_row, 1] += factor
            table[position_row, 0] -= factor
        elif level == count_levels - 1:
            table[position_row, level] += factor
            table[position_row, level - 1] -= factor
        else:
            table[position_row, level + 1] += 0.5 * factor
            table[position_row, level - 1] -= 0.5 * factor

    for substep in range(count_sub):
        position = (substep + 0.5) * (count_levels - 1) / count_sub
        lower = min(int(math.floor(position)), count_levels - 2)
        fraction = position - lower
        table[substep, lower] += 2 * fraction**3 - 3 * fraction**2 + 1
        table[substep, lower + 1] += -2 * fraction**3 + 3 * fraction**2
        add_slope(substep, lower, fraction**3 - 2 * fraction**2 + fraction)
        add_slope(substep, lower + 1, fraction**3 - fraction**2)
    return table


WIDTHS = [2 * (SUB - s) - (1 if f < 2 else 2) for s in range(SUB) for f in range(DYN)]
WIDTHS += [2 * SUB, 2 * SUB - 1, 2 * SUB - 1, 2 * SUB - 1]
PLANES = SUB * DYN
ITEMS = len(WIDTHS)
ROW_AT = np.concatenate([[0], np.cumsum(WIDTHS)]).tolist()
LANE_AT = ROW_AT[:PLANES] + [ROW_AT[i] - ROW_AT[PLANES] for i in range(PLANES, ITEMS)]
MAIN = -(-ROW_AT[-1] // 8) * 8
GROUPS = 2


def interp_kernel(table, mean, rows, atmo_ref, out_ref):
    fields, levels, tiles, _ = atmo_ref.shape
    for f in range(DYN):
        level = [atmo_ref[f, k] for k in range(levels)]
        for s in range(SUB):
            terms = [float(table[s, k]) * level[k] for k in range(levels) if table[s, k] != 0]
            out_ref[pl.ds(s * DYN + f, tiles, stride=rows), :] = functools.reduce(jnp.add, terms)
    for f in range(DYN, fields):
        terms = [float(mean[k]) * atmo_ref[f, k] for k in range(levels)]
        out_ref[pl.ds(PLANES + f - DYN, tiles, stride=rows), :] = functools.reduce(jnp.add, terms)
    pad = out_ref.shape[0] - tiles * rows
    out_ref[tiles * rows :, :] = jnp.zeros((pad, out_ref.shape[1]), jnp.float32)


def split_tiles(source_ref, split_ref, base, tiles, rows):
    for g in range(tiles):
        value = source_ref[g * rows : g * rows + 32, :]
        high = value.astype(jnp.bfloat16)
        split_ref[base + g, 0:32, :] = high
        split_ref[base + g, 32:64, :] = (value - high.astype(jnp.float32)).astype(jnp.bfloat16)


def remap_row(split_ref, first, second, wa, wb):
    left = jnp.concatenate([split_ref[first], split_ref[second]], axis=1)
    weights = jnp.concatenate([wa, wb], axis=0)
    high = weights.astype(jnp.bfloat16)
    low = (weights - high.astype(jnp.float32)).astype(jnp.bfloat16)
    both = jnp.dot(left, high, preferred_element_type=jnp.float32)
    return both[0:32] + both[32:64] + jnp.dot(left[0:32], low, preferred_element_type=jnp.float32)


def own_kernel(rows, tiles_ref, own_ref, wa_ref, wb_ref, acc_ref, split_ref):
    step = pl.program_id(0)
    per = wa_ref.shape[0]
    slots = 4

    @pl.when(step == 0)
    def _():
        split_tiles(own_ref, split_ref, 0, split_ref.shape[0], rows)

    for x in range(per):
        at = (step * per + x) * slots
        tiles = split_ref.shape[0]
        first, second = tiles_ref[at + 1] - tiles, tiles_ref[at + 2] - tiles
        acc_ref[:, x, :] = remap_row(split_ref, first, second, wa_ref[x, 0], wb_ref[x, 0])


def rim_kernel(rows, tiles_ref, odd_ref, one_ref, two_ref, wa_ref, wb_ref, own_ref, state_ref, mask_ref,
               force_ref, mean_ref, main1_ref, main2_ref, edge1_ref, edge2_ref, split_ref, total_ref):
    step = pl.program_id(0)
    per = wa_ref.shape[0]
    slots = 4
    tiles = split_ref.shape[0] // 2
    row_odd, col_odd = odd_ref[0], odd_ref[1]

    @pl.when(step == 0)
    def _():
        split_tiles(one_ref, split_ref, 0, tiles, rows)
        split_tiles(two_ref, split_ref, tiles, tiles, rows)

    for x in range(per):
        at = (step * per + x) * slots
        first = tiles_ref[at] + tiles * (1 - row_odd)
        second = tiles_ref[at + 3] - 2 * tiles + tiles * row_odd
        value = remap_row(split_ref, first, second, wa_ref[x, 0], wb_ref[x, 0])
        total_ref[step, :, x, :] = value + own_ref[:, x, :]

    @pl.when(step == pl.num_programs(0) - 1)
    def _():
        plane = [jnp.concatenate([total_ref[k, j] for k in range(total_ref.shape[0])], axis=0) for j in range(rows)]
        for p in range(PLANES):
            force_ref[p] = plane[p]
        for f in range(DYN):
            mean_ref[f] = functools.reduce(jnp.add, [plane[s * DYN + f] for s in range(SUB)]) * (1.0 / SUB)
        for f in range(DYN, mean_ref.shape[0]):
            mean_ref[f] = plane[PLANES + f - DYN]
        items = plane[:PLANES] + [state_ref[k] for k in range(DYN)] + [mask_ref[...].astype(jnp.float32)]
        high = items[0].shape[0]
        wide = items[0].shape[1]

        def pack(down_ref, up_ref):
            for i, value in enumerate(items):
                w = WIDTHS[i]
                if w:
                    down_ref[ROW_AT[i] : ROW_AT[i] + w, :] = value[high - w :]
                    up_ref[ROW_AT[i] : ROW_AT[i] + w, :] = value[:w]
            for ref in (down_ref, up_ref):
                ref[ROW_AT[-1] :, :] = jnp.zeros((MAIN - ROW_AT[-1], wide), jnp.float32)

        @pl.when(row_odd == 0)
        def _():
            pack(main1_ref, main2_ref)

        @pl.when(row_odd != 0)
        def _():
            pack(main2_ref, main1_ref)

        lane = lax.broadcasted_iota(jnp.int32, (high, wide), 1)
        for g, group in enumerate((range(PLANES), range(PLANES, ITEMS))):
            last = jnp.zeros((high, wide), jnp.float32)
            head = jnp.zeros((high, wide), jnp.float32)
            for i in group:
                w, at = WIDTHS[i], LANE_AT[i]
                if w:
                    last = jnp.where(lane >= at, pltpu.roll(items[i], (at + w) % wide, 1), last)
                    head = jnp.where(lane >= at, pltpu.roll(items[i], at, 1), head)
            edge1_ref[g * high : (g + 1) * high, :] = jnp.where(col_odd == 0, last, head)
            edge2_ref[g * high : (g + 1) * high, :] = jnp.where(col_odd == 0, head, last)


def ocean_kernel(odd_ref, force_ref, state_ref, mask_ref, edge1_ref, edge2_ref, one_ref, two_ref, out_ref, top_ref, low_ref):
    row_odd, col_odd = odd_ref[0], odd_ref[1]
    high, wide = mask_ref.shape
    top_ref[...] = jnp.where(row_odd == 0, two_ref[...], one_ref[...])
    low_ref[...] = jnp.where(row_odd == 0, one_ref[...], two_ref[...])
    rim = GROUPS * high
    second = rim + MAIN
    lane = lax.broadcasted_iota(jnp.int32, (3 * high, wide), 1)

    def edges(g):
        own = slice(g * high, (g + 1) * high)
        far = slice(second + g * high, second + (g + 1) * high)
        a = jnp.concatenate([top_ref[own], edge1_ref[own], low_ref[own]], axis=0)
        b = jnp.concatenate([top_ref[far], edge2_ref[own], low_ref[far]], axis=0)
        return jnp.where(col_odd == 0, b, a), jnp.where(col_odd == 0, a, b)

    sides = [edges(g) for g in range(GROUPS)]

    def extended(i, own):
        w, at = WIDTHS[i], LANE_AT[i]
        start = rim + ROW_AT[i]
        main = jnp.concatenate([top_ref[start + w - high : start + w, :], own, low_ref[start : start + high, :]], axis=0)
        left, right = sides[0 if i < PLANES else 1]
        edge = jnp.where(lane < wide // 2, pltpu.roll(right, (wide - at) % wide, 1), pltpu.roll(left, (2 * wide - w - at) % wide, 1))
        return jnp.concatenate([main, edge], axis=1)

    rows, lanes = 3 * high, 2 * wide
    before = lambda v, axis: pltpu.roll(v, 1, axis)
    after = lambda v, axis: pltpu.roll(v, (rows, lanes)[axis] - 1, axis)
    height = extended(PLANES, state_ref[0])
    zonal = extended(PLANES + 1, state_ref[1])
    merid = extended(PLANES + 2, state_ref[2])
    ocean = extended(PLANES + 3, mask_ref[...].astype(jnp.float32))
    for s in range(SUB):
        push_u, push_v, push_h = (extended(s * DYN + f, force_ref[s * DYN + f]) for f in range(DYN))
        grad_x = (after(height, 0) - before(height, 0)) * 0.5
        grad_y = (after(height, 1) - before(height, 1)) * 0.5
        zonal = ocean * (zonal - grad_x + 0.2 * merid + 0.5 * push_u)
        merid = ocean * (merid - grad_y - 0.2 * zonal + 0.5 * push_v)
        spread = (after(zonal, 0) - before(zonal, 0)) * 0.5 + (after(merid, 1) - before(merid, 1)) * 0.5
        height = height - spread + 0.5 * push_h
    for k, value in enumerate((height, zonal, merid)):
        out_ref[k] = value[high : 2 * high, :wide]


def per_device(size_row, size_col, atmo_states, remap_weights, intersection_tiles, land_mask, ocean_state):
    fields, levels, tiles, cells = atmo_states.shape
    high, wide = land_mask.shape
    rows = PLANES + fields - DYN
    vmem = pl.BlockSpec(memory_space=pltpu.VMEM)
    smem = pl.BlockSpec(memory_space=pltpu.SMEM)
    f32 = lambda *shape: jax.ShapeDtypeStruct(shape, jnp.float32)
    params = lambda: pltpu.CompilerParams(vmem_limit_bytes=32 << 20)

    def pairs(size):
        near = [(i, i ^ 1) for i in range(size)]
        far = [(i, (i + 1) % size if i % 2 else (i - 1) % size) for i in range(size)]
        return near, far

    row_near, row_far = pairs(size_row)
    col_near, col_far = pairs(size_col)
    odd = jnp.stack([lax.axis_index("row") % 2, lax.axis_index("col") % 2]).astype(jnp.int32)
    flat_tiles = intersection_tiles.reshape(-1)

    table = hermite_table(SUB, levels).astype(np.float32)
    mean = table.astype(np.float64).mean(axis=0)
    own = pl.pallas_call(
        functools.partial(interp_kernel, table, mean, rows),
        out_shape=f32(tiles * rows + 8, cells),
        in_specs=[vmem],
        out_specs=vmem,
        compiler_params=params(),
    )(atmo_states)
    two = lax.ppermute(own, "row", row_far)
    one = lax.ppermute(own, "row", row_near)

    steps = 2
    per = high // steps
    weight = lambda slot: pl.BlockSpec((per, 1, cells, wide), lambda i, *_: (i, slot, 0, 0))
    whole = lambda *shape: pl.BlockSpec(shape, lambda i, *_: (0,) * len(shape))
    split = pltpu.VMEM((tiles, 64, cells), jnp.bfloat16)
    length = tiles * rows + 8
    acc = pl.pallas_call(
        functools.partial(own_kernel, rows),
        out_shape=f32(32, high, wide),
        grid_spec=pltpu.PrefetchScalarGridSpec(
            num_scalar_prefetch=1,
            grid=(steps,),
            in_specs=[whole(length, cells), weight(1), weight(2)],
            out_specs=pl.BlockSpec((32, per, wide), lambda i, *_: (0, i, 0)),
            scratch_shapes=[split],
        ),
        compiler_params=params(),
        cost_estimate=pl.CostEstimate(flops=10**9, bytes_accessed=4 << 20, transcendentals=0),
    )(flat_tiles, own, remap_weights, remap_weights)

    force, flux_mean, main1, main2, edge1, edge2 = pl.pallas_call(
        functools.partial(rim_kernel, rows),
        out_shape=(f32(PLANES, high, wide), f32(fields, high, wide), f32(MAIN, wide), f32(MAIN, wide),
                   f32(GROUPS * high, wide), f32(GROUPS * high, wide)),
        grid_spec=pltpu.PrefetchScalarGridSpec(
            num_scalar_prefetch=2,
            grid=(steps,),
            in_specs=[whole(length, cells), whole(length, cells), weight(0), weight(3),
                      pl.BlockSpec((32, per, wide), lambda i, *_: (0, i, 0)),
                      whole(3, high, wide), whole(high, wide)],
            out_specs=(whole(PLANES, high, wide), whole(fields, high, wide), whole(MAIN, wide), whole(MAIN, wide),
                       whole(GROUPS * high, wide), whole(GROUPS * high, wide)),
            scratch_shapes=[pltpu.VMEM((2 * tiles, 64, cells), jnp.bfloat16), pltpu.VMEM((steps, 32, per, wide), jnp.float32)],
        ),
        compiler_params=params(),
        cost_estimate=pl.CostEstimate(flops=10**9, bytes_accessed=4 << 20, transcendentals=0),
    )(flat_tiles, odd, one, two, remap_weights, remap_weights, acc, ocean_state, land_mask)

    from2 = lax.ppermute(edge2, "col", col_far)
    from1 = lax.ppermute(edge1, "col", col_near)
    join = lambda main: jnp.concatenate([from1, main, from2], axis=0)
    rim2 = lax.ppermute(join(main2), "row", row_far)
    rim1 = lax.ppermute(join(main1), "row", row_near)

    length = 2 * GROUPS * high + MAIN
    final = pl.pallas_call(
        ocean_kernel,
        out_shape=f32(3, high, wide),
        in_specs=[smem] + [vmem] * 7,
        out_specs=vmem,
        scratch_shapes=[pltpu.VMEM((length, wide), jnp.float32)] * 2,
        compiler_params=params(),
    )(odd, force, ocean_state, land_mask, from1, from2, rim1, rim2)
    return flux_mean, final


def solution(mesh):
    placed = (
        P(None, None, "row", None),
        P("row", "col", None, None),
        P("row", "col"),
        P("row", "col"),
        P(None, "row", "col"),
    )
    return jax.shard_map(
        functools.partial(per_device, mesh.shape["row"], mesh.shape["col"]),
        mesh=mesh,
        in_specs=placed,
        out_specs=(P(None, "row", "col"), P(None, "row", "col")),
        check_vma=False,
    )
```

time: 154 us -> 35 us (0.23)
  waiting for transfers between devices: 96.9 us -> 14.2 us
  starting transfers between devices: 38.3 us -> 9.55 us
  matrix products: 8.5 us -> 0 us
  Pallas kernels: 0 us -> 5.93 us
  local copies, waits for them, and re-layouts: 6.57 us -> 4.23 us
  other arithmetic: 2.09 us -> 0.1 us
    ppermute x50 -> x6, waiting for transfers between devices: 96.9 us -> 14.2 us  [the longest x1 6.45 us: per_device(): rim2 = lax.ppermute(join(main2), 'row', row_far)]
    ppermute x50 -> x6, starting transfers between devices: 38.3 us -> 9.55 us  [the longest x1 6.07 us: per_device(): two = lax.ppermute(own, 'row', row_far)]
    dot_general x2 -> x0, matrix products: 8.5 us -> none  [the longest x1 6.83 us: per_device(): jnp.einsum('fsrqa,rqao->sfro', picked, remap_weights, precision=highest)]
    pallas_call x0 -> x4, Pallas kernels: none -> 5.93 us  [the longest x1 2.27 us: per_device(): pl.pallas_call(functools.partial(rim_kernel, rows), out_shape=(f32(PLANES...]
    gather x1 -> x0, local copies, waits for them, and re-layouts: 2.35 us -> none  [per_device(): picked = window[:, :, intersection_tiles, :]]
    unnamed x13 -> x11, local copies, waits for them, and re-layouts: 2.71 us -> 4.15 us
  transfers between devices with their start and end apart: 50 -> 6, of which waited for: 45 -> 5; matrix products, arithmetic and copies ran while one was open for 7% -> 3% of each run, Pallas kernels for 0% -> 4%
where the time goes in v1:
time: 35 us; the launch traced here: 34.7 us
  waiting for transfers between devices  14.2 us (41%)
  starting transfers between devices  9.55 us (27%)
  Pallas kernels  5.93 us (17%)
  local copies, waits for them, and re-layouts  4.23 us (12%)
  between operations  0.69 us (2%)
    ppermute x1, waiting for transfers between devices, per_device(): rim2 = lax.ppermute(join(main2), 'row', row_far)  6.45 us
    ppermute x1, starting transfers between devices, per_device(): two = lax.ppermute(own, 'row', row_far)  6.07 us
    ppermute x1, waiting for transfers between devices, per_device(): one = lax.ppermute(own, 'row', row_near)  4.37 us
    unnamed x11, local copies, waits for them, and re-layouts  4.15 us
    pallas_call x1, Pallas kernels, per_device(): pl.pallas_call(functools.partial(rim_kernel, rows), out_shape=(f32(PLANES...  2.27 us
    pallas_call x1, Pallas kernels, per_device(): pl.pallas_call(ocean_kernel, out_shape=f32(3, high, wide), in_specs=[smem...  2.2 us
    ppermute x1, starting transfers between devices, per_device(): rim2 = lax.ppermute(join(main2), 'row', row_far)  1.87 us
    ppermute x1, starting transfers between devices, per_device(): from2 = lax.ppermute(edge2, 'col', col_far)  1.59 us
  transfers between devices with their start and end apart: 6, of which 5 were waited for; matrix products, arithmetic and copies ran while one was open for 3% of the time, Pallas kernels for 4%

profile of v1, /device:TPU:0, one launch (start us, length us, event | category | flops | bytes accessed | tf_op | source)
XLA Modules:
  0.0 34.7 jit_solution(12821349471117148883)
XLA Ops:
  0.6 0.0 copy-start.2
  0.6 1.2 %copy-done.2 = f32[10,12,16,128]{3,2,1,0:T(8,128)S(1)} copy-done((f32[10,12,16,128]{3,2,1,0:T(8,128)S(1)}, f32[10,12,16,128]{3,2,1,0:T(8,128)}, u32[]{:S(2)}) %copy-start.2) | copy-done | bytes 983064
  1.8 0.1 shard_map.68.own_ref
  1.9 6.1 %collective-permute-start.1 = (f32[408,128]{1,0:T(8,128)S(1)}, f32[408,128]{1,0:T(8,128)S(1)}, u32[]{:S(2)}, u32[]{:S(2)}) collective-permute-start(f32[408,128]{1,0:T(8,128)S(1)} %shard_map.68.own_ref), channel_id=1, source_target_pairs={{0,28},{4,8},{8,4},{12,16},{16,12},{20,24},{24,20},{28,0},{1,29},{... | collective-permute-start | bytes 626696 | tf_op jit(solution)/shard_map/ppermute | solution.py:234
  8.0 0.0 collective-permute-start
  8.0 0.8 %copy.8 = s32[16,4]{1,0:T(8,128)S(1)} copy(s32[16,4]{0,1:T(4,128)} %param.7) | data formatting | bytes 512 | tf_op args[2]
  8.8 0.1 reshape.7.tiles_ref
  8.9 0.0 copy-start
  8.9 2.2 %copy-done = f32[16,4,128,128]{3,2,1,0:T(8,128)S(1)} copy-done((f32[16,4,128,128]{3,2,1,0:T(8,128)S(1)}, f32[16,4,128,128]{3,2,1,0:T(8,128)}, u32[]{:S(2)}) %copy-start) | copy-done | bytes 4194328
  11.0 0.0 copy-start.1
  11.1 0.0 copy-start.3
  11.1 0.0 copy-start.4
  11.1 1.4 %shard_map.69.own_ref = f32[32,16,128]{2,1,0:T(8,128)S(1)} custom-call(s32[64]{0:T(128)S(1)} %reshape.7.tiles_ref, f32[408,128]{1,0:T(8,128)S(1)} %shard_map.68.own_ref, f32[16,4,128,128]{3,2,1,0:T(8,128)S(1)} %copy-done, f32[16,4,128,128]{3,2,1,0:T(8,128)S(1)} %copy-done), custom_call_target="tpu_custom_call" | custom-call | flops 1000000000 | bytes 4194304 | tf_op jit(solution)/shard_map/pallas_call | solution.py:243
  12.4 0.1 pad_add_fusion.odd_ref
  12.5 0.7 %collective-permute-done.1.two_ref = f32[408,128]{1,0:T(8,128)S(1)} collective-permute-done((f32[408,128]{1,0:T(8,128)S(1)}, f32[408,128]{1,0:T(8,128)S(1)}, u32[]{:S(2)}, u32[]{:S(2)}) %collective-permute-start.1) | collective-permute-done | bytes 208928 | tf_op jit(solution)/shard_map/ppermute | solution.py:234
  13.3 4.4 %collective-permute-done.one_ref = f32[408,128]{1,0:T(8,128)S(1)} collective-permute-done((f32[408,128]{1,0:T(8,128)S(1)}, f32[408,128]{1,0:T(8,128)S(1)}, u32[]{:S(2)}, u32[]{:S(2)}) %collective-permute-start) | collective-permute-done | bytes 208928 | tf_op jit(solution)/shard_map/ppermute | solution.py:235
  17.6 0.0 copy-done.1
  17.6 0.0 copy-done.3
  17.6 0.0 copy-done.4
  17.6 2.3 %shard_map.70 = (f32[18,16,128]{2,1,0:T(8,128)S(1)}, f32[10,16,128]{2,1,0:T(8,128)}, f32[152,128]{1,0:T(8,128)S(1)}, f32[152,128]{1,0:T(8,128)S(1)}, f32[32,128]{1,0:T(8,128)S(1)}, /*index=5*/f32[32,128]{1,0:T(8,128)S(1)}) custom-call(s32[64]{0:T(128)S(1)} %reshape.7.tiles_ref, s32[2]{0:T(128)S(1)} %pad_add_fusion.odd_ref, ...), custom_call_target="tpu_custom_call" | custom-call | flops 1000000000 | bytes 4194304 | tf_op jit(solution)/shard_map/pallas_call | solution.py:257
  19.9 0.0 collective-permute-start.2
  19.9 1.6 %collective-permute-start.3 = (f32[32,128]{1,0:T(8,128)S(1)}, f32[32,128]{1,0:T(8,128)S(1)}, u32[]{:S(2)}, u32[]{:S(2)}) collective-permute-start(f32[32,128]{1,0:T(8,128)S(1)} %get-tuple-element.11), channel_id=1, source_target_pairs={{0,3},{1,2},{2,1},{3,0},{4,7},{5,6},{6,5},{7,4},{8,11},{9,10},{10,... | collective-permute-start | bytes 49160 | tf_op jit(solution)/shard_map/ppermute | solution.py:275
  21.5 0.0 collective-permute-done.2.edge1_ref
  21.5 1.6 %collective-permute-done.3.edge2_ref = f32[32,128]{1,0:T(8,128)S(1)} collective-permute-done((f32[32,128]{1,0:T(8,128)S(1)}, f32[32,128]{1,0:T(8,128)S(1)}, u32[]{:S(2)}, u32[]{:S(2)}) %collective-permute-start.3) | collective-permute-done | bytes 16416 | tf_op jit(solution)/shard_map/ppermute | solution.py:275
  23.1 1.9 %collective-permute-start.5 = (f32[216,128]{1,0:T(8,128)S(1)}, f32[216,128]{1,0:T(8,128)S(1)}, u32[]{:S(2)}, u32[]{:S(2)}) collective-permute-start(f32[216,128]{1,0:T(8,128)S(1)} %get-tuple-element.14), channel_id=1, source_target_pairs={{0,28},{4,8},{8,4},{12,16},{16,12},{20,24},{24,20},{28,0},{1,29},{... | collective-permute-start | bytes 331784 | tf_op jit(solution)/shard_map/ppermute | solution.py:278
  25.0 0.0 collective-permute-start.4
  25.0 6.4 %collective-permute-done.5.two_ref = f32[216,128]{1,0:T(8,128)S(1)} collective-permute-done((f32[216,128]{1,0:T(8,128)S(1)}, f32[216,128]{1,0:T(8,128)S(1)}, u32[]{:S(2)}, u32[]{:S(2)}) %collective-permute-start.5) | collective-permute-done | bytes 110624 | tf_op jit(solution)/shard_map/ppermute | solution.py:278
  31.4 1.1 %collective-permute-done.4.one_ref = f32[216,128]{1,0:T(8,128)S(1)} collective-permute-done((f32[216,128]{1,0:T(8,128)S(1)}, f32[216,128]{1,0:T(8,128)S(1)}, u32[]{:S(2)}, u32[]{:S(2)}) %collective-permute-start.4) | collective-permute-done | bytes 110624 | tf_op jit(solution)/shard_map/ppermute | solution.py:279
  32.5 2.2 %shard_map.71 = f32[3,16,128]{2,1,0:T(8,128)} custom-call(s32[2]{0:T(128)S(1)} %pad_add_fusion.odd_ref, f32[18,16,128]{2,1,0:T(8,128)S(1)} %get-tuple-element.9.force_ref, f32[3,16,128]{2,1,0:T(8,128)S(1)} %copy-done.3, s32[16,128]{1,0:T(8,128)S(1)} %copy-done.4, f32[32,128]{1,0:T(8,128)S(1)} %collective-permute-done.2.edge1_ref, ...), custom_call_target="tpu_custom_call" | custom-call | tf_op jit(solution)/shard_map/pallas_call | solution.py:282
  (1 shorter events, 0.0 us)
Async XLA Ops:
  0.6 1.2 %copy-start.2 = (f32[10,12,16,128]{3,2,1,0:T(8,128)S(1)}, f32[10,12,16,128]{3,2,1,0:T(8,128)}, u32[]{:S(2)}) copy-start(f32[10,12,16,128]{3,2,1,0:T(8,128)} %atmo_ref.1) | copy-start | bytes 2949124
  1.9 11.3 %collective-permute-start.1 = (f32[408,128]{1,0:T(8,128)S(1)}, f32[408,128]{1,0:T(8,128)S(1)}, u32[]{:S(2)}, u32[]{:S(2)}) collective-permute-start(f32[408,128]{1,0:T(8,128)S(1)} %shard_map.68.own_ref), channel_id=1, source_target_pairs={{0,28},{4,8},{8,4},{12,16},{16,12},{20,24},{24,20},{28,0},{1,29},{... | collective-permute-start | bytes 626696 | tf_op jit(solution)/shard_map/ppermute | solution.py:234
  8.0 9.6 %collective-permute-start = (f32[408,128]{1,0:T(8,128)S(1)}, f32[408,128]{1,0:T(8,128)S(1)}, u32[]{:S(2)}, u32[]{:S(2)}) collective-permute-start(f32[408,128]{1,0:T(8,128)S(1)} %shard_map.68.own_ref), channel_id=1, source_target_pairs={{0,4},{4,0},{8,12},{12,8},{16,20},{20,16},{24,28},{28,24},{1,5},{5... | collective-permute-start | bytes 626696 | tf_op jit(solution)/shard_map/ppermute | solution.py:235
  8.9 2.2 %copy-start = (f32[16,4,128,128]{3,2,1,0:T(8,128)S(1)}, f32[16,4,128,128]{3,2,1,0:T(8,128)}, u32[]{:S(2)}) copy-start(f32[16,4,128,128]{3,2,1,0:T(8,128)} %wb_ref.3) | copy-start | bytes 12582916
  11.0 6.6 %copy-start.1 = (f32[16,4,128,128]{3,2,1,0:T(8,128)S(1)}, f32[16,4,128,128]{3,2,1,0:T(8,128)}, u32[]{:S(2)}) copy-start(f32[16,4,128,128]{3,2,1,0:T(8,128)} %wb_ref.3) | copy-start | bytes 12582916
  11.1 6.6 %copy-start.3 = (f32[3,16,128]{2,1,0:T(8,128)S(1)}, f32[3,16,128]{2,1,0:T(8,128)}, u32[]{:S(2)}) copy-start(f32[3,16,128]{2,1,0:T(8,128)} %state_ref.3) | copy-start | bytes 73732
  11.1 6.6 %copy-start.4 = (s32[16,128]{1,0:T(8,128)S(1)}, s32[16,128]{1,0:T(8,128)}, u32[]{:S(2)}) copy-start(s32[16,128]{1,0:T(8,128)} %mask_ref.3) | copy-start | bytes 24580
  19.9 1.6 %collective-permute-start.2 = (f32[32,128]{1,0:T(8,128)S(1)}, f32[32,128]{1,0:T(8,128)S(1)}, u32[]{:S(2)}, u32[]{:S(2)}) collective-permute-start(f32[32,128]{1,0:T(8,128)S(1)} %get-tuple-element.10), channel_id=1, source_target_pairs={{0,1},{1,0},{2,3},{3,2},{4,5},{5,4},{6,7},{7,6},{8,9},{9,8},{10,11... | collective-permute-start | bytes 49160 | tf_op jit(solution)/shard_map/ppermute | solution.py:276
  19.9 3.2 %collective-permute-start.3 = (f32[32,128]{1,0:T(8,128)S(1)}, f32[32,128]{1,0:T(8,128)S(1)}, u32[]{:S(2)}, u32[]{:S(2)}) collective-permute-start(f32[32,128]{1,0:T(8,128)S(1)} %get-tuple-element.11), channel_id=1, source_target_pairs={{0,3},{1,2},{2,1},{3,0},{4,7},{5,6},{6,5},{7,4},{8,11},{9,10},{10,... | collective-permute-start | bytes 49160 | tf_op jit(solution)/shard_map/ppermute | solution.py:275
  23.1 8.3 %collective-permute-start.5 = (f32[216,128]{1,0:T(8,128)S(1)}, f32[216,128]{1,0:T(8,128)S(1)}, u32[]{:S(2)}, u32[]{:S(2)}) collective-permute-start(f32[216,128]{1,0:T(8,128)S(1)} %get-tuple-element.14), channel_id=1, source_target_pairs={{0,28},{4,8},{8,4},{12,16},{16,12},{20,24},{24,20},{28,0},{1,29},{... | collective-permute-start | bytes 331784 | tf_op jit(solution)/shard_map/ppermute | solution.py:278
  25.0 7.6 %collective-permute-start.4 = (f32[216,128]{1,0:T(8,128)S(1)}, f32[216,128]{1,0:T(8,128)S(1)}, u32[]{:S(2)}, u32[]{:S(2)}) collective-permute-start(f32[216,128]{1,0:T(8,128)S(1)} %get-tuple-element.15), channel_id=1, source_target_pairs={{0,4},{4,0},{8,12},{12,8},{16,20},{20,16},{24,28},{28,24},{1,5},{5... | collective-permute-start | bytes 331784 | tf_op jit(solution)/shard_map/ppermute | solution.py:279

commit v2 on v0

v2 whole, which is shorter than its diff:
```python
import functools
import math

import jax
import jax.numpy as jnp
import numpy as np
from jax import lax
from jax.experimental import pallas as pl
from jax.experimental.pallas import tpu as pltpu
from jax.sharding import PartitionSpec as P

SUB = 6
DYN = 3


def hermite_table(count_sub, count_levels):
    table = np.zeros((count_sub, count_levels))

    def add_slope(position_row, level, factor):
        if level == 0:
            table[position_row, 1] += factor
            table[position_row, 0] -= factor
        elif level == count_levels - 1:
            table[position_row, level] += factor
            table[position_row, level - 1] -= factor
        else:
            table[position_row, level + 1] += 0.5 * factor
            table[position_row, level - 1] -= 0.5 * factor

    for substep in range(count_sub):
        position = (substep + 0.5) * (count_levels - 1) / count_sub
        lower = min(int(math.floor(position)), count_levels - 2)
        fraction = position - lower
        table[substep, lower] += 2 * fraction**3 - 3 * fraction**2 + 1
        table[substep, lower + 1] += -2 * fraction**3 + 3 * fraction**2
        add_slope(substep, lower, fraction**3 - 2 * fraction**2 + fraction)
        add_slope(substep, lower + 1, fraction**3 - fraction**2)
    return table


WIDTHS = [2 * (SUB - s) - (1 if f < 2 else 2) for s in range(SUB) for f in range(DYN)]
WIDTHS += [2 * SUB, 2 * SUB - 1, 2 * SUB - 1, 2 * SUB - 1]
PLANES = SUB * DYN
ITEMS = len(WIDTHS)
ROW_AT = np.concatenate([[0], np.cumsum(WIDTHS)]).tolist()
LANE_AT = ROW_AT[:PLANES] + [ROW_AT[i] - ROW_AT[PLANES] for i in range(PLANES, ITEMS)]
CORNERS = [max(w - 1, 0) for w in WIDTHS]
CORNER_AT = np.concatenate([[0], np.cumsum(CORNERS)]).tolist()
MAIN = -(-ROW_AT[-1] // 8) * 8
GROUPS = 3


def interp_kernel(table, mean, rows, atmo_ref, out_ref, half_ref):
    fields, levels, tiles, _ = atmo_ref.shape
    for f in range(fields):
        level = [atmo_ref[f, k] for k in range(levels)]
        if f < DYN:
            for s in range(SUB):
                terms = [float(table[s, k]) * level[k] for k in range(levels) if table[s, k] != 0]
                out_ref[pl.ds(s * DYN + f, tiles, stride=rows), :] = functools.reduce(jnp.add, terms)
        else:
            terms = [float(mean[k]) * level[k] for k in range(levels)]
            out_ref[pl.ds(PLANES + f - DYN, tiles, stride=rows), :] = functools.reduce(jnp.add, terms)
    part = half_ref.shape[0]
    half_ref[...] = out_ref[pl.ds(pl.multiple_of(lax.axis_index("col") % 2 * part, 8), part), :]


def split_tiles(source_ref, split_ref, base, rows):
    tiles = source_ref.shape[0] // rows
    for g in range(tiles):
        value = source_ref[g * rows : min(g * rows + 32, source_ref.shape[0]), :]
        if value.shape[0] < 32:
            value = jnp.concatenate([value, jnp.zeros((32 - value.shape[0], value.shape[1]), value.dtype)], axis=0)
        high = value.astype(jnp.bfloat16)
        split_ref[base + g, 0:32, :] = high
        split_ref[base + g, 32:64, :] = (value - high.astype(jnp.float32)).astype(jnp.bfloat16)


def split_weights(wa, wb):
    weights = jnp.concatenate([wa, wb], axis=0)
    high = weights.astype(jnp.bfloat16)
    low = (weights - high.astype(jnp.float32)).astype(jnp.bfloat16)
    return jnp.concatenate([high, low], axis=1)


def remap_row(split_ref, first, second, weights):
    left = jnp.concatenate([split_ref[first], split_ref[second]], axis=1)
    both = jnp.dot(left, weights, preferred_element_type=jnp.float32)
    wide = weights.shape[1] // 2
    return both[0:32, :wide] + both[32:64, :wide] + both[0:32, wide:]


def own_kernel(rows, tiles_ref, own_ref, weight_ref, acc_ref, rest_ref, split_ref):
    index = tiles_ref[...] - split_ref.shape[0]
    split_tiles(own_ref, split_ref, 0, rows)
    for x in range(weight_ref.shape[0]):
        first, second = index[1, x], index[2, x]
        weights = split_weights(weight_ref[x, 1], weight_ref[x, 2])
        acc_ref[:, x, :] = remap_row(split_ref, first, second, weights)
        rest_ref[x] = split_weights(weight_ref[x, 0], weight_ref[x, 3])


def rim_kernel(rows, tiles_ref, two_far_ref, two_ref, one_far_ref, one_ref, rest_ref, own_ref, state_ref, mask_ref,
               total_ref, main1_ref, main2_ref, edge1_ref, edge2_ref, split_ref):
    part = split_ref.shape[0] // 4
    for k, ref in enumerate((one_ref, one_far_ref, two_ref, two_far_ref)):
        split_tiles(ref, split_ref, k * part, rows)
    row_odd, col_odd = lax.axis_index("row") % 2, lax.axis_index("col") % 2
    names = tiles_ref[...]
    place = lambda name: name % part + part * ((name // part + col_odd) % 2)
    before = place(names) + 2 * part * (1 - row_odd)
    after = place(names - 4 * part) + 2 * part * row_odd
    for x in range(rest_ref.shape[0]):
        total_ref[:, x, :] = remap_row(split_ref, before[0, x], after[3, x], rest_ref[x]) + own_ref[:, x, :]

    items = [total_ref[p] for p in range(PLANES)] + [state_ref[k] for k in range(DYN)] + [mask_ref[...].astype(jnp.float32)]
    high, wide = mask_ref.shape
    row_even, col_even = row_odd == 0, col_odd == 0

    for i, value in enumerate(items):
        w, at = WIDTHS[i], ROW_AT[i]
        if w:
            down, up = value[high - w :], value[:w]
            main1_ref[at : at + w, :] = jnp.where(row_even, down, up)
            main2_ref[at : at + w, :] = jnp.where(row_even, up, down)
    for ref in (main1_ref, main2_ref):
        ref[ROW_AT[-1] :, :] = jnp.zeros((MAIN - ROW_AT[-1], wide), jnp.float32)

    lane = lax.broadcasted_iota(jnp.int32, (high, wide), 1)
    groups = ((range(PLANES), WIDTHS, LANE_AT), (range(PLANES, ITEMS), WIDTHS, LANE_AT), (range(ITEMS), CORNERS, CORNER_AT))
    for g, (members, widths, places) in enumerate(groups):
        last = jnp.zeros((high, wide), jnp.float32)
        head = jnp.zeros((high, wide), jnp.float32)
        for i in members:
            w, at = widths[i], places[i]
            if w:
                last = jnp.where(lane >= at, pltpu.roll(items[i], (at + w) % wide, 1), last)
                head = jnp.where(lane >= at, pltpu.roll(items[i], at, 1), head)
        edge1_ref[g * high : (g + 1) * high, :] = jnp.where(col_even, last, head)
        edge2_ref[g * high : (g + 1) * high, :] = jnp.where(col_even, head, last)


def ocean_kernel(force_ref, state_ref, mask_ref, edge1_ref, edge2_ref, two_ref, one_ref, out_ref, top_ref, low_ref):
    high, wide = mask_ref.shape
    row_even, col_even = lax.axis_index("row") % 2 == 0, lax.axis_index("col") % 2 == 0
    one, two = one_ref[...], two_ref[...]
    top_ref[...] = jnp.where(row_even, two, one)
    low_ref[...] = jnp.where(row_even, one, two)
    second = high + MAIN
    lane = lax.broadcasted_iota(jnp.int32, (high, wide), 1)

    def sides(a, b):
        return jnp.where(col_even, b, a), jnp.where(col_even, a, b)

    beside = [sides(edge1_ref[g * high : (g + 1) * high], edge2_ref[g * high : (g + 1) * high]) for g in range(2)]
    above = sides(top_ref[:high], top_ref[second:])
    below = sides(low_ref[:high], low_ref[second:])

    def edge(pair, w, at):
        left, right = pair
        if w == 0:
            return jnp.zeros_like(left)
        return jnp.where(lane < wide // 2, pltpu.roll(right, (wide - at) % wide, 1), pltpu.roll(left, (2 * wide - w - at) % wide, 1))

    def extended(i, own, rim):
        w, start = WIDTHS[i], high + ROW_AT[i]
        main = [top_ref[start + w - rim : start + w, :], own, low_ref[start : start + rim, :]]
        rest = [
            edge(above, CORNERS[i], CORNER_AT[i])[high - rim :],
            edge(beside[0 if i < PLANES else 1], w, LANE_AT[i]),
            edge(below, CORNERS[i], CORNER_AT[i])[:rim],
        ]
        return jnp.concatenate([jnp.concatenate(main, axis=0), jnp.concatenate(rest, axis=0)], axis=1)

    before = lambda v, axis: pltpu.roll(v, 1, axis)
    after = lambda v, axis: pltpu.roll(v, v.shape[axis] - 1, axis)
    rim = high
    height = extended(PLANES, state_ref[0], rim)
    zonal = extended(PLANES + 1, state_ref[1], rim)
    merid = extended(PLANES + 2, state_ref[2], rim)
    ocean = extended(PLANES + 3, mask_ref[...].astype(jnp.float32), rim)
    for s in range(SUB):
        reach = -(-2 * (SUB - s) // 8) * 8
        if reach < rim:
            cut = rim - reach
            height, zonal, merid, ocean = (v[cut : v.shape[0] - cut] for v in (height, zonal, merid, ocean))
            rim = reach
        push_u, push_v, push_h = (extended(s * DYN + f, force_ref[s * DYN + f], rim) for f in range(DYN))
        grad_x = (after(height, 0) - before(height, 0)) * 0.5
        grad_y = (after(height, 1) - before(height, 1)) * 0.5
        zonal = ocean * (zonal - grad_x + 0.2 * merid + 0.5 * push_u)
        merid = ocean * (merid - grad_y - 0.2 * zonal + 0.5 * push_v)
        spread = (after(zonal, 0) - before(zonal, 0)) * 0.5 + (after(merid, 1) - before(merid, 1)) * 0.5
        height = height - spread + 0.5 * push_h
    for k, value in enumerate((height, zonal, merid)):
        out_ref[k] = value[rim : rim + high, :wide]


def per_device(size_row, size_col, atmo_states, remap_weights, intersection_tiles, land_mask, ocean_state):
    fields, levels, tiles, cells = atmo_states.shape
    high, wide = land_mask.shape
    rows = PLANES + fields - DYN
    vmem = pl.BlockSpec(memory_space=pltpu.VMEM)
    f32 = lambda *shape: jax.ShapeDtypeStruct(shape, jnp.float32)
    params = lambda: pltpu.CompilerParams(vmem_limit_bytes=32 << 20)

    def pairs(size):
        near = [(i, i ^ 1) for i in range(size)]
        far = [(i, (i + 1) % size if i % 2 else (i - 1) % size) for i in range(size)]
        return near, far

    row_near, row_far = pairs(size_row)
    col_near, col_far = pairs(size_col)
    half = tiles // 2
    names = intersection_tiles.T

    table = hermite_table(SUB, levels).astype(np.float32)
    mean = table.astype(np.float64).mean(axis=0)
    own, part = pl.pallas_call(
        functools.partial(interp_kernel, table, mean, rows),
        out_shape=(f32(tiles * rows, cells), f32(half * rows, cells)),
        in_specs=[vmem],
        out_specs=(vmem, vmem),
        compiler_params=params(),
        cost_estimate=pl.CostEstimate(flops=10**10, bytes_accessed=4 << 20, transcendentals=0),
    )(atmo_states)
    one = lax.ppermute(part, "row", row_near)
    two = lax.ppermute(part, "row", row_far)

    acc, rest = pl.pallas_call(
        functools.partial(own_kernel, rows),
        out_shape=(f32(32, high, wide), jax.ShapeDtypeStruct((high, 2 * cells, 2 * wide), jnp.bfloat16)),
        in_specs=[vmem] * 3,
        out_specs=(vmem, vmem),
        scratch_shapes=[pltpu.VMEM((tiles, 64, cells), jnp.bfloat16)],
        compiler_params=params(),
        cost_estimate=pl.CostEstimate(flops=10**9, bytes_accessed=4 << 20, transcendentals=0),
    )(names, own, remap_weights)

    two, one, acc, rest = lax.optimization_barrier((two, one, acc, rest))
    one_far = lax.ppermute(one, "col", col_near)
    two_far = lax.ppermute(two, "col", col_near)

    total, main1, main2, edge1, edge2 = pl.pallas_call(
        functools.partial(rim_kernel, rows),
        out_shape=(f32(32, high, wide), f32(MAIN, wide), f32(MAIN, wide), f32(GROUPS * high, wide), f32(GROUPS * high, wide)),
        in_specs=[vmem] * 9,
        out_specs=(vmem,) * 5,
        scratch_shapes=[pltpu.VMEM((2 * tiles, 64, cells), jnp.bfloat16)],
        compiler_params=params(),
        cost_estimate=pl.CostEstimate(flops=10**9, bytes_accessed=4 << 20, transcendentals=0),
    )(names, two_far, two, one_far, one, rest, acc, ocean_state, land_mask)
    forced = total[:PLANES].reshape(SUB, DYN, high, wide)
    flux_mean = jnp.concatenate([jnp.mean(forced, axis=0), total[PLANES:rows]], axis=0)

    from2 = lax.ppermute(edge2, "col", col_far)
    from1 = lax.ppermute(edge1, "col", col_near)
    join = lambda main: jnp.concatenate([from1[2 * high :], main, from2[2 * high :]], axis=0)
    rim2 = lax.ppermute(join(main2), "row", row_far)
    rim1 = lax.ppermute(join(main1), "row", row_near)

    length = 2 * high + MAIN
    final = pl.pallas_call(
        ocean_kernel,
        out_shape=f32(3, high, wide),
        in_specs=[vmem] * 7,
        out_specs=vmem,
        scratch_shapes=[pltpu.VMEM((length, wide), jnp.float32)] * 2,
        compiler_params=params(),
    )(total, ocean_state, land_mask, from1, from2, rim2, rim1)
    return flux_mean, final


def solution(mesh):
    placed = (
        P(None, None, "row", None),
        P("row", "col", None, None),
        P("row", "col"),
        P("row", "col"),
        P(None, "row", "col"),
    )
    return jax.shard_map(
        functools.partial(per_device, mesh.shape["row"], mesh.shape["col"]),
        mesh=mesh,
        in_specs=placed,
        out_specs=(P(None, "row", "col"), P(None, "row", "col")),
        check_vma=False,
    )
```

time: 154 us -> 27.9 us (0.18)
  waiting for transfers between devices: 96.9 us -> 9.12 us
  starting transfers between devices: 38.3 us -> 12.4 us
  matrix products: 8.5 us -> 0 us
  local copies, waits for them, and re-layouts: 6.57 us -> 1.38 us
  Pallas kernels: 0 us -> 3.42 us
    ppermute x50 -> x8, waiting for transfers between devices: 96.9 us -> 9.12 us  [the longest x1 2.97 us: per_device(): two = lax.ppermute(part, 'row', row_far)]
    ppermute x50 -> x8, starting transfers between devices: 38.3 us -> 12.4 us  [the longest x1 3.61 us: per_device(): rim2 = lax.ppermute(join(main2), 'row', row_far)]
    dot_general x2 -> x0, matrix products: 8.5 us -> none  [the longest x1 6.83 us: per_device(): jnp.einsum('fsrqa,rqao->sfro', picked, remap_weights, precision=highest)]
    pallas_call x0 -> x4, Pallas kernels: none -> 3.42 us  [the longest x1 1.65 us: per_device(): pl.pallas_call(ocean_kernel, out_shape=f32(3, high, wide), in_specs=[vmem...]
    gather x1 -> x0, local copies, waits for them, and re-layouts: 2.35 us -> none  [per_device(): picked = window[:, :, intersection_tiles, :]]
  transfers between devices with their start and end apart: 50 -> 8, of which waited for: 45 -> 6; matrix products, arithmetic and copies ran while one was open for 7% -> 2% of each run, Pallas kernels for 0% -> 3%
where the time goes in v2:
time: 27.9 us; the launch traced here: 27.8 us
  starting transfers between devices  12.4 us (44%)
  waiting for transfers between devices  9.12 us (33%)
  Pallas kernels  3.42 us (12%)
  local copies, waits for them, and re-layouts  1.38 us (5%)
  between operations  0.76 us (3%)
  other arithmetic  0.67 us (2%)
    ppermute x1, starting transfers between devices, per_device(): rim2 = lax.ppermute(join(main2), 'row', row_far)  3.61 us
    ppermute x1, starting transfers between devices, per_device(): two = lax.ppermute(part, 'row', row_far)  3.54 us
    ppermute x1, starting transfers between devices, per_device(): one = lax.ppermute(part, 'row', row_near)  3.03 us
    ppermute x1, waiting for transfers between devices, per_device(): two = lax.ppermute(part, 'row', row_far)  2.97 us
    ppermute x1, waiting for transfers between devices, per_device(): rim2 = lax.ppermute(join(main2), 'row', row_far)  2.77 us
    ppermute x1, waiting for transfers between devices, per_device(): from2 = lax.ppermute(edge2, 'col', col_far)  1.92 us
    pallas_call x1, Pallas kernels, per_device(): pl.pallas_call(ocean_kernel, out_shape=f32(3, high, wide), in_specs=[vmem...  1.65 us
    unnamed x10, local copies, waits for them, and re-layouts  1.36 us
  transfers between devices with their start and end apart: 8, of which 6 were waited for; matrix products, arithmetic and copies ran while one was open for 2% of the time, Pallas kernels for 3%

profile of v2, /device:TPU:0, one launch (start us, length us, event | category | flops | bytes accessed | tf_op | source)
XLA Modules:
  0.0 27.8 jit_solution(5600271060946273822)
XLA Ops:
  0.6 0.0 copy-start.3
  0.6 0.0 copy-start
  0.6 0.0 copy-start.4
  0.7 1.3 %copy-done.4 = f32[10,12,16,128]{3,2,1,0:T(8,128)S(1)} copy-done((f32[10,12,16,128]{3,2,1,0:T(8,128)S(1)}, f32[10,12,16,128]{3,2,1,0:T(8,128)}, u32[]{:S(2)}) %copy-start.4) | copy-done | bytes 983064
  2.0 0.1 shard_map.68
  2.1 0.0 copy-start.1
  2.1 0.0 copy-start.2
  2.1 3.0 %collective-permute-start.1 = (f32[200,128]{1,0:T(8,128)S(1)}, f32[200,128]{1,0:T(8,128)S(1)}, u32[]{:S(2)}, u32[]{:S(2)}) collective-permute-start(f32[200,128]{1,0:T(8,128)S(1)} %get-tuple-element.15), channel_id=1, source_target_pairs={{0,4},{4,0},{8,12},{12,8},{16,20},{20,16},{24,28},{28,24},{1,5},{5... | collective-permute-start | bytes 307208 | tf_op jit(solution)/shard_map/ppermute | solution.py:227
  5.2 3.5 %collective-permute-start = (f32[200,128]{1,0:T(8,128)S(1)}, f32[200,128]{1,0:T(8,128)S(1)}, u32[]{:S(2)}, u32[]{:S(2)}) collective-permute-start(f32[200,128]{1,0:T(8,128)S(1)} %get-tuple-element.15), channel_id=1, source_target_pairs={{0,28},{4,8},{8,4},{12,16},{16,12},{20,24},{24,20},{28,0},{1,29},{... | collective-permute-start | bytes 307208 | tf_op jit(solution)/shard_map/ppermute | solution.py:228
  8.7 0.0 copy-done.3
  8.7 0.0 copy-done
  8.7 0.8 %shard_map.69 = (f32[32,16,128]{2,1,0:T(8,128)S(1)}, bf16[16,256,256]{2,1,0:T(8,128)(2,1)S(1)}) custom-call(s32[4,16]{1,0:T(4,128)S(1)} %bitcast.2, f32[400,128]{1,0:T(8,128)S(1)} %get-tuple-element.16.own_ref, f32[16,4,128,128]{3,2,1,0:T(8,128)S(1)} %copy-done), custom_call_target="tpu_custom_call" | custom-call | flops 1000000000 | bytes 4194304 | tf_op jit(solution)/shard_map/pallas_call | solution.py:230
  9.5 0.0 collective-permute-done.1.one_ref
  9.5 3.0 %collective-permute-done.two_ref = f32[200,128]{1,0:T(8,128)S(1)} collective-permute-done((f32[200,128]{1,0:T(8,128)S(1)}, f32[200,128]{1,0:T(8,128)S(1)}, u32[]{:S(2)}, u32[]{:S(2)}) %collective-permute-start) | collective-permute-done | bytes 102432 | tf_op jit(solution)/shard_map/ppermute | solution.py:228
  12.5 0.0 collective-permute-start.2
  12.5 0.5 %collective-permute-start.3 = (f32[200,128]{1,0:T(8,128)S(1)}, f32[200,128]{1,0:T(8,128)S(1)}, u32[]{:S(2)}, u32[]{:S(2)}) collective-permute-start(f32[200,128]{1,0:T(8,128)S(1)} %collective-permute-done.1.one_ref), channel_id=1, source_target_pairs={{0,1},{1,0},{2,3},{3,2},{4,5},{5,4},{6,7},{7,6},{8,9},{9,8},{10,11... | collective-permute-start | bytes 307208 | tf_op jit(solution)/shard_map/ppermute | solution.py:241
  13.0 0.8 %collective-permute-done.2.two_far_ref = f32[200,128]{1,0:T(8,128)S(1)} collective-permute-done((f32[200,128]{1,0:T(8,128)S(1)}, f32[200,128]{1,0:T(8,128)S(1)}, u32[]{:S(2)}, u32[]{:S(2)}) %collective-permute-start.2) | collective-permute-done | bytes 102432 | tf_op jit(solution)/shard_map/ppermute | solution.py:242
  13.8 0.2 collective-permute-done.3.one_far_ref
  14.0 0.0 copy-done.1
  14.0 0.0 copy-done.2
  14.0 0.9 %shard_map.70 = (f32[32,16,128]{2,1,0:T(8,128)S(1)}, f32[152,128]{1,0:T(8,128)S(1)}, f32[152,128]{1,0:T(8,128)S(1)}, f32[48,128]{1,0:T(8,128)S(1)}, f32[48,128]{1,0:T(8,128)S(1)}) custom-call(s32[4,16]{1,0:T(4,128)S(1)} %bitcast.3, f32[200,128]{1,0:T(8,128)S(1)} %collective-permute-done.2.two_far_ref, f32[200,128]{1,0:T(8,128)S(1)} %collective-permute-done.two_ref, ...), custom_call_target="tpu_custom_call" | custom-call | flops 1000000000 | bytes 4194304 | tf_op jit(solution)/shard_map/pallas_call | solution.py:244
  14.8 0.4 %collective-permute-start.4 = (f32[48,128]{1,0:T(8,128)S(1)}, f32[48,128]{1,0:T(8,128)S(1)}, u32[]{:S(2)}, u32[]{:S(2)}) collective-permute-start(f32[48,128]{1,0:T(8,128)S(1)} %get-tuple-element.24), channel_id=1, source_target_pairs={{0,1},{1,0},{2,3},{3,2},{4,5},{5,4},{6,7},{7,6},{8,9},{9,8},{10,11... | collective-permute-start | bytes 73736 | tf_op jit(solution)/shard_map/ppermute | solution.py:257
  15.3 1.2 %collective-permute-start.5 = (f32[48,128]{1,0:T(8,128)S(1)}, f32[48,128]{1,0:T(8,128)S(1)}, u32[]{:S(2)}, u32[]{:S(2)}) collective-permute-start(f32[48,128]{1,0:T(8,128)S(1)} %get-tuple-element.25), channel_id=1, source_target_pairs={{0,3},{1,2},{2,1},{3,0},{4,7},{5,6},{6,5},{7,4},{8,11},{9,10},{10,... | collective-permute-start | bytes 73736 | tf_op jit(solution)/shard_map/ppermute | solution.py:256
  16.6 0.0 collective-permute-done.4.edge1_ref
  16.6 1.9 %collective-permute-done.5.edge2_ref = f32[48,128]{1,0:T(8,128)S(1)} collective-permute-done((f32[48,128]{1,0:T(8,128)S(1)}, f32[48,128]{1,0:T(8,128)S(1)}, u32[]{:S(2)}, u32[]{:S(2)}) %collective-permute-start.5) | collective-permute-done | bytes 24608 | tf_op jit(solution)/shard_map/ppermute | solution.py:256
  18.5 0.1 collective-permute-start.7
  18.6 3.6 %collective-permute-start.6 = (f32[184,128]{1,0:T(8,128)S(1)}, f32[184,128]{1,0:T(8,128)S(1)}, u32[]{:S(2)}, u32[]{:S(2)}) collective-permute-start(f32[184,128]{1,0:T(8,128)S(1)} %get-tuple-element.29), channel_id=1, source_target_pairs={{0,28},{4,8},{8,4},{12,16},{16,12},{20,24},{24,20},{28,0},{1,29},{... | collective-permute-start | bytes 282632 | tf_op jit(solution)/shard_map/ppermute | solution.py:259
  22.2 0.6 %pad_maximum_fusion.4 = f32[10,16,128]{2,1,0:T(8,128)} fusion(f32[7,16,128]{2,1,0:T(8,128)S(1)} %slice.15, f32[3,16,128]{2,1,0:T(8,128)S(1)} %broadcast_multiply_fusion), kind=kLoop, calls=%fused_computation.4 | loop fusion | flops 20480 | bytes 163840 | tf_op jit(solution)/shard_map/concatenate | solution.py:254
  22.9 0.5 %collective-permute-done.7.one_ref = f32[184,128]{1,0:T(8,128)S(1)} collective-permute-done((f32[184,128]{1,0:T(8,128)S(1)}, f32[184,128]{1,0:T(8,128)S(1)}, u32[]{:S(2)}, u32[]{:S(2)}) %collective-permute-start.7) | collective-permute-done | bytes 94240 | tf_op jit(solution)/shard_map/ppermute | solution.py:260
  23.4 2.8 %collective-permute-done.6.two_ref = f32[184,128]{1,0:T(8,128)S(1)} collective-permute-done((f32[184,128]{1,0:T(8,128)S(1)}, f32[184,128]{1,0:T(8,128)S(1)}, u32[]{:S(2)}, u32[]{:S(2)}) %collective-permute-start.6) | collective-permute-done | bytes 94240 | tf_op jit(solution)/shard_map/ppermute | solution.py:259
  26.1 1.6 %shard_map.71 = f32[3,16,128]{2,1,0:T(8,128)} custom-call(f32[32,16,128]{2,1,0:T(8,128)S(1)} %get-tuple-element.23.force_ref, f32[3,16,128]{2,1,0:T(8,128)S(1)} %copy-done.1, s32[16,128]{1,0:T(8,128)S(1)} %copy-done.2, f32[48,128]{1,0:T(8,128)S(1)} %collective-permute-done.4.edge1_ref, f32[48,128]{1,0:T(8,128)S(1)} %collective-permute-done.5.edge2_ref, ...), custom_call_target="tpu_custom_call" | custom-call | tf_op jit(solution)/shard_map/pallas_call | solution.py:263
  (7 shorter events, 0.1 us)
Async XLA Ops:
  0.6 8.1 %copy-start.3 = (s32[16,4]{0,1:T(4,128)S(1)}, s32[16,4]{0,1:T(4,128)}, u32[]{:S(2)}) copy-start(s32[16,4]{0,1:T(4,128)} %param.7) | copy-start | bytes 772
  0.6 8.1 %copy-start = (f32[16,4,128,128]{3,2,1,0:T(8,128)S(1)}, f32[16,4,128,128]{3,2,1,0:T(8,128)}, u32[]{:S(2)}) copy-start(f32[16,4,128,128]{3,2,1,0:T(8,128)} %weight_ref.1) | copy-start | bytes 12582916
  0.6 1.4 %copy-start.4 = (f32[10,12,16,128]{3,2,1,0:T(8,128)S(1)}, f32[10,12,16,128]{3,2,1,0:T(8,128)}, u32[]{:S(2)}) copy-start(f32[10,12,16,128]{3,2,1,0:T(8,128)} %atmo_ref.1) | copy-start | bytes 2949124
  2.1 11.9 %copy-start.1 = (f32[3,16,128]{2,1,0:T(8,128)S(1)}, f32[3,16,128]{2,1,0:T(8,128)}, u32[]{:S(2)}) copy-start(f32[3,16,128]{2,1,0:T(8,128)} %state_ref.3) | copy-start | bytes 73732
  2.1 11.9 %copy-start.2 = (s32[16,128]{1,0:T(8,128)S(1)}, s32[16,128]{1,0:T(8,128)}, u32[]{:S(2)}) copy-start(s32[16,128]{1,0:T(8,128)} %mask_ref.3) | copy-start | bytes 24580
  2.1 7.4 %collective-permute-start.1 = (f32[200,128]{1,0:T(8,128)S(1)}, f32[200,128]{1,0:T(8,128)S(1)}, u32[]{:S(2)}, u32[]{:S(2)}) collective-permute-start(f32[200,128]{1,0:T(8,128)S(1)} %get-tuple-element.15), channel_id=1, source_target_pairs={{0,4},{4,0},{8,12},{12,8},{16,20},{20,16},{24,28},{28,24},{1,5},{5... | collective-permute-start | bytes 307208 | tf_op jit(solution)/shard_map/ppermute | solution.py:227
  5.2 7.4 %collective-permute-start = (f32[200,128]{1,0:T(8,128)S(1)}, f32[200,128]{1,0:T(8,128)S(1)}, u32[]{:S(2)}, u32[]{:S(2)}) collective-permute-start(f32[200,128]{1,0:T(8,128)S(1)} %get-tuple-element.15), channel_id=1, source_target_pairs={{0,28},{4,8},{8,4},{12,16},{16,12},{20,24},{24,20},{28,0},{1,29},{... | collective-permute-start | bytes 307208 | tf_op jit(solution)/shard_map/ppermute | solution.py:228
  12.5 1.3 %collective-permute-start.2 = (f32[200,128]{1,0:T(8,128)S(1)}, f32[200,128]{1,0:T(8,128)S(1)}, u32[]{:S(2)}, u32[]{:S(2)}) collective-permute-start(f32[200,128]{1,0:T(8,128)S(1)} %collective-permute-done.two_ref), channel_id=1, source_target_pairs={{0,1},{1,0},{2,3},{3,2},{4,5},{5,4},{6,7},{7,6},{8,9},{9,8},{10,11... | collective-permute-start | bytes 307208 | tf_op jit(solution)/shard_map/ppermute | solution.py:242
  12.5 1.5 %collective-permute-start.3 = (f32[200,128]{1,0:T(8,128)S(1)}, f32[200,128]{1,0:T(8,128)S(1)}, u32[]{:S(2)}, u32[]{:S(2)}) collective-permute-start(f32[200,128]{1,0:T(8,128)S(1)} %collective-permute-done.1.one_ref), channel_id=1, source_target_pairs={{0,1},{1,0},{2,3},{3,2},{4,5},{5,4},{6,7},{7,6},{8,9},{9,8},{10,11... | collective-permute-start | bytes 307208 | tf_op jit(solution)/shard_map/ppermute | solution.py:241
  14.8 1.7 %collective-permute-start.4 = (f32[48,128]{1,0:T(8,128)S(1)}, f32[48,128]{1,0:T(8,128)S(1)}, u32[]{:S(2)}, u32[]{:S(2)}) collective-permute-start(f32[48,128]{1,0:T(8,128)S(1)} %get-tuple-element.24), channel_id=1, source_target_pairs={{0,1},{1,0},{2,3},{3,2},{4,5},{5,4},{6,7},{7,6},{8,9},{9,8},{10,11... | collective-permute-start | bytes 73736 | tf_op jit(solution)/shard_map/ppermute | solution.py:257
  15.3 3.3 %collective-permute-start.5 = (f32[48,128]{1,0:T(8,128)S(1)}, f32[48,128]{1,0:T(8,128)S(1)}, u32[]{:S(2)}, u32[]{:S(2)}) collective-permute-start(f32[48,128]{1,0:T(8,128)S(1)} %get-tuple-element.25), channel_id=1, source_target_pairs={{0,3},{1,2},{2,1},{3,0},{4,7},{5,6},{6,5},{7,4},{8,11},{9,10},{10,... | collective-permute-start | bytes 73736 | tf_op jit(solution)/shard_map/ppermute | solution.py:256
  18.5 4.8 %collective-permute-start.7 = (f32[184,128]{1,0:T(8,128)S(1)}, f32[184,128]{1,0:T(8,128)S(1)}, u32[]{:S(2)}, u32[]{:S(2)}) collective-permute-start(f32[184,128]{1,0:T(8,128)S(1)} %get-tuple-element.28), channel_id=1, source_target_pairs={{0,4},{4,0},{8,12},{12,8},{16,20},{20,16},{24,28},{28,24},{1,5},{5... | collective-permute-start | bytes 282632 | tf_op jit(solution)/shard_map/ppermute | solution.py:260
  18.6 7.5 %collective-permute-start.6 = (f32[184,128]{1,0:T(8,128)S(1)}, f32[184,128]{1,0:T(8,128)S(1)}, u32[]{:S(2)}, u32[]{:S(2)}) collective-permute-start(f32[184,128]{1,0:T(8,128)S(1)} %get-tuple-element.29), channel_id=1, source_target_pairs={{0,28},{4,8},{8,4},{12,16},{16,12},{20,24},{24,20},{28,0},{1,29},{... | collective-permute-start | bytes 282632 | tf_op jit(solution)/shard_map/ppermute | solution.py:259

commit v3 on v2

--- a/solution.py
+++ b/solution.py
@@ -100,30 +100,29 @@
         rest_ref[x] = split_weights(weight_ref[x, 0], weight_ref[x, 3])
 
 
-def rim_kernel(rows, tiles_ref, two_far_ref, two_ref, one_far_ref, one_ref, rest_ref, own_ref, state_ref, mask_ref,
-               total_ref, main1_ref, main2_ref, edge1_ref, edge2_ref, split_ref):
+def rim_kernel(rows, tiles_ref, near_ref, far_ref, rest_ref, own_ref, state_ref, mask_ref,
+               total_ref, down_ref, up_ref, edge1_ref, edge2_ref, split_ref):
     part = split_ref.shape[0] // 4
-    for k, ref in enumerate((one_ref, one_far_ref, two_ref, two_far_ref)):
-        split_tiles(ref, split_ref, k * part, rows)
-    row_odd, col_odd = lax.axis_index("row") % 2, lax.axis_index("col") % 2
+    for side in range(2):
+        split_tiles(near_ref.at[side], split_ref, 2 * side * part, rows)
+        split_tiles(far_ref.at[side], split_ref, (2 * side + 1) * part, rows)
+    col_odd = lax.axis_index("col") % 2
     names = tiles_ref[...]
     place = lambda name: name % part + part * ((name // part + col_odd) % 2)
-    before = place(names) + 2 * part * (1 - row_odd)
-    after = place(names - 4 * part) + 2 * part * row_odd
+    before, after = place(names), place(names - 4 * part) + 2 * part
     for x in range(rest_ref.shape[0]):
         total_ref[:, x, :] = remap_row(split_ref, before[0, x], after[3, x], rest_ref[x]) + own_ref[:, x, :]
 
     items = [total_ref[p] for p in range(PLANES)] + [state_ref[k] for k in range(DYN)] + [mask_ref[...].astype(jnp.float32)]
     high, wide = mask_ref.shape
-    row_even, col_even = row_odd == 0, col_odd == 0
+    col_even = col_odd == 0
 
     for i, value in enumerate(items):
         w, at = WIDTHS[i], ROW_AT[i]
         if w:
-            down, up = value[high - w :], value[:w]
-            main1_ref[at : at + w, :] = jnp.where(row_even, down, up)
-            main2_ref[at : at + w, :] = jnp.where(row_even, up, down)
-    for ref in (main1_ref, main2_ref):
+            down_ref[at : at + w, :] = value[high - w :]
+            up_ref[at : at + w, :] = value[:w]
+    for ref in (down_ref, up_ref):
         ref[ROW_AT[-1] :, :] = jnp.zeros((MAIN - ROW_AT[-1], wide), jnp.float32)
 
     lane = lax.broadcasted_iota(jnp.int32, (high, wide), 1)
@@ -140,12 +139,9 @@
         edge2_ref[g * high : (g + 1) * high, :] = jnp.where(col_even, head, last)
 
 
-def ocean_kernel(force_ref, state_ref, mask_ref, edge1_ref, edge2_ref, two_ref, one_ref, out_ref, top_ref, low_ref):
+def ocean_kernel(force_ref, state_ref, mask_ref, edge1_ref, edge2_ref, low_ref, corner_ref, top_ref, out_ref):
     high, wide = mask_ref.shape
-    row_even, col_even = lax.axis_index("row") % 2 == 0, lax.axis_index("col") % 2 == 0
-    one, two = one_ref[...], two_ref[...]
-    top_ref[...] = jnp.where(row_even, two, one)
-    low_ref[...] = jnp.where(row_even, one, two)
+    col_even = lax.axis_index("col") % 2 == 0
     second = high + MAIN
     lane = lax.broadcasted_iota(jnp.int32, (high, wide), 1)
 
@@ -153,7 +149,7 @@
         return jnp.where(col_even, b, a), jnp.where(col_even, a, b)
 
     beside = [sides(edge1_ref[g * high : (g + 1) * high], edge2_ref[g * high : (g + 1) * high]) for g in range(2)]
-    above = sides(top_ref[:high], top_ref[second:])
+    above = sides(corner_ref[:high], corner_ref[high:])
     below = sides(low_ref[:high], low_ref[second:])
 
     def edge(pair, w, at):
@@ -163,8 +159,10 @@
         return jnp.where(lane < wide // 2, pltpu.roll(right, (wide - at) % wide, 1), pltpu.roll(left, (2 * wide - w - at) % wide, 1))
 
     def extended(i, own, rim):
-        w, start = WIDTHS[i], high + ROW_AT[i]
-        main = [top_ref[start + w - rim : start + w, :], own, low_ref[start : start + rim, :]]
+        w, at = WIDTHS[i], ROW_AT[i]
+        room = max(rim - at - w, 0)
+        main = [jnp.zeros((room, wide), jnp.float32)] if room else []
+        main += [top_ref[at + w - rim + room : at + w, :], own, low_ref[high + at : high + at + rim, :]]
         rest = [
             edge(above, CORNERS[i], CORNER_AT[i])[high - rim :],
             edge(beside[0 if i < PLANES else 1], w, LANE_AT[i]),
@@ -204,13 +202,10 @@
     f32 = lambda *shape: jax.ShapeDtypeStruct(shape, jnp.float32)
     params = lambda: pltpu.CompilerParams(vmem_limit_bytes=32 << 20)
 
-    def pairs(size):
-        near = [(i, i ^ 1) for i in range(size)]
-        far = [(i, (i + 1) % size if i % 2 else (i - 1) % size) for i in range(size)]
-        return near, far
-
-    row_near, row_far = pairs(size_row)
-    col_near, col_far = pairs(size_col)
+    onward = [(i, (i + 1) % size_row) for i in range(size_row)]
+    back = [(j, i) for i, j in onward]
+    col_near = [(i, i ^ 1) for i in range(size_col)]
+    col_far = [(i, (i + 1) % size_col if i % 2 else (i - 1) % size_col) for i in range(size_col)]
     half = tiles // 2
     names = intersection_tiles.T
 
@@ -224,8 +219,8 @@
         compiler_params=params(),
         cost_estimate=pl.CostEstimate(flops=10**10, bytes_accessed=4 << 20, transcendentals=0),
     )(atmo_states)
-    one = lax.ppermute(part, "row", row_near)
-    two = lax.ppermute(part, "row", row_far)
+    previous = lax.ppermute(part, "row", onward)
+    following = lax.ppermute(part, "row", back)
 
     acc, rest = pl.pallas_call(
         functools.partial(own_kernel, rows),
@@ -237,37 +232,37 @@
         cost_estimate=pl.CostEstimate(flops=10**9, bytes_accessed=4 << 20, transcendentals=0),
     )(names, own, remap_weights)
 
-    two, one, acc, rest = lax.optimization_barrier((two, one, acc, rest))
-    one_far = lax.ppermute(one, "col", col_near)
-    two_far = lax.ppermute(two, "col", col_near)
-
-    total, main1, main2, edge1, edge2 = pl.pallas_call(
+    following, previous, acc, rest = lax.optimization_barrier((following, previous, acc, rest))
+    near = jnp.stack([previous, following])
+    far = lax.ppermute(near, "col", col_near)
+
+    total, down, up, edge1, edge2 = pl.pallas_call(
         functools.partial(rim_kernel, rows),
         out_shape=(f32(32, high, wide), f32(MAIN, wide), f32(MAIN, wide), f32(GROUPS * high, wide), f32(GROUPS * high, wide)),
-        in_specs=[vmem] * 9,
+        in_specs=[vmem] * 7,
         out_specs=(vmem,) * 5,
         scratch_shapes=[pltpu.VMEM((2 * tiles, 64, cells), jnp.bfloat16)],
         compiler_params=params(),
         cost_estimate=pl.CostEstimate(flops=10**9, bytes_accessed=4 << 20, transcendentals=0),
-    )(names, two_far, two, one_far, one, rest, acc, ocean_state, land_mask)
+    )(names, near, far, rest, acc, ocean_state, land_mask)
     forced = total[:PLANES].reshape(SUB, DYN, high, wide)
     flux_mean = jnp.concatenate([jnp.mean(forced, axis=0), total[PLANES:rows]], axis=0)
 
+    from1 = lax.ppermute(edge1, "col", col_near)
     from2 = lax.ppermute(edge2, "col", col_far)
-    from1 = lax.ppermute(edge1, "col", col_near)
-    join = lambda main: jnp.concatenate([from1[2 * high :], main, from2[2 * high :]], axis=0)
-    rim2 = lax.ppermute(join(main2), "row", row_far)
-    rim1 = lax.ppermute(join(main1), "row", row_near)
-
-    length = 2 * high + MAIN
+    from2, from1 = lax.optimization_barrier((from2, from1))
+    corners = from1[2 * high :], from2[2 * high :]
+    top = lax.ppermute(down, "row", onward)
+    corner = lax.ppermute(jnp.concatenate(corners), "row", onward)
+    low = lax.ppermute(jnp.concatenate([corners[0], up, corners[1]]), "row", back)
+
     final = pl.pallas_call(
         ocean_kernel,
         out_shape=f32(3, high, wide),
-        in_specs=[vmem] * 7,
+        in_specs=[vmem] * 8,
         out_specs=vmem,
-        scratch_shapes=[pltpu.VMEM((length, wide), jnp.float32)] * 2,
-        compiler_params=params(),
-    )(total, ocean_state, land_mask, from1, from2, rim2, rim1)
+        compiler_params=params(),
+    )(total, ocean_state, land_mask, from1, from2, low, corner, top)
     return flux_mean, final
 
 

time: 27.9 us -> 26.7 us (0.957)
  waiting for transfers between devices: 9.12 us -> 7.51 us
  starting transfers between devices: 12.4 us -> 12.9 us
    ppermute x6, waiting for transfers between devices: 7.2 us -> 6.12 us  [the longest x1 2.09 us: per_device(): previous = lax.ppermute(part, 'row', onward)]
    ppermute x1, waiting for transfers between devices: 1.92 us -> 1.39 us  [per_device(): from2 = lax.ppermute(edge2, 'col', col_far)]
    ppermute x6, starting transfers between devices: 10.8 us -> 11.2 us  [the longest x1 3.92 us: per_device(): lax.ppermute(jnp.concatenate([corners[0], up, corners[1]]), 'row', back)]
  transfers between devices with their start and end apart: 8 -> 8, of which waited for: 6 -> 6; matrix products, arithmetic and copies ran while one was open for 2% -> 3% of each run, Pallas kernels for 3% -> 3%
where the time goes in v3:
time: 26.7 us; the launch traced here: 26.6 us
  starting transfers between devices  12.9 us (48%)
  waiting for transfers between devices  7.51 us (28%)
  Pallas kernels  3.39 us (13%)
  local copies, waits for them, and re-layouts  1.38 us (5%)
  between operations  0.74 us (3%)
  other arithmetic  0.7 us (3%)
    ppermute x1, starting transfers between devices, per_device(): lax.ppermute(jnp.concatenate([corners[0], up, corners[1]]), 'row', back)  3.92 us
    ppermute x1, starting transfers between devices, per_device(): following = lax.ppermute(part, 'row', back)  3.1 us
    ppermute x1, starting transfers between devices, per_device(): previous = lax.ppermute(part, 'row', onward)  3.02 us
    ppermute x1, waiting for transfers between devices, per_device(): previous = lax.ppermute(part, 'row', onward)  2.09 us
    pallas_call x1, Pallas kernels, per_device(): pl.pallas_call(ocean_kernel, out_shape=f32(3, high, wide), in_specs=[vmem...  1.64 us
    ppermute x1, waiting for transfers between devices, per_device(): far = lax.ppermute(near, 'col', col_near)  1.44 us
    ppermute x1, waiting for transfers between devices, per_device(): from2 = lax.ppermute(edge2, 'col', col_far)  1.39 us
    unnamed x10, local copies, waits for them, and re-layouts  1.36 us
  transfers between devices with their start and end apart: 8, of which 6 were waited for; matrix products, arithmetic and copies ran while one was open for 3% of the time, Pallas kernels for 3%

profile of v3, /device:TPU:0, one launch (start us, length us, event | category | flops | bytes accessed | tf_op | source)
XLA Modules:
  0.0 26.6 jit_solution(13671629916771227629)
XLA Ops:
  0.6 0.0 copy-start.3
  0.6 0.0 copy-start
  0.6 0.0 copy-start.4
  0.7 1.3 %copy-done.4 = f32[10,12,16,128]{3,2,1,0:T(8,128)S(1)} copy-done((f32[10,12,16,128]{3,2,1,0:T(8,128)S(1)}, f32[10,12,16,128]{3,2,1,0:T(8,128)}, u32[]{:S(2)}) %copy-start.4) | copy-done | bytes 983064
  2.0 0.1 shard_map.68
  2.1 0.0 copy-start.1
  2.1 0.0 copy-start.2
  2.1 3.0 %collective-permute-start.1 = (f32[200,128]{1,0:T(8,128)S(1)}, f32[200,128]{1,0:T(8,128)S(1)}, u32[]{:S(2)}, u32[]{:S(2)}) collective-permute-start(f32[200,128]{1,0:T(8,128)S(1)} %get-tuple-element.17), channel_id=1, source_target_pairs={{0,4},{4,8},{8,12},{12,16},{16,20},{20,24},{24,28},{28,0},{1,5},{5... | collective-permute-start | bytes 307208 | tf_op jit(solution)/shard_map/ppermute | solution.py:222
  5.1 3.1 %collective-permute-start = (f32[200,128]{1,0:T(8,128)S(1)}, f32[200,128]{1,0:T(8,128)S(1)}, u32[]{:S(2)}, u32[]{:S(2)}) collective-permute-start(f32[200,128]{1,0:T(8,128)S(1)} %get-tuple-element.17), channel_id=1, source_target_pairs={{4,0},{8,4},{12,8},{16,12},{20,16},{24,20},{28,24},{0,28},{5,1},{9... | collective-permute-start | bytes 307208 | tf_op jit(solution)/shard_map/ppermute | solution.py:223
  8.2 0.0 copy-done.3
  8.2 0.0 copy-done
  8.3 0.8 %shard_map.69 = (f32[32,16,128]{2,1,0:T(8,128)S(1)}, bf16[16,256,256]{2,1,0:T(8,128)(2,1)S(1)}) custom-call(s32[4,16]{1,0:T(4,128)S(1)} %bitcast.4, f32[400,128]{1,0:T(8,128)S(1)} %get-tuple-element.18.own_ref, f32[16,4,128,128]{3,2,1,0:T(8,128)S(1)} %copy-done), custom_call_target="tpu_custom_call" | custom-call | flops 1000000000 | bytes 4194304 | tf_op jit(solution)/shard_map/pallas_call | solution.py:225
  9.1 2.1 %collective-permute-done.1 = f32[200,128]{1,0:T(8,128)S(1)} collective-permute-done((f32[200,128]{1,0:T(8,128)S(1)}, f32[200,128]{1,0:T(8,128)S(1)}, u32[]{:S(2)}, u32[]{:S(2)}) %collective-permute-start.1) | collective-permute-done | bytes 102432 | tf_op jit(solution)/shard_map/ppermute | solution.py:222
  11.2 0.8 %collective-permute-done = f32[200,128]{1,0:T(8,128)S(1)} collective-permute-done((f32[200,128]{1,0:T(8,128)S(1)}, f32[200,128]{1,0:T(8,128)S(1)}, u32[]{:S(2)}, u32[]{:S(2)}) %collective-permute-start) | collective-permute-done | bytes 102432 | tf_op jit(solution)/shard_map/ppermute | solution.py:223
  12.0 0.1 collective-permute-start.2
  12.1 1.4 %collective-permute-done.2.far_ref = f32[2,200,128]{2,1,0:T(8,128)S(1)} collective-permute-done((f32[2,200,128]{2,1,0:T(8,128)S(1)}, f32[2,200,128]{2,1,0:T(8,128)S(1)}, u32[]{:S(2)}, u32[]{:S(2)}) %collective-permute-start.2) | collective-permute-done | bytes 204832 | tf_op jit(solution)/shard_map/ppermute | solution.py:237
  13.5 0.0 copy-done.1
  13.5 0.0 copy-done.2
  13.5 0.8 %shard_map.70 = (f32[32,16,128]{2,1,0:T(8,128)S(1)}, f32[152,128]{1,0:T(8,128)S(1)}, f32[152,128]{1,0:T(8,128)S(1)}, f32[48,128]{1,0:T(8,128)S(1)}, f32[48,128]{1,0:T(8,128)S(1)}) custom-call(s32[4,16]{1,0:T(4,128)S(1)} %bitcast.5, f32[2,200,128]{2,1,0:T(8,128)S(1)} %pad_maximum_fusion.near_ref, f32[2,200,128]{2,1,0:T(8,128)S(1)} %collective-permute-done.2.far_ref, ...), custom_call_target="tpu_custom_call" | custom-call | flops 1000000000 | bytes 4194304 | tf_op jit(solution)/shard_map/pallas_call | solution.py:239
  14.4 1.3 %collective-permute-start.3 = (f32[48,128]{1,0:T(8,128)S(1)}, f32[48,128]{1,0:T(8,128)S(1)}, u32[]{:S(2)}, u32[]{:S(2)}) collective-permute-start(f32[48,128]{1,0:T(8,128)S(1)} %get-tuple-element.26), channel_id=1, source_target_pairs={{0,3},{1,2},{2,1},{3,0},{4,7},{5,6},{6,5},{7,4},{8,11},{9,10},{10,... | collective-permute-start | bytes 73736 | tf_op jit(solution)/shard_map/ppermute | solution.py:252
  15.7 0.4 %collective-permute-start.4 = (f32[48,128]{1,0:T(8,128)S(1)}, f32[48,128]{1,0:T(8,128)S(1)}, u32[]{:S(2)}, u32[]{:S(2)}) collective-permute-start(f32[48,128]{1,0:T(8,128)S(1)} %get-tuple-element.27), channel_id=1, source_target_pairs={{0,1},{1,0},{2,3},{3,2},{4,5},{5,4},{6,7},{7,6},{8,9},{9,8},{10,11... | collective-permute-start | bytes 73736 | tf_op jit(solution)/shard_map/ppermute | solution.py:251
  16.1 0.2 collective-permute-start.7
  16.3 1.4 %collective-permute-done.3.edge2_ref = f32[48,128]{1,0:T(8,128)S(1)} collective-permute-done((f32[48,128]{1,0:T(8,128)S(1)}, f32[48,128]{1,0:T(8,128)S(1)}, u32[]{:S(2)}, u32[]{:S(2)}) %collective-permute-start.3) | collective-permute-done | bytes 24608 | tf_op jit(solution)/shard_map/ppermute | solution.py:252
  17.7 0.0 collective-permute-done.4.edge1_ref
  17.8 0.9 %collective-permute-start.6 = (f32[32,128]{1,0:T(8,128)S(1)}, f32[32,128]{1,0:T(8,128)S(1)}, u32[]{:S(2)}, u32[]{:S(2)}) collective-permute-start(f32[32,128]{1,0:T(8,128)S(1)} %pad_maximum_fusion.3), channel_id=1, source_target_pairs={{0,4},{4,8},{8,12},{12,16},{16,20},{20,24},{24,28},{28,0},{1,5},{5... | collective-permute-start | bytes 49160 | tf_op jit(solution)/shard_map/ppermute | solution.py:256
  18.6 3.9 %collective-permute-start.5 = (f32[184,128]{1,0:T(8,128)S(1)}, f32[184,128]{1,0:T(8,128)S(1)}, u32[]{:S(2)}, u32[]{:S(2)}) collective-permute-start(f32[184,128]{1,0:T(8,128)S(1)} %pad_maximum_fusion.1), channel_id=1, source_target_pairs={{4,0},{8,4},{12,8},{16,12},{20,16},{24,20},{28,24},{0,28},{5,1},{9... | collective-permute-start | bytes 282632 | tf_op jit(solution)/shard_map/ppermute | solution.py:257
  22.5 0.6 %pad_maximum_fusion.2 = f32[10,16,128]{2,1,0:T(8,128)} fusion(f32[7,16,128]{2,1,0:T(8,128)S(1)} %slice.13, f32[3,16,128]{2,1,0:T(8,128)S(1)} %broadcast_multiply_fusion), kind=kLoop, calls=%fused_computation.2 | loop fusion | flops 20480 | bytes 163840 | tf_op jit(solution)/shard_map/concatenate | solution.py:249
  23.2 1.2 %collective-permute-done.6.corner_ref = f32[32,128]{1,0:T(8,128)S(1)} collective-permute-done((f32[32,128]{1,0:T(8,128)S(1)}, f32[32,128]{1,0:T(8,128)S(1)}, u32[]{:S(2)}, u32[]{:S(2)}) %collective-permute-start.6) | collective-permute-done | bytes 16416 | tf_op jit(solution)/shard_map/ppermute | solution.py:256
  24.4 0.0 collective-permute-done.7.top_ref
  24.4 0.6 %collective-permute-done.5.low_ref = f32[184,128]{1,0:T(8,128)S(1)} collective-permute-done((f32[184,128]{1,0:T(8,128)S(1)}, f32[184,128]{1,0:T(8,128)S(1)}, u32[]{:S(2)}, u32[]{:S(2)}) %collective-permute-start.5) | collective-permute-done | bytes 94240 | tf_op jit(solution)/shard_map/ppermute | solution.py:257
  24.9 1.6 %shard_map.71 = f32[3,16,128]{2,1,0:T(8,128)} custom-call(f32[32,16,128]{2,1,0:T(8,128)S(1)} %get-tuple-element.25.force_ref, f32[3,16,128]{2,1,0:T(8,128)S(1)} %copy-done.1, s32[16,128]{1,0:T(8,128)S(1)} %copy-done.2, f32[48,128]{1,0:T(8,128)S(1)} %collective-permute-done.4.edge1_ref, f32[48,128]{1,0:T(8,128)S(1)} %collective-permute-done.3.edge2_ref, ...), custom_call_target="tpu_custom_call" | custom-call | tf_op jit(solution)/shard_map/pallas_call | solution.py:259
  (9 shorter events, 0.1 us)
Async XLA Ops:
  0.6 7.6 %copy-start.3 = (s32[16,4]{0,1:T(4,128)S(1)}, s32[16,4]{0,1:T(4,128)}, u32[]{:S(2)}) copy-start(s32[16,4]{0,1:T(4,128)} %param.7) | copy-start | bytes 772
  0.6 7.6 %copy-start = (f32[16,4,128,128]{3,2,1,0:T(8,128)S(1)}, f32[16,4,128,128]{3,2,1,0:T(8,128)}, u32[]{:S(2)}) copy-start(f32[16,4,128,128]{3,2,1,0:T(8,128)} %weight_ref.1) | copy-start | bytes 12582916
  0.6 1.4 %copy-start.4 = (f32[10,12,16,128]{3,2,1,0:T(8,128)S(1)}, f32[10,12,16,128]{3,2,1,0:T(8,128)}, u32[]{:S(2)}) copy-start(f32[10,12,16,128]{3,2,1,0:T(8,128)} %atmo_ref.1) | copy-start | bytes 2949124
  2.1 11.4 %copy-start.1 = (f32[3,16,128]{2,1,0:T(8,128)S(1)}, f32[3,16,128]{2,1,0:T(8,128)}, u32[]{:S(2)}) copy-start(f32[3,16,128]{2,1,0:T(8,128)} %state_ref.3) | copy-start | bytes 73732
  2.1 11.4 %copy-start.2 = (s32[16,128]{1,0:T(8,128)S(1)}, s32[16,128]{1,0:T(8,128)}, u32[]{:S(2)}) copy-start(s32[16,128]{1,0:T(8,128)} %mask_ref.3) | copy-start | bytes 24580
  2.1 9.0 %collective-permute-start.1 = (f32[200,128]{1,0:T(8,128)S(1)}, f32[200,128]{1,0:T(8,128)S(1)}, u32[]{:S(2)}, u32[]{:S(2)}) collective-permute-start(f32[200,128]{1,0:T(8,128)S(1)} %get-tuple-element.17), channel_id=1, source_target_pairs={{0,4},{4,8},{8,12},{12,16},{16,20},{20,24},{24,28},{28,0},{1,5},{5... | collective-permute-start | bytes 307208 | tf_op jit(solution)/shard_map/ppermute | solution.py:222
  5.1 6.9 %collective-permute-start = (f32[200,128]{1,0:T(8,128)S(1)}, f32[200,128]{1,0:T(8,128)S(1)}, u32[]{:S(2)}, u32[]{:S(2)}) collective-permute-start(f32[200,128]{1,0:T(8,128)S(1)} %get-tuple-element.17), channel_id=1, source_target_pairs={{4,0},{8,4},{12,8},{16,12},{20,16},{24,20},{28,24},{0,28},{5,1},{9... | collective-permute-start | bytes 307208 | tf_op jit(solution)/shard_map/ppermute | solution.py:223
  12.0 1.5 %collective-permute-start.2 = (f32[2,200,128]{2,1,0:T(8,128)S(1)}, f32[2,200,128]{2,1,0:T(8,128)S(1)}, u32[]{:S(2)}, u32[]{:S(2)}) collective-permute-start(f32[2,200,128]{2,1,0:T(8,128)S(1)} %pad_maximum_fusion.near_ref), channel_id=1, source_target_pairs={{0,1},{1,0},{2,3},{3,2},{4,5},{5,4},{6,7},{7,6},{8,9},{9,8},{10,11... | collective-permute-start | bytes 614408 | tf_op jit(solution)/shard_map/ppermute | solution.py:237
  14.4 3.3 %collective-permute-start.3 = (f32[48,128]{1,0:T(8,128)S(1)}, f32[48,128]{1,0:T(8,128)S(1)}, u32[]{:S(2)}, u32[]{:S(2)}) collective-permute-start(f32[48,128]{1,0:T(8,128)S(1)} %get-tuple-element.26), channel_id=1, source_target_pairs={{0,3},{1,2},{2,1},{3,0},{4,7},{5,6},{6,5},{7,4},{8,11},{9,10},{10,... | collective-permute-start | bytes 73736 | tf_op jit(solution)/shard_map/ppermute | solution.py:252
  15.7 2.0 %collective-permute-start.4 = (f32[48,128]{1,0:T(8,128)S(1)}, f32[48,128]{1,0:T(8,128)S(1)}, u32[]{:S(2)}, u32[]{:S(2)}) collective-permute-start(f32[48,128]{1,0:T(8,128)S(1)} %get-tuple-element.27), channel_id=1, source_target_pairs={{0,1},{1,0},{2,3},{3,2},{4,5},{5,4},{6,7},{7,6},{8,9},{9,8},{10,11... | collective-permute-start | bytes 73736 | tf_op jit(solution)/shard_map/ppermute | solution.py:251
  16.1 8.3 %collective-permute-start.7 = (f32[152,128]{1,0:T(8,128)S(1)}, f32[152,128]{1,0:T(8,128)S(1)}, u32[]{:S(2)}, u32[]{:S(2)}) collective-permute-start(f32[152,128]{1,0:T(8,128)S(1)} %get-tuple-element.31), channel_id=1, source_target_pairs={{0,4},{4,8},{8,12},{12,16},{16,20},{20,24},{24,28},{28,0},{1,5},{5... | collective-permute-start | bytes 233480 | tf_op jit(solution)/shard_map/ppermute | solution.py:255
  17.8 6.6 %collective-permute-start.6 = (f32[32,128]{1,0:T(8,128)S(1)}, f32[32,128]{1,0:T(8,128)S(1)}, u32[]{:S(2)}, u32[]{:S(2)}) collective-permute-start(f32[32,128]{1,0:T(8,128)S(1)} %pad_maximum_fusion.3), channel_id=1, source_target_pairs={{0,4},{4,8},{8,12},{12,16},{16,20},{20,24},{24,28},{28,0},{1,5},{5... | collective-permute-start | bytes 49160 | tf_op jit(solution)/shard_map/ppermute | solution.py:256
  18.6 6.3 %collective-permute-start.5 = (f32[184,128]{1,0:T(8,128)S(1)}, f32[184,128]{1,0:T(8,128)S(1)}, u32[]{:S(2)}, u32[]{:S(2)}) collective-permute-start(f32[184,128]{1,0:T(8,128)S(1)} %pad_maximum_fusion.1), channel_id=1, source_target_pairs={{4,0},{8,4},{12,8},{16,12},{20,16},{24,20},{28,24},{0,28},{5,1},{9... | collective-permute-start | bytes 282632 | tf_op jit(solution)/shard_map/ppermute | solution.py:257

commit v4 on v3

--- a/solution.py
+++ b/solution.py
@@ -83,8 +83,7 @@
     return jnp.concatenate([high, low], axis=1)
 
 
-def remap_row(split_ref, first, second, weights):
-    left = jnp.concatenate([split_ref[first], split_ref[second]], axis=1)
+def remap_row(left, weights):
     both = jnp.dot(left, weights, preferred_element_type=jnp.float32)
     wide = weights.shape[1] // 2
     return both[0:32, :wide] + both[32:64, :wide] + both[0:32, wide:]
@@ -96,22 +95,27 @@
     for x in range(weight_ref.shape[0]):
         first, second = index[1, x], index[2, x]
         weights = split_weights(weight_ref[x, 1], weight_ref[x, 2])
-        acc_ref[:, x, :] = remap_row(split_ref, first, second, weights)
+        acc_ref[:, x, :] = remap_row(jnp.concatenate([split_ref[first], split_ref[second]], axis=1), weights)
         rest_ref[x] = split_weights(weight_ref[x, 0], weight_ref[x, 3])
 
 
-def rim_kernel(rows, tiles_ref, near_ref, far_ref, rest_ref, own_ref, state_ref, mask_ref,
+def add_slot(rows, slot, offset, tiles_ref, near_ref, far_ref, rest_ref, add_ref, total_ref, split_ref):
+    part = split_ref.shape[0] // 2
+    split_tiles(near_ref, split_ref, 0, rows)
+    split_tiles(far_ref, split_ref, part, rows)
+    col_odd = lax.axis_index("col") % 2
+    name = tiles_ref[...] - offset * 2 * part
+    index = name % part + part * ((name // part + col_odd) % 2)
+    cells = split_ref.shape[2]
+    at = (slot > 0) * cells
+    for x in range(rest_ref.shape[0]):
+        total_ref[:, x, :] = remap_row(split_ref[index[slot, x]], rest_ref[x, at : at + cells, :]) + add_ref[:, x, :]
+
+
+def rim_kernel(rows, tiles_ref, near_ref, far_ref, rest_ref, add_ref, state_ref, mask_ref,
                total_ref, down_ref, up_ref, edge1_ref, edge2_ref, split_ref):
-    part = split_ref.shape[0] // 4
-    for side in range(2):
-        split_tiles(near_ref.at[side], split_ref, 2 * side * part, rows)
-        split_tiles(far_ref.at[side], split_ref, (2 * side + 1) * part, rows)
+    add_slot(rows, 3, 2, tiles_ref, near_ref, far_ref, rest_ref, add_ref, total_ref, split_ref)
     col_odd = lax.axis_index("col") % 2
-    names = tiles_ref[...]
-    place = lambda name: name % part + part * ((name // part + col_odd) % 2)
-    before, after = place(names), place(names - 4 * part) + 2 * part
-    for x in range(rest_ref.shape[0]):
-        total_ref[:, x, :] = remap_row(split_ref, before[0, x], after[3, x], rest_ref[x]) + own_ref[:, x, :]
 
     items = [total_ref[p] for p in range(PLANES)] + [state_ref[k] for k in range(DYN)] + [mask_ref[...].astype(jnp.float32)]
     high, wide = mask_ref.shape
@@ -139,7 +143,7 @@
         edge2_ref[g * high : (g + 1) * high, :] = jnp.where(col_even, head, last)
 
 
-def ocean_kernel(force_ref, state_ref, mask_ref, edge1_ref, edge2_ref, low_ref, corner_ref, top_ref, out_ref):
+def ocean_kernel(force_ref, state_ref, mask_ref, edge1_ref, edge2_ref, low_ref, corner_ref, top_ref, out_ref, *shift_refs):
     high, wide = mask_ref.shape
     col_even = lax.axis_index("col") % 2 == 0
     second = high + MAIN
@@ -168,30 +172,55 @@
             edge(beside[0 if i < PLANES else 1], w, LANE_AT[i]),
             edge(below, CORNERS[i], CORNER_AT[i])[:rim],
         ]
-        return jnp.concatenate([jnp.concatenate(main, axis=0), jnp.concatenate(rest, axis=0)], axis=1)
-
-    before = lambda v, axis: pltpu.roll(v, 1, axis)
-    after = lambda v, axis: pltpu.roll(v, v.shape[axis] - 1, axis)
+        return [jnp.concatenate(main, axis=0), jnp.concatenate(rest, axis=0)]
+
+    each = lambda f, *fields: [f(*parts) for parts in zip(*fields)]
+
+    def slope_x(field, refs):
+        out = []
+        for ref, value in zip(refs, field):
+            rows = value.shape[0]
+            ref[8 : 8 + rows, :] = value
+            out.append((ref[9 : 9 + rows, :] - ref[7 : 7 + rows, :]) * 0.5)
+        return out
+
+    def along(field, step):
+        place = lax.broadcasted_iota(jnp.int32, field[0].shape, 1)
+        crosses = place >= wide - step if step > 0 else place < -step
+        moved = [pltpu.roll(v, -step % wide, 1) for v in field]
+        return [jnp.where(crosses, moved[1], moved[0]), jnp.where(crosses, moved[0], moved[1])]
+
+    def slope_y(field):
+        return each(lambda a, b: (a - b) * 0.5, along(field, 1), along(field, -1))
+
+    def slope_yy(field):
+        return each(lambda a, v, b: ((a - v) - (v - b)) * 0.25, along(field, 2), field, along(field, -2))
+
     rim = high
     height = extended(PLANES, state_ref[0], rim)
     zonal = extended(PLANES + 1, state_ref[1], rim)
     merid = extended(PLANES + 2, state_ref[2], rim)
     ocean = extended(PLANES + 3, mask_ref[...].astype(jnp.float32), rim)
+    grad_y = slope_y(height)
     for s in range(SUB):
         reach = -(-2 * (SUB - s) // 8) * 8
         if reach < rim:
             cut = rim - reach
-            height, zonal, merid, ocean = (v[cut : v.shape[0] - cut] for v in (height, zonal, merid, ocean))
+            height, zonal, merid, ocean, grad_y = (
+                each(lambda v: v[cut : v.shape[0] - cut], field) for field in (height, zonal, merid, ocean, grad_y)
+            )
             rim = reach
         push_u, push_v, push_h = (extended(s * DYN + f, force_ref[s * DYN + f], rim) for f in range(DYN))
-        grad_x = (after(height, 0) - before(height, 0)) * 0.5
-        grad_y = (after(height, 1) - before(height, 1)) * 0.5
-        zonal = ocean * (zonal - grad_x + 0.2 * merid + 0.5 * push_u)
-        merid = ocean * (merid - grad_y - 0.2 * zonal + 0.5 * push_v)
-        spread = (after(zonal, 0) - before(zonal, 0)) * 0.5 + (after(merid, 1) - before(merid, 1)) * 0.5
-        height = height - spread + 0.5 * push_h
+        grad_x = slope_x(height, shift_refs[:2])
+        zonal = each(lambda m, u, g, v, p: m * (u - g + 0.2 * v + 0.5 * p), ocean, zonal, grad_x, merid, push_u)
+        merid = each(lambda m, v, g, u, p: m * (v - g - 0.2 * u + 0.5 * p), ocean, merid, grad_y, zonal, push_v)
+        spread = each(jnp.add, slope_x(zonal, shift_refs[2:]), slope_y(merid))
+        height = each(lambda h, d, p: h - d + 0.5 * p, height, spread, push_h)
+        if s < SUB - 1:
+            bend = each(jnp.add, slope_x(slope_y(zonal), shift_refs[4:]), slope_yy(merid))
+            grad_y = each(lambda g, d, p: g - d + 0.5 * p, grad_y, bend, slope_y(push_h))
     for k, value in enumerate((height, zonal, merid)):
-        out_ref[k] = value[rim : rim + high, :wide]
+        out_ref[k] = value[0][rim : rim + high]
 
 
 def per_device(size_row, size_col, atmo_states, remap_weights, intersection_tiles, land_mask, ocean_state):
@@ -232,19 +261,28 @@
         cost_estimate=pl.CostEstimate(flops=10**9, bytes_accessed=4 << 20, transcendentals=0),
     )(names, own, remap_weights)
 
-    following, previous, acc, rest = lax.optimization_barrier((following, previous, acc, rest))
-    near = jnp.stack([previous, following])
-    far = lax.ppermute(near, "col", col_near)
+    previous, acc, rest = lax.optimization_barrier((previous, acc, rest))
+    previous_far = lax.ppermute(previous, "col", col_near)
+    following_far = lax.ppermute(following, "col", col_near)
+    acc = pl.pallas_call(
+        functools.partial(add_slot, rows, 0, 0),
+        out_shape=f32(32, high, wide),
+        in_specs=[vmem] * 5,
+        out_specs=vmem,
+        scratch_shapes=[pltpu.VMEM((tiles, 64, cells), jnp.bfloat16)],
+        compiler_params=params(),
+        cost_estimate=pl.CostEstimate(flops=10**9, bytes_accessed=2 << 20, transcendentals=0),
+    )(names, previous, previous_far, rest, acc)
 
     total, down, up, edge1, edge2 = pl.pallas_call(
         functools.partial(rim_kernel, rows),
         out_shape=(f32(32, high, wide), f32(MAIN, wide), f32(MAIN, wide), f32(GROUPS * high, wide), f32(GROUPS * high, wide)),
         in_specs=[vmem] * 7,
         out_specs=(vmem,) * 5,
-        scratch_shapes=[pltpu.VMEM((2 * tiles, 64, cells), jnp.bfloat16)],
+        scratch_shapes=[pltpu.VMEM((tiles, 64, cells), jnp.bfloat16)],
         compiler_params=params(),
         cost_estimate=pl.CostEstimate(flops=10**9, bytes_accessed=4 << 20, transcendentals=0),
-    )(names, near, far, rest, acc, ocean_state, land_mask)
+    )(names, following, following_far, rest, acc, ocean_state, land_mask)
     forced = total[:PLANES].reshape(SUB, DYN, high, wide)
     flux_mean = jnp.concatenate([jnp.mean(forced, axis=0), total[PLANES:rows]], axis=0)
 
@@ -261,6 +299,7 @@
         out_shape=f32(3, high, wide),
         in_specs=[vmem] * 8,
         out_specs=vmem,
+        scratch_shapes=[pltpu.VMEM((3 * high + 16, wide), jnp.float32)] * 6,
         compiler_params=params(),
     )(total, ocean_state, land_mask, from1, from2, low, corner, top)
     return flux_mean, final

time: 26.7 us -> 26.4 us (0.989)
  waiting for transfers between devices: 7.51 us -> 6.87 us
  Pallas kernels: 3.39 us -> 3.79 us
    ppermute x1 -> x2, waiting for transfers between devices: 1.44 us -> 0.78 us  [the longest x1 0.48 us: per_device(): previous_far = lax.ppermute(previous, 'col', col_near)]
    pallas_call x0 -> x1, Pallas kernels: none -> 0.52 us  [per_device(): pl.pallas_call(functools.partial(add_slot, rows, 0, 0), out_shape=f32(32,...]
  transfers between devices with their start and end apart: 8 -> 9, of which waited for: 6 -> 7; matrix products, arithmetic and copies ran while one was open for 3% -> 3% of each run, Pallas kernels for 3% -> 5%
where the time goes in v4:
time: 26.4 us; the launch traced here: 26.2 us
  starting transfers between devices  12.8 us (48%)
  waiting for transfers between devices  6.87 us (26%)
  Pallas kernels  3.79 us (14%)
  local copies, waits for them, and re-layouts  1.38 us (5%)
  between operations  0.74 us (3%)
  other arithmetic  0.67 us (3%)
    ppermute x1, starting transfers between devices, per_device(): lax.ppermute(jnp.concatenate([corners[0], up, corners[1]]), 'row', back)  3.92 us
    ppermute x1, starting transfers between devices, per_device(): following = lax.ppermute(part, 'row', back)  3.1 us
    ppermute x1, starting transfers between devices, per_device(): previous = lax.ppermute(part, 'row', onward)  3.02 us
    ppermute x1, waiting for transfers between devices, per_device(): previous = lax.ppermute(part, 'row', onward)  2.09 us
    pallas_call x1, Pallas kernels, per_device(): pl.pallas_call(ocean_kernel, out_shape=f32(3, high, wide), in_specs=[vmem...  1.6 us
    ppermute x1, waiting for transfers between devices, per_device(): from2 = lax.ppermute(edge2, 'col', col_far)  1.4 us
    unnamed x10, local copies, waits for them, and re-layouts  1.36 us
    ppermute x1, starting transfers between devices, per_device(): from2 = lax.ppermute(edge2, 'col', col_far)  1.31 us
  transfers between devices with their start and end apart: 9, of which 7 were waited for; matrix products, arithmetic and copies ran while one was open for 3% of the time, Pallas kernels for 5%

profile of v4, /device:TPU:0, one launch (start us, length us, event | category | flops | bytes accessed | tf_op | source)
XLA Modules:
  0.0 26.2 jit_solution(3750311828274666251)
XLA Ops:
  0.6 0.0 copy-start.3
  0.6 0.0 copy-start
  0.6 0.0 copy-start.4
  0.7 1.3 %copy-done.4 = f32[10,12,16,128]{3,2,1,0:T(8,128)S(1)} copy-done((f32[10,12,16,128]{3,2,1,0:T(8,128)S(1)}, f32[10,12,16,128]{3,2,1,0:T(8,128)}, u32[]{:S(2)}) %copy-start.4) | copy-done | bytes 983064
  2.0 0.1 shard_map.68
  2.1 0.0 copy-start.1
  2.1 0.0 copy-start.2
  2.1 3.0 %collective-permute-start.2 = (f32[200,128]{1,0:T(8,128)S(1)}, f32[200,128]{1,0:T(8,128)S(1)}, u32[]{:S(2)}, u32[]{:S(2)}) collective-permute-start(f32[200,128]{1,0:T(8,128)S(1)} %get-tuple-element.16), channel_id=1, source_target_pairs={{0,4},{4,8},{8,12},{12,16},{16,20},{20,24},{24,28},{28,0},{1,5},{5... | collective-permute-start | bytes 307208 | tf_op jit(solution)/shard_map/ppermute | solution.py:251
  5.1 3.1 %collective-permute-start = (f32[200,128]{1,0:T(8,128)S(1)}, f32[200,128]{1,0:T(8,128)S(1)}, u32[]{:S(2)}, u32[]{:S(2)}) collective-permute-start(f32[200,128]{1,0:T(8,128)S(1)} %get-tuple-element.16), channel_id=1, source_target_pairs={{4,0},{8,4},{12,8},{16,12},{20,16},{24,20},{28,24},{0,28},{5,1},{9... | collective-permute-start | bytes 307208 | tf_op jit(solution)/shard_map/ppermute | solution.py:252
  8.2 0.0 copy-done
  8.3 0.8 %shard_map.69 = (f32[32,16,128]{2,1,0:T(8,128)S(1)}, bf16[16,256,256]{2,1,0:T(8,128)(2,1)S(1)}) custom-call(s32[4,16]{1,0:T(4,128)S(1)} %bitcast.2, f32[400,128]{1,0:T(8,128)S(1)} %get-tuple-element.17.own_ref, f32[16,4,128,128]{3,2,1,0:T(8,128)S(1)} %copy-done), custom_call_target="tpu_custom_call" | custom-call | flops 1000000000 | bytes 4194304 | tf_op jit(solution)/shard_map/pallas_call | solution.py:254
  9.1 2.1 %collective-permute-done.2.near_ref = f32[200,128]{1,0:T(8,128)S(1)} collective-permute-done((f32[200,128]{1,0:T(8,128)S(1)}, f32[200,128]{1,0:T(8,128)S(1)}, u32[]{:S(2)}, u32[]{:S(2)}) %collective-permute-start.2) | collective-permute-done | bytes 102432 | tf_op jit(solution)/shard_map/ppermute | solution.py:251
  11.2 0.0 collective-permute-start.3
  11.2 0.8 %collective-permute-done.near_ref = f32[200,128]{1,0:T(8,128)S(1)} collective-permute-done((f32[200,128]{1,0:T(8,128)S(1)}, f32[200,128]{1,0:T(8,128)S(1)}, u32[]{:S(2)}, u32[]{:S(2)}) %collective-permute-start) | collective-permute-done | bytes 102432 | tf_op jit(solution)/shard_map/ppermute | solution.py:252
  12.0 0.0 collective-permute-start.1
  12.0 0.5 %collective-permute-done.3.far_ref = f32[200,128]{1,0:T(8,128)S(1)} collective-permute-done((f32[200,128]{1,0:T(8,128)S(1)}, f32[200,128]{1,0:T(8,128)S(1)}, u32[]{:S(2)}, u32[]{:S(2)}) %collective-permute-start.3) | collective-permute-done | bytes 102432 | tf_op jit(solution)/shard_map/ppermute | solution.py:265
  12.5 0.5 %shard_map.70.add_ref = f32[32,16,128]{2,1,0:T(8,128)S(1)} custom-call(s32[4,16]{1,0:T(4,128)S(1)} %bitcast.3, f32[200,128]{1,0:T(8,128)S(1)} %collective-permute-done.2.near_ref, f32[200,128]{1,0:T(8,128)S(1)} %collective-permute-done.3.far_ref, bf16[16,256,256]{2,1,0:T(8,128)(2,1)S(1)} %get-tuple-element.20.rest_ref, ...), custom_call_target="tpu_custom_call" | custom-call | flops 1000000000 | bytes 2097152 | tf_op jit(solution)/shard_map/pallas_call | solution.py:267
  13.0 0.3 %collective-permute-done.1.far_ref = f32[200,128]{1,0:T(8,128)S(1)} collective-permute-done((f32[200,128]{1,0:T(8,128)S(1)}, f32[200,128]{1,0:T(8,128)S(1)}, u32[]{:S(2)}, u32[]{:S(2)}) %collective-permute-start.1) | collective-permute-done | bytes 102432 | tf_op jit(solution)/shard_map/ppermute | solution.py:266
  13.3 0.0 copy-done.1
  13.3 0.7 %shard_map.71 = (f32[32,16,128]{2,1,0:T(8,128)S(1)}, f32[152,128]{1,0:T(8,128)S(1)}, f32[152,128]{1,0:T(8,128)S(1)}, f32[48,128]{1,0:T(8,128)S(1)}, f32[48,128]{1,0:T(8,128)S(1)}) custom-call(s32[4,16]{1,0:T(4,128)S(1)} %bitcast.4, f32[200,128]{1,0:T(8,128)S(1)} %collective-permute-done.near_ref, f32[200,128]{1,0:T(8,128)S(1)} %collective-permute-done.1.far_ref, ...), custom_call_target="tpu_custom_call" | custom-call | flops 1000000000 | bytes 4194304 | tf_op jit(solution)/shard_map/pallas_call | solution.py:277
  14.1 1.3 %collective-permute-start.4 = (f32[48,128]{1,0:T(8,128)S(1)}, f32[48,128]{1,0:T(8,128)S(1)}, u32[]{:S(2)}, u32[]{:S(2)}) collective-permute-start(f32[48,128]{1,0:T(8,128)S(1)} %get-tuple-element.24), channel_id=1, source_target_pairs={{0,3},{1,2},{2,1},{3,0},{4,7},{5,6},{6,5},{7,4},{8,11},{9,10},{10,... | collective-permute-start | bytes 73736 | tf_op jit(solution)/shard_map/ppermute | solution.py:290
  15.4 0.4 %collective-permute-start.5 = (f32[48,128]{1,0:T(8,128)S(1)}, f32[48,128]{1,0:T(8,128)S(1)}, u32[]{:S(2)}, u32[]{:S(2)}) collective-permute-start(f32[48,128]{1,0:T(8,128)S(1)} %get-tuple-element.25), channel_id=1, source_target_pairs={{0,1},{1,0},{2,3},{3,2},{4,5},{5,4},{6,7},{7,6},{8,9},{9,8},{10,11... | collective-permute-start | bytes 73736 | tf_op jit(solution)/shard_map/ppermute | solution.py:289
  15.8 0.2 collective-permute-start.8
  16.0 1.4 %collective-permute-done.4.edge2_ref = f32[48,128]{1,0:T(8,128)S(1)} collective-permute-done((f32[48,128]{1,0:T(8,128)S(1)}, f32[48,128]{1,0:T(8,128)S(1)}, u32[]{:S(2)}, u32[]{:S(2)}) %collective-permute-start.4) | collective-permute-done | bytes 24608 | tf_op jit(solution)/shard_map/ppermute | solution.py:290
  17.4 0.0 collective-permute-done.5.edge1_ref
  17.5 0.9 %collective-permute-start.7 = (f32[32,128]{1,0:T(8,128)S(1)}, f32[32,128]{1,0:T(8,128)S(1)}, u32[]{:S(2)}, u32[]{:S(2)}) collective-permute-start(f32[32,128]{1,0:T(8,128)S(1)} %pad_maximum_fusion.2), channel_id=1, source_target_pairs={{0,4},{4,8},{8,12},{12,16},{16,20},{20,24},{24,28},{28,0},{1,5},{5... | collective-permute-start | bytes 49160 | tf_op jit(solution)/shard_map/ppermute | solution.py:294
  18.3 3.9 %collective-permute-start.6 = (f32[184,128]{1,0:T(8,128)S(1)}, f32[184,128]{1,0:T(8,128)S(1)}, u32[]{:S(2)}, u32[]{:S(2)}) collective-permute-start(f32[184,128]{1,0:T(8,128)S(1)} %pad_maximum_fusion), channel_id=1, source_target_pairs={{4,0},{8,4},{12,8},{16,12},{20,16},{24,20},{28,24},{0,28},{5,1},{9... | collective-permute-start | bytes 282632 | tf_op jit(solution)/shard_map/ppermute | solution.py:295
  22.2 0.6 %pad_maximum_fusion.1 = f32[10,16,128]{2,1,0:T(8,128)} fusion(f32[7,16,128]{2,1,0:T(8,128)S(1)} %slice.13, f32[3,16,128]{2,1,0:T(8,128)S(1)} %broadcast_multiply_fusion), kind=kLoop, calls=%fused_computation.1 | loop fusion | flops 20480 | bytes 163840 | tf_op jit(solution)/shard_map/concatenate | solution.py:287
  22.9 1.2 %collective-permute-done.7.corner_ref = f32[32,128]{1,0:T(8,128)S(1)} collective-permute-done((f32[32,128]{1,0:T(8,128)S(1)}, f32[32,128]{1,0:T(8,128)S(1)}, u32[]{:S(2)}, u32[]{:S(2)}) %collective-permute-start.7) | collective-permute-done | bytes 16416 | tf_op jit(solution)/shard_map/ppermute | solution.py:294
  24.0 0.0 collective-permute-done.8.top_ref
  24.0 0.6 %collective-permute-done.6.low_ref = f32[184,128]{1,0:T(8,128)S(1)} collective-permute-done((f32[184,128]{1,0:T(8,128)S(1)}, f32[184,128]{1,0:T(8,128)S(1)}, u32[]{:S(2)}, u32[]{:S(2)}) %collective-permute-start.6) | collective-permute-done | bytes 94240 | tf_op jit(solution)/shard_map/ppermute | solution.py:295
  24.6 1.6 %shard_map.72 = f32[3,16,128]{2,1,0:T(8,128)} custom-call(f32[32,16,128]{2,1,0:T(8,128)S(1)} %get-tuple-element.23.force_ref, f32[3,16,128]{2,1,0:T(8,128)S(1)} %copy-done.1, s32[16,128]{1,0:T(8,128)S(1)} %copy-done.2, f32[48,128]{1,0:T(8,128)S(1)} %collective-permute-done.5.edge1_ref, f32[48,128]{1,0:T(8,128)S(1)} %collective-permute-done.4.edge2_ref, ...), custom_call_target="tpu_custom_call" | custom-call | tf_op jit(solution)/shard_map/pallas_call | solution.py:297
  (10 shorter events, 0.1 us)
Async XLA Ops:
  0.6 7.6 %copy-start.3 = (s32[16,4]{0,1:T(4,128)S(1)}, s32[16,4]{0,1:T(4,128)}, u32[]{:S(2)}) copy-start(s32[16,4]{0,1:T(4,128)} %param.7) | copy-start | bytes 772
  0.6 7.6 %copy-start = (f32[16,4,128,128]{3,2,1,0:T(8,128)S(1)}, f32[16,4,128,128]{3,2,1,0:T(8,128)}, u32[]{:S(2)}) copy-start(f32[16,4,128,128]{3,2,1,0:T(8,128)} %weight_ref.1) | copy-start | bytes 12582916
  0.6 1.4 %copy-start.4 = (f32[10,12,16,128]{3,2,1,0:T(8,128)S(1)}, f32[10,12,16,128]{3,2,1,0:T(8,128)}, u32[]{:S(2)}) copy-start(f32[10,12,16,128]{3,2,1,0:T(8,128)} %atmo_ref.1) | copy-start | bytes 2949124
  2.1 11.2 %copy-start.1 = (f32[3,16,128]{2,1,0:T(8,128)S(1)}, f32[3,16,128]{2,1,0:T(8,128)}, u32[]{:S(2)}) copy-start(f32[3,16,128]{2,1,0:T(8,128)} %state_ref.3) | copy-start | bytes 73732
  2.1 11.2 %copy-start.2 = (s32[16,128]{1,0:T(8,128)S(1)}, s32[16,128]{1,0:T(8,128)}, u32[]{:S(2)}) copy-start(s32[16,128]{1,0:T(8,128)} %mask_ref.3) | copy-start | bytes 24580
  2.1 9.0 %collective-permute-start.2 = (f32[200,128]{1,0:T(8,128)S(1)}, f32[200,128]{1,0:T(8,128)S(1)}, u32[]{:S(2)}, u32[]{:S(2)}) collective-permute-start(f32[200,128]{1,0:T(8,128)S(1)} %get-tuple-element.16), channel_id=1, source_target_pairs={{0,4},{4,8},{8,12},{12,16},{16,20},{20,24},{24,28},{28,0},{1,5},{5... | collective-permute-start | bytes 307208 | tf_op jit(solution)/shard_map/ppermute | solution.py:251
  5.1 6.9 %collective-permute-start = (f32[200,128]{1,0:T(8,128)S(1)}, f32[200,128]{1,0:T(8,128)S(1)}, u32[]{:S(2)}, u32[]{:S(2)}) collective-permute-start(f32[200,128]{1,0:T(8,128)S(1)} %get-tuple-element.16), channel_id=1, source_target_pairs={{4,0},{8,4},{12,8},{16,12},{20,16},{24,20},{28,24},{0,28},{5,1},{9... | collective-permute-start | bytes 307208 | tf_op jit(solution)/shard_map/ppermute | solution.py:252
  11.2 1.3 %collective-permute-start.3 = (f32[200,128]{1,0:T(8,128)S(1)}, f32[200,128]{1,0:T(8,128)S(1)}, u32[]{:S(2)}, u32[]{:S(2)}) collective-permute-start(f32[200,128]{1,0:T(8,128)S(1)} %collective-permute-done.2.near_ref), channel_id=1, source_target_pairs={{0,1},{1,0},{2,3},{3,2},{4,5},{5,4},{6,7},{7,6},{8,9},{9,8},{10,11... | collective-permute-start | bytes 307208 | tf_op jit(solution)/shard_map/ppermute | solution.py:265
  12.0 1.3 %collective-permute-start.1 = (f32[200,128]{1,0:T(8,128)S(1)}, f32[200,128]{1,0:T(8,128)S(1)}, u32[]{:S(2)}, u32[]{:S(2)}) collective-permute-start(f32[200,128]{1,0:T(8,128)S(1)} %collective-permute-done.near_ref), channel_id=1, source_target_pairs={{0,1},{1,0},{2,3},{3,2},{4,5},{5,4},{6,7},{7,6},{8,9},{9,8},{10,11... | collective-permute-start | bytes 307208 | tf_op jit(solution)/shard_map/ppermute | solution.py:266
  14.1 3.3 %collective-permute-start.4 = (f32[48,128]{1,0:T(8,128)S(1)}, f32[48,128]{1,0:T(8,128)S(1)}, u32[]{:S(2)}, u32[]{:S(2)}) collective-permute-start(f32[48,128]{1,0:T(8,128)S(1)} %get-tuple-element.24), channel_id=1, source_target_pairs={{0,3},{1,2},{2,1},{3,0},{4,7},{5,6},{6,5},{7,4},{8,11},{9,10},{10,... | collective-permute-start | bytes 73736 | tf_op jit(solution)/shard_map/ppermute | solution.py:290
  15.4 2.0 %collective-permute-start.5 = (f32[48,128]{1,0:T(8,128)S(1)}, f32[48,128]{1,0:T(8,128)S(1)}, u32[]{:S(2)}, u32[]{:S(2)}) collective-permute-start(f32[48,128]{1,0:T(8,128)S(1)} %get-tuple-element.25), channel_id=1, source_target_pairs={{0,1},{1,0},{2,3},{3,2},{4,5},{5,4},{6,7},{7,6},{8,9},{9,8},{10,11... | collective-permute-start | bytes 73736 | tf_op jit(solution)/shard_map/ppermute | solution.py:289
  15.8 8.3 %collective-permute-start.8 = (f32[152,128]{1,0:T(8,128)S(1)}, f32[152,128]{1,0:T(8,128)S(1)}, u32[]{:S(2)}, u32[]{:S(2)}) collective-permute-start(f32[152,128]{1,0:T(8,128)S(1)} %get-tuple-element.29), channel_id=1, source_target_pairs={{0,4},{4,8},{8,12},{12,16},{16,20},{20,24},{24,28},{28,0},{1,5},{5... | collective-permute-start | bytes 233480 | tf_op jit(solution)/shard_map/ppermute | solution.py:293
  17.5 6.6 %collective-permute-start.7 = (f32[32,128]{1,0:T(8,128)S(1)}, f32[32,128]{1,0:T(8,128)S(1)}, u32[]{:S(2)}, u32[]{:S(2)}) collective-permute-start(f32[32,128]{1,0:T(8,128)S(1)} %pad_maximum_fusion.2), channel_id=1, source_target_pairs={{0,4},{4,8},{8,12},{12,16},{16,20},{20,24},{24,28},{28,0},{1,5},{5... | collective-permute-start | bytes 49160 | tf_op jit(solution)/shard_map/ppermute | solution.py:294
  18.3 6.3 %collective-permute-start.6 = (f32[184,128]{1,0:T(8,128)S(1)}, f32[184,128]{1,0:T(8,128)S(1)}, u32[]{:S(2)}, u32[]{:S(2)}) collective-permute-start(f32[184,128]{1,0:T(8,128)S(1)} %pad_maximum_fusion), channel_id=1, source_target_pairs={{4,0},{8,4},{12,8},{16,12},{20,16},{24,20},{28,24},{0,28},{5,1},{9... | collective-permute-start | bytes 282632 | tf_op jit(solution)/shard_map/ppermute | solution.py:295

commit v5 on v4

--- a/solution.py
+++ b/solution.py
@@ -43,17 +43,18 @@
 PLANES = SUB * DYN
 ITEMS = len(WIDTHS)
 ROW_AT = np.concatenate([[0], np.cumsum(WIDTHS)]).tolist()
-LANE_AT = ROW_AT[:PLANES] + [ROW_AT[i] - ROW_AT[PLANES] for i in range(PLANES, ITEMS)]
+LANE_AT = ROW_AT[:PLANES] + [ROW_AT[PLANES] + i for i in range(ITEMS - PLANES)]
 CORNERS = [max(w - 1, 0) for w in WIDTHS]
 CORNER_AT = np.concatenate([[0], np.cumsum(CORNERS)]).tolist()
 MAIN = -(-ROW_AT[-1] // 8) * 8
-GROUPS = 3
-
-
-def interp_kernel(table, mean, rows, atmo_ref, out_ref, half_ref):
-    fields, levels, tiles, _ = atmo_ref.shape
+GROUPS = 2
+
+
+def interp_kernel(table, mean, rows, first_ref, second_ref, out_ref, half_ref):
+    part, levels, tiles, _ = first_ref.shape
+    fields = part + second_ref.shape[0]
     for f in range(fields):
-        level = [atmo_ref[f, k] for k in range(levels)]
+        level = [first_ref[f, k] if f < part else second_ref[f - part, k] for k in range(levels)]
         if f < DYN:
             for s in range(SUB):
                 terms = [float(table[s, k]) * level[k] for k in range(levels) if table[s, k] != 0]
@@ -61,8 +62,8 @@
         else:
             terms = [float(mean[k]) * level[k] for k in range(levels)]
             out_ref[pl.ds(PLANES + f - DYN, tiles, stride=rows), :] = functools.reduce(jnp.add, terms)
-    part = half_ref.shape[0]
-    half_ref[...] = out_ref[pl.ds(pl.multiple_of(lax.axis_index("col") % 2 * part, 8), part), :]
+    size = half_ref.shape[0]
+    half_ref[...] = out_ref[pl.ds(pl.multiple_of(lax.axis_index("col") % 2 * size, 8), size), :]
 
 
 def split_tiles(source_ref, split_ref, base, rows):
@@ -130,15 +131,15 @@
         ref[ROW_AT[-1] :, :] = jnp.zeros((MAIN - ROW_AT[-1], wide), jnp.float32)
 
     lane = lax.broadcasted_iota(jnp.int32, (high, wide), 1)
-    groups = ((range(PLANES), WIDTHS, LANE_AT), (range(PLANES, ITEMS), WIDTHS, LANE_AT), (range(ITEMS), CORNERS, CORNER_AT))
-    for g, (members, widths, places) in enumerate(groups):
+    own = [(i, WIDTHS[i] if i < PLANES else 1, WIDTHS[i], LANE_AT[i]) for i in range(ITEMS)]
+    out = [(i, CORNERS[i], CORNERS[i], CORNER_AT[i]) for i in range(ITEMS)]
+    for g, group in enumerate((own, out)):
         last = jnp.zeros((high, wide), jnp.float32)
         head = jnp.zeros((high, wide), jnp.float32)
-        for i in members:
-            w, at = widths[i], places[i]
-            if w:
+        for i, count, w, at in group:
+            if count:
                 last = jnp.where(lane >= at, pltpu.roll(items[i], (at + w) % wide, 1), last)
-                head = jnp.where(lane >= at, pltpu.roll(items[i], at, 1), head)
+                head = jnp.where(lane >= at, pltpu.roll(items[i], (at + count - w) % wide, 1), head)
         edge1_ref[g * high : (g + 1) * high, :] = jnp.where(col_even, last, head)
         edge2_ref[g * high : (g + 1) * high, :] = jnp.where(col_even, head, last)
 
@@ -167,9 +168,16 @@
         room = max(rim - at - w, 0)
         main = [jnp.zeros((room, wide), jnp.float32)] if room else []
         main += [top_ref[at + w - rim + room : at + w, :], own, low_ref[high + at : high + at + rim, :]]
+        if i < PLANES:
+            along_own = edge(beside[0], w, LANE_AT[i])
+        else:
+            along_own = edge(beside[1], CORNERS[i], CORNER_AT[i])
+            left, right = beside[0]
+            along_own = jnp.where(lane == w - 1, pltpu.roll(right, (wide + w - 1 - LANE_AT[i]) % wide, 1), along_own)
+            along_own = jnp.where(lane == wide - w, pltpu.roll(left, (2 * wide - w - LANE_AT[i]) % wide, 1), along_own)
         rest = [
             edge(above, CORNERS[i], CORNER_AT[i])[high - rim :],
-            edge(beside[0 if i < PLANES else 1], w, LANE_AT[i]),
+            along_own,
             edge(below, CORNERS[i], CORNER_AT[i])[:rim],
         ]
         return [jnp.concatenate(main, axis=0), jnp.concatenate(rest, axis=0)]
@@ -214,11 +222,12 @@
         grad_x = slope_x(height, shift_refs[:2])
         zonal = each(lambda m, u, g, v, p: m * (u - g + 0.2 * v + 0.5 * p), ocean, zonal, grad_x, merid, push_u)
         merid = each(lambda m, v, g, u, p: m * (v - g - 0.2 * u + 0.5 * p), ocean, merid, grad_y, zonal, push_v)
-        spread = each(jnp.add, slope_x(zonal, shift_refs[2:]), slope_y(merid))
+        slope = slope_x(zonal, shift_refs[2:])
+        spread = each(jnp.add, slope, slope_y(merid))
         height = each(lambda h, d, p: h - d + 0.5 * p, height, spread, push_h)
         if s < SUB - 1:
-            bend = each(jnp.add, slope_x(slope_y(zonal), shift_refs[4:]), slope_yy(merid))
-            grad_y = each(lambda g, d, p: g - d + 0.5 * p, grad_y, bend, slope_y(push_h))
+            rest = slope_y(each(lambda d, p: 0.5 * p - d, slope, push_h))
+            grad_y = each(lambda g, r, b: g + r - b, grad_y, rest, slope_yy(merid))
     for k, value in enumerate((height, zonal, merid)):
         out_ref[k] = value[0][rim : rim + high]
 
@@ -243,11 +252,11 @@
     own, part = pl.pallas_call(
         functools.partial(interp_kernel, table, mean, rows),
         out_shape=(f32(tiles * rows, cells), f32(half * rows, cells)),
-        in_specs=[vmem],
+        in_specs=[vmem] * 2,
         out_specs=(vmem, vmem),
         compiler_params=params(),
         cost_estimate=pl.CostEstimate(flops=10**10, bytes_accessed=4 << 20, transcendentals=0),
-    )(atmo_states)
+    )(atmo_states[: fields // 2], atmo_states[fields // 2 :])
     previous = lax.ppermute(part, "row", onward)
     following = lax.ppermute(part, "row", back)
 
@@ -289,7 +298,7 @@
     from1 = lax.ppermute(edge1, "col", col_near)
     from2 = lax.ppermute(edge2, "col", col_far)
     from2, from1 = lax.optimization_barrier((from2, from1))
-    corners = from1[2 * high :], from2[2 * high :]
+    corners = from1[high:], from2[high:]
     top = lax.ppermute(down, "row", onward)
     corner = lax.ppermute(jnp.concatenate(corners), "row", onward)
     low = lax.ppermute(jnp.concatenate([corners[0], up, corners[1]]), "row", back)
@@ -299,7 +308,7 @@
         out_shape=f32(3, high, wide),
         in_specs=[vmem] * 8,
         out_specs=vmem,
-        scratch_shapes=[pltpu.VMEM((3 * high + 16, wide), jnp.float32)] * 6,
+        scratch_shapes=[pltpu.VMEM((3 * high + 16, wide), jnp.float32)] * 4,
         compiler_params=params(),
     )(total, ocean_state, land_mask, from1, from2, low, corner, top)
     return flux_mean, final

time: 26.4 us -> 26.2 us (level)
    unnamed x10 -> x8, local copies, waits for them, and re-layouts: 1.36 us -> 0.03 us
    slice x2 -> x3, local copies, waits for them, and re-layouts: 0.01 us -> 1.25 us  [the longest x1 1.24 us: per_device(): atmo_states[fields // 2:]]
where the time goes in v5:
time: 26.2 us; the launch traced here: 26 us
  starting transfers between devices  12.8 us (49%)
  waiting for transfers between devices  6.76 us (26%)
  Pallas kernels  3.72 us (14%)
  local copies, waits for them, and re-layouts  1.29 us (5%)
  between operations  0.73 us (3%)
  other arithmetic  0.67 us (3%)
    ppermute x1, starting transfers between devices, per_device(): lax.ppermute(jnp.concatenate([corners[0], up, corners[1]]), 'row', back)  3.85 us
    ppermute x1, starting transfers between devices, per_device(): following = lax.ppermute(part, 'row', back)  3.1 us
    ppermute x1, starting transfers between devices, per_device(): previous = lax.ppermute(part, 'row', onward)  3.02 us
    ppermute x1, waiting for transfers between devices, per_device(): previous = lax.ppermute(part, 'row', onward)  2.09 us
    pallas_call x1, Pallas kernels, per_device(): pl.pallas_call(ocean_kernel, out_shape=f32(3, high, wide), in_specs=[vmem...  1.54 us
    ppermute x1, starting transfers between devices, per_device(): from2 = lax.ppermute(edge2, 'col', col_far)  1.31 us
    ppermute x1, waiting for transfers between devices, per_device(): from2 = lax.ppermute(edge2, 'col', col_far)  1.27 us
    slice x1, local copies, waits for them, and re-layouts, per_device(): atmo_states[fields // 2:]  1.24 us
  transfers between devices with their start and end apart: 9, of which 7 were waited for; matrix products, arithmetic and copies ran while one was open for 3% of the time, Pallas kernels for 5%

profile of v5, /device:TPU:0, one launch (start us, length us, event | category | flops | bytes accessed | tf_op | source)
XLA Modules:
  0.0 26.0 jit_solution(12781502725698618089)
XLA Ops:
  0.6 1.2 %fusion = (f32[5,12,16,128]{3,2,1,0:T(8,128)S(1)}, f32[5,12,16,128]{3,2,1,0:T(8,128)S(1)}) fusion(f32[10,12,16,128]{3,2,1,0:T(8,128)} %param.5), kind=kLoop, calls=%fused_computation.4 | loop fusion | bytes 1966080 | tf_op jit(solution)/shard_map/slice | solution.py:259
  1.9 0.0 copy-start
  1.9 0.0 copy-start.3
  1.9 0.1 shard_map.68
  2.0 0.0 copy-start.1
  2.0 0.0 copy-start.2
  2.0 3.0 %collective-permute-start.2 = (f32[200,128]{1,0:T(8,128)S(1)}, f32[200,128]{1,0:T(8,128)S(1)}, u32[]{:S(2)}, u32[]{:S(2)}) collective-permute-start(f32[200,128]{1,0:T(8,128)S(1)} %get-tuple-element.16), channel_id=1, source_target_pairs={{0,4},{4,8},{8,12},{12,16},{16,20},{20,24},{24,28},{28,0},{1,5},{5... | collective-permute-start | bytes 307208 | tf_op jit(solution)/shard_map/ppermute | solution.py:260
  5.0 3.1 %collective-permute-start = (f32[200,128]{1,0:T(8,128)S(1)}, f32[200,128]{1,0:T(8,128)S(1)}, u32[]{:S(2)}, u32[]{:S(2)}) collective-permute-start(f32[200,128]{1,0:T(8,128)S(1)} %get-tuple-element.16), channel_id=1, source_target_pairs={{4,0},{8,4},{12,8},{16,12},{20,16},{24,20},{28,24},{0,28},{5,1},{9... | collective-permute-start | bytes 307208 | tf_op jit(solution)/shard_map/ppermute | solution.py:261
  8.2 0.0 copy-done
  8.2 0.0 copy-done.3
  8.2 0.8 %shard_map.69 = (f32[32,16,128]{2,1,0:T(8,128)S(1)}, bf16[16,256,256]{2,1,0:T(8,128)(2,1)S(1)}) custom-call(s32[4,16]{1,0:T(4,128)S(1)} %bitcast.2, f32[400,128]{1,0:T(8,128)S(1)} %get-tuple-element.17.own_ref, f32[16,4,128,128]{3,2,1,0:T(8,128)S(1)} %copy-done), custom_call_target="tpu_custom_call" | custom-call | flops 1000000000 | bytes 4194304 | tf_op jit(solution)/shard_map/pallas_call | solution.py:263
  9.0 2.1 %collective-permute-done.2.near_ref = f32[200,128]{1,0:T(8,128)S(1)} collective-permute-done((f32[200,128]{1,0:T(8,128)S(1)}, f32[200,128]{1,0:T(8,128)S(1)}, u32[]{:S(2)}, u32[]{:S(2)}) %collective-permute-start.2) | collective-permute-done | bytes 102432 | tf_op jit(solution)/shard_map/ppermute | solution.py:260
  11.1 0.0 collective-permute-start.3
  11.1 0.8 %collective-permute-done.near_ref = f32[200,128]{1,0:T(8,128)S(1)} collective-permute-done((f32[200,128]{1,0:T(8,128)S(1)}, f32[200,128]{1,0:T(8,128)S(1)}, u32[]{:S(2)}, u32[]{:S(2)}) %collective-permute-start) | collective-permute-done | bytes 102432 | tf_op jit(solution)/shard_map/ppermute | solution.py:261
  11.9 0.0 collective-permute-start.1
  11.9 0.5 %collective-permute-done.3.far_ref = f32[200,128]{1,0:T(8,128)S(1)} collective-permute-done((f32[200,128]{1,0:T(8,128)S(1)}, f32[200,128]{1,0:T(8,128)S(1)}, u32[]{:S(2)}, u32[]{:S(2)}) %collective-permute-start.3) | collective-permute-done | bytes 102432 | tf_op jit(solution)/shard_map/ppermute | solution.py:274
  12.4 0.5 %shard_map.70.add_ref = f32[32,16,128]{2,1,0:T(8,128)S(1)} custom-call(s32[4,16]{1,0:T(4,128)S(1)} %bitcast.3, f32[200,128]{1,0:T(8,128)S(1)} %collective-permute-done.2.near_ref, f32[200,128]{1,0:T(8,128)S(1)} %collective-permute-done.3.far_ref, bf16[16,256,256]{2,1,0:T(8,128)(2,1)S(1)} %get-tuple-element.20.rest_ref, ...), custom_call_target="tpu_custom_call" | custom-call | flops 1000000000 | bytes 2097152 | tf_op jit(solution)/shard_map/pallas_call | solution.py:276
  12.9 0.3 %collective-permute-done.1.far_ref = f32[200,128]{1,0:T(8,128)S(1)} collective-permute-done((f32[200,128]{1,0:T(8,128)S(1)}, f32[200,128]{1,0:T(8,128)S(1)}, u32[]{:S(2)}, u32[]{:S(2)}) %collective-permute-start.1) | collective-permute-done | bytes 102432 | tf_op jit(solution)/shard_map/ppermute | solution.py:275
  13.2 0.0 copy-done.1
  13.2 0.7 %shard_map.71 = (f32[32,16,128]{2,1,0:T(8,128)S(1)}, f32[152,128]{1,0:T(8,128)S(1)}, f32[152,128]{1,0:T(8,128)S(1)}, f32[32,128]{1,0:T(8,128)S(1)}, f32[32,128]{1,0:T(8,128)S(1)}) custom-call(s32[4,16]{1,0:T(4,128)S(1)} %bitcast.4, f32[200,128]{1,0:T(8,128)S(1)} %collective-permute-done.near_ref, f32[200,128]{1,0:T(8,128)S(1)} %collective-permute-done.1.far_ref, ...), custom_call_target="tpu_custom_call" | custom-call | flops 1000000000 | bytes 4194304 | tf_op jit(solution)/shard_map/pallas_call | solution.py:286
  14.0 1.3 %collective-permute-start.4 = (f32[32,128]{1,0:T(8,128)S(1)}, f32[32,128]{1,0:T(8,128)S(1)}, u32[]{:S(2)}, u32[]{:S(2)}) collective-permute-start(f32[32,128]{1,0:T(8,128)S(1)} %get-tuple-element.24), channel_id=1, source_target_pairs={{0,3},{1,2},{2,1},{3,0},{4,7},{5,6},{6,5},{7,4},{8,11},{9,10},{10,... | collective-permute-start | bytes 49160 | tf_op jit(solution)/shard_map/ppermute | solution.py:299
  15.3 0.4 %collective-permute-start.5 = (f32[32,128]{1,0:T(8,128)S(1)}, f32[32,128]{1,0:T(8,128)S(1)}, u32[]{:S(2)}, u32[]{:S(2)}) collective-permute-start(f32[32,128]{1,0:T(8,128)S(1)} %get-tuple-element.25), channel_id=1, source_target_pairs={{0,1},{1,0},{2,3},{3,2},{4,5},{5,4},{6,7},{7,6},{8,9},{9,8},{10,11... | collective-permute-start | bytes 49160 | tf_op jit(solution)/shard_map/ppermute | solution.py:298
  15.6 0.2 collective-permute-start.8
  15.9 1.3 %collective-permute-done.4.edge2_ref = f32[32,128]{1,0:T(8,128)S(1)} collective-permute-done((f32[32,128]{1,0:T(8,128)S(1)}, f32[32,128]{1,0:T(8,128)S(1)}, u32[]{:S(2)}, u32[]{:S(2)}) %collective-permute-start.4) | collective-permute-done | bytes 16416 | tf_op jit(solution)/shard_map/ppermute | solution.py:299
  17.2 0.0 collective-permute-done.5.edge1_ref
  17.2 1.0 %collective-permute-start.7 = (f32[32,128]{1,0:T(8,128)S(1)}, f32[32,128]{1,0:T(8,128)S(1)}, u32[]{:S(2)}, u32[]{:S(2)}) collective-permute-start(f32[32,128]{1,0:T(8,128)S(1)} %pad_maximum_fusion.2), channel_id=1, source_target_pairs={{0,4},{4,8},{8,12},{12,16},{16,20},{20,24},{24,28},{28,0},{1,5},{5... | collective-permute-start | bytes 49160 | tf_op jit(solution)/shard_map/ppermute | solution.py:303
  18.2 3.8 %collective-permute-start.6 = (f32[184,128]{1,0:T(8,128)S(1)}, f32[184,128]{1,0:T(8,128)S(1)}, u32[]{:S(2)}, u32[]{:S(2)}) collective-permute-start(f32[184,128]{1,0:T(8,128)S(1)} %pad_maximum_fusion), channel_id=1, source_target_pairs={{4,0},{8,4},{12,8},{16,12},{20,16},{24,20},{28,24},{0,28},{5,1},{9... | collective-permute-start | bytes 282632 | tf_op jit(solution)/shard_map/ppermute | solution.py:304
  22.0 0.6 %pad_maximum_fusion.1 = f32[10,16,128]{2,1,0:T(8,128)} fusion(f32[7,16,128]{2,1,0:T(8,128)S(1)} %slice.21, f32[3,16,128]{2,1,0:T(8,128)S(1)} %broadcast_multiply_fusion), kind=kLoop, calls=%fused_computation.1 | loop fusion | flops 20480 | bytes 163840 | tf_op jit(solution)/shard_map/concatenate | solution.py:296
  22.7 1.1 %collective-permute-done.7.corner_ref = f32[32,128]{1,0:T(8,128)S(1)} collective-permute-done((f32[32,128]{1,0:T(8,128)S(1)}, f32[32,128]{1,0:T(8,128)S(1)}, u32[]{:S(2)}, u32[]{:S(2)}) %collective-permute-start.7) | collective-permute-done | bytes 16416 | tf_op jit(solution)/shard_map/ppermute | solution.py:303
  23.8 0.0 collective-permute-done.8.top_ref
  23.8 0.7 %collective-permute-done.6.low_ref = f32[184,128]{1,0:T(8,128)S(1)} collective-permute-done((f32[184,128]{1,0:T(8,128)S(1)}, f32[184,128]{1,0:T(8,128)S(1)}, u32[]{:S(2)}, u32[]{:S(2)}) %collective-permute-start.6) | collective-permute-done | bytes 94240 | tf_op jit(solution)/shard_map/ppermute | solution.py:304
  24.5 1.5 %shard_map.72 = f32[3,16,128]{2,1,0:T(8,128)} custom-call(f32[32,16,128]{2,1,0:T(8,128)S(1)} %get-tuple-element.23.force_ref, f32[3,16,128]{2,1,0:T(8,128)S(1)} %copy-done.1, s32[16,128]{1,0:T(8,128)S(1)} %copy-done.2, f32[32,128]{1,0:T(8,128)S(1)} %collective-permute-done.5.edge1_ref, f32[32,128]{1,0:T(8,128)S(1)} %collective-permute-done.4.edge2_ref, ...), custom_call_target="tpu_custom_call" | custom-call | tf_op jit(solution)/shard_map/pallas_call | solution.py:306
  (9 shorter events, 0.1 us)
Async XLA Ops:
  1.9 6.3 %copy-start = (f32[16,4,128,128]{3,2,1,0:T(8,128)S(1)}, f32[16,4,128,128]{3,2,1,0:T(8,128)}, u32[]{:S(2)}) copy-start(f32[16,4,128,128]{3,2,1,0:T(8,128)} %weight_ref.1) | copy-start | bytes 12582916
  1.9 6.3 %copy-start.3 = (s32[16,4]{0,1:T(4,128)S(1)}, s32[16,4]{0,1:T(4,128)}, u32[]{:S(2)}) copy-start(s32[16,4]{0,1:T(4,128)} %param.7) | copy-start | bytes 772
  2.0 11.2 %copy-start.1 = (f32[3,16,128]{2,1,0:T(8,128)S(1)}, f32[3,16,128]{2,1,0:T(8,128)}, u32[]{:S(2)}) copy-start(f32[3,16,128]{2,1,0:T(8,128)} %state_ref.3) | copy-start | bytes 73732
  2.0 11.2 %copy-start.2 = (s32[16,128]{1,0:T(8,128)S(1)}, s32[16,128]{1,0:T(8,128)}, u32[]{:S(2)}) copy-start(s32[16,128]{1,0:T(8,128)} %mask_ref.3) | copy-start | bytes 24580
  2.0 9.0 %collective-permute-start.2 = (f32[200,128]{1,0:T(8,128)S(1)}, f32[200,128]{1,0:T(8,128)S(1)}, u32[]{:S(2)}, u32[]{:S(2)}) collective-permute-start(f32[200,128]{1,0:T(8,128)S(1)} %get-tuple-element.16), channel_id=1, source_target_pairs={{0,4},{4,8},{8,12},{12,16},{16,20},{20,24},{24,28},{28,0},{1,5},{5... | collective-permute-start | bytes 307208 | tf_op jit(solution)/shard_map/ppermute | solution.py:260
  5.0 6.9 %collective-permute-start = (f32[200,128]{1,0:T(8,128)S(1)}, f32[200,128]{1,0:T(8,128)S(1)}, u32[]{:S(2)}, u32[]{:S(2)}) collective-permute-start(f32[200,128]{1,0:T(8,128)S(1)} %get-tuple-element.16), channel_id=1, source_target_pairs={{4,0},{8,4},{12,8},{16,12},{20,16},{24,20},{28,24},{0,28},{5,1},{9... | collective-permute-start | bytes 307208 | tf_op jit(solution)/shard_map/ppermute | solution.py:261
  11.1 1.3 %collective-permute-start.3 = (f32[200,128]{1,0:T(8,128)S(1)}, f32[200,128]{1,0:T(8,128)S(1)}, u32[]{:S(2)}, u32[]{:S(2)}) collective-permute-start(f32[200,128]{1,0:T(8,128)S(1)} %collective-permute-done.2.near_ref), channel_id=1, source_target_pairs={{0,1},{1,0},{2,3},{3,2},{4,5},{5,4},{6,7},{7,6},{8,9},{9,8},{10,11... | collective-permute-start | bytes 307208 | tf_op jit(solution)/shard_map/ppermute | solution.py:274
  11.9 1.3 %collective-permute-start.1 = (f32[200,128]{1,0:T(8,128)S(1)}, f32[200,128]{1,0:T(8,128)S(1)}, u32[]{:S(2)}, u32[]{:S(2)}) collective-permute-start(f32[200,128]{1,0:T(8,128)S(1)} %collective-permute-done.near_ref), channel_id=1, source_target_pairs={{0,1},{1,0},{2,3},{3,2},{4,5},{5,4},{6,7},{7,6},{8,9},{9,8},{10,11... | collective-permute-start | bytes 307208 | tf_op jit(solution)/shard_map/ppermute | solution.py:275
  14.0 3.2 %collective-permute-start.4 = (f32[32,128]{1,0:T(8,128)S(1)}, f32[32,128]{1,0:T(8,128)S(1)}, u32[]{:S(2)}, u32[]{:S(2)}) collective-permute-start(f32[32,128]{1,0:T(8,128)S(1)} %get-tuple-element.24), channel_id=1, source_target_pairs={{0,3},{1,2},{2,1},{3,0},{4,7},{5,6},{6,5},{7,4},{8,11},{9,10},{10,... | collective-permute-start | bytes 49160 | tf_op jit(solution)/shard_map/ppermute | solution.py:299
  15.3 1.9 %collective-permute-start.5 = (f32[32,128]{1,0:T(8,128)S(1)}, f32[32,128]{1,0:T(8,128)S(1)}, u32[]{:S(2)}, u32[]{:S(2)}) collective-permute-start(f32[32,128]{1,0:T(8,128)S(1)} %get-tuple-element.25), channel_id=1, source_target_pairs={{0,1},{1,0},{2,3},{3,2},{4,5},{5,4},{6,7},{7,6},{8,9},{9,8},{10,11... | collective-permute-start | bytes 49160 | tf_op jit(solution)/shard_map/ppermute | solution.py:298
  15.6 8.2 %collective-permute-start.8 = (f32[152,128]{1,0:T(8,128)S(1)}, f32[152,128]{1,0:T(8,128)S(1)}, u32[]{:S(2)}, u32[]{:S(2)}) collective-permute-start(f32[152,128]{1,0:T(8,128)S(1)} %get-tuple-element.29), channel_id=1, source_target_pairs={{0,4},{4,8},{8,12},{12,16},{16,20},{20,24},{24,28},{28,0},{1,5},{5... | collective-permute-start | bytes 233480 | tf_op jit(solution)/shard_map/ppermute | solution.py:302
  17.2 6.6 %collective-permute-start.7 = (f32[32,128]{1,0:T(8,128)S(1)}, f32[32,128]{1,0:T(8,128)S(1)}, u32[]{:S(2)}, u32[]{:S(2)}) collective-permute-start(f32[32,128]{1,0:T(8,128)S(1)} %pad_maximum_fusion.2), channel_id=1, source_target_pairs={{0,4},{4,8},{8,12},{12,16},{16,20},{20,24},{24,28},{28,0},{1,5},{5... | collective-permute-start | bytes 49160 | tf_op jit(solution)/shard_map/ppermute | solution.py:303
  18.2 6.3 %collective-permute-start.6 = (f32[184,128]{1,0:T(8,128)S(1)}, f32[184,128]{1,0:T(8,128)S(1)}, u32[]{:S(2)}, u32[]{:S(2)}) collective-permute-start(f32[184,128]{1,0:T(8,128)S(1)} %pad_maximum_fusion), channel_id=1, source_target_pairs={{4,0},{8,4},{12,8},{16,12},{20,16},{24,20},{28,24},{0,28},{5,1},{9... | collective-permute-start | bytes 282632 | tf_op jit(solution)/shard_map/ppermute | solution.py:304

commit v6 on v5

--- a/solution.py
+++ b/solution.py
@@ -39,11 +39,11 @@
 
 
 WIDTHS = [2 * (SUB - s) - (1 if f < 2 else 2) for s in range(SUB) for f in range(DYN)]
-WIDTHS += [2 * SUB, 2 * SUB - 1, 2 * SUB - 1, 2 * SUB - 1]
+WIDTHS += [2 * SUB, 2 * SUB - 1]
 PLANES = SUB * DYN
 ITEMS = len(WIDTHS)
 ROW_AT = np.concatenate([[0], np.cumsum(WIDTHS)]).tolist()
-LANE_AT = ROW_AT[:PLANES] + [ROW_AT[PLANES] + i for i in range(ITEMS - PLANES)]
+LANE_AT = ROW_AT[:ITEMS]
 CORNERS = [max(w - 1, 0) for w in WIDTHS]
 CORNER_AT = np.concatenate([[0], np.cumsum(CORNERS)]).tolist()
 MAIN = -(-ROW_AT[-1] // 8) * 8
@@ -113,12 +113,18 @@
         total_ref[:, x, :] = remap_row(split_ref[index[slot, x]], rest_ref[x, at : at + cells, :]) + add_ref[:, x, :]
 
 
+def first_push(force_ref, state_ref):
+    zonal, merid = state_ref[1], state_ref[2]
+    return zonal + 0.2 * merid + 0.5 * force_ref[0], merid + 0.5 * force_ref[1]
+
+
 def rim_kernel(rows, tiles_ref, near_ref, far_ref, rest_ref, add_ref, state_ref, mask_ref,
                total_ref, down_ref, up_ref, edge1_ref, edge2_ref, split_ref):
     add_slot(rows, 3, 2, tiles_ref, near_ref, far_ref, rest_ref, add_ref, total_ref, split_ref)
     col_odd = lax.axis_index("col") % 2
 
-    items = [total_ref[p] for p in range(PLANES)] + [state_ref[k] for k in range(DYN)] + [mask_ref[...].astype(jnp.float32)]
+    items = [*first_push(total_ref, state_ref)] + [total_ref[p] for p in range(2, PLANES)]
+    items += [state_ref[0], mask_ref[...].astype(jnp.float32)]
     high, wide = mask_ref.shape
     col_even = col_odd == 0
 
@@ -131,7 +137,7 @@
         ref[ROW_AT[-1] :, :] = jnp.zeros((MAIN - ROW_AT[-1], wide), jnp.float32)
 
     lane = lax.broadcasted_iota(jnp.int32, (high, wide), 1)
-    own = [(i, WIDTHS[i] if i < PLANES else 1, WIDTHS[i], LANE_AT[i]) for i in range(ITEMS)]
+    own = [(i, WIDTHS[i], WIDTHS[i], LANE_AT[i]) for i in range(ITEMS)]
     out = [(i, CORNERS[i], CORNERS[i], CORNER_AT[i]) for i in range(ITEMS)]
     for g, group in enumerate((own, out)):
         last = jnp.zeros((high, wide), jnp.float32)
@@ -153,7 +159,7 @@
     def sides(a, b):
         return jnp.where(col_even, b, a), jnp.where(col_even, a, b)
 
-    beside = [sides(edge1_ref[g * high : (g + 1) * high], edge2_ref[g * high : (g + 1) * high]) for g in range(2)]
+    beside = sides(edge1_ref[:high], edge2_ref[:high])
     above = sides(corner_ref[:high], corner_ref[high:])
     below = sides(low_ref[:high], low_ref[second:])
 
@@ -168,16 +174,9 @@
         room = max(rim - at - w, 0)
         main = [jnp.zeros((room, wide), jnp.float32)] if room else []
         main += [top_ref[at + w - rim + room : at + w, :], own, low_ref[high + at : high + at + rim, :]]
-        if i < PLANES:
-            along_own = edge(beside[0], w, LANE_AT[i])
-        else:
-            along_own = edge(beside[1], CORNERS[i], CORNER_AT[i])
-            left, right = beside[0]
-            along_own = jnp.where(lane == w - 1, pltpu.roll(right, (wide + w - 1 - LANE_AT[i]) % wide, 1), along_own)
-            along_own = jnp.where(lane == wide - w, pltpu.roll(left, (2 * wide - w - LANE_AT[i]) % wide, 1), along_own)
         rest = [
             edge(above, CORNERS[i], CORNER_AT[i])[high - rim :],
-            along_own,
+            edge(beside, w, LANE_AT[i]),
             edge(below, CORNERS[i], CORNER_AT[i])[:rim],
         ]
         return [jnp.concatenate(main, axis=0), jnp.concatenate(rest, axis=0)]
@@ -206,10 +205,9 @@
 
     rim = high
     height = extended(PLANES, state_ref[0], rim)
-    zonal = extended(PLANES + 1, state_ref[1], rim)
-    merid = extended(PLANES + 2, state_ref[2], rim)
-    ocean = extended(PLANES + 3, mask_ref[...].astype(jnp.float32), rim)
+    ocean = extended(PLANES + 1, mask_ref[...].astype(jnp.float32), rim)
     grad_y = slope_y(height)
+    own = [*first_push(force_ref, state_ref)] + [force_ref[p] for p in range(2, PLANES)]
     for s in range(SUB):
         reach = -(-2 * (SUB - s) // 8) * 8
         if reach < rim:
@@ -218,10 +216,13 @@
                 each(lambda v: v[cut : v.shape[0] - cut], field) for field in (height, zonal, merid, ocean, grad_y)
             )
             rim = reach
-        push_u, push_v, push_h = (extended(s * DYN + f, force_ref[s * DYN + f], rim) for f in range(DYN))
+        push_u, push_v, push_h = (extended(s * DYN + f, own[s * DYN + f], rim) for f in range(DYN))
+        if s > 0:
+            push_u = each(lambda u, v, p: u + 0.2 * v + 0.5 * p, zonal, merid, push_u)
+            push_v = each(lambda v, p: v + 0.5 * p, merid, push_v)
         grad_x = slope_x(height, shift_refs[:2])
-        zonal = each(lambda m, u, g, v, p: m * (u - g + 0.2 * v + 0.5 * p), ocean, zonal, grad_x, merid, push_u)
-        merid = each(lambda m, v, g, u, p: m * (v - g - 0.2 * u + 0.5 * p), ocean, merid, grad_y, zonal, push_v)
+        zonal = each(lambda m, p, g: m * (p - g), ocean, push_u, grad_x)
+        merid = each(lambda m, p, g, u: m * (p - g - 0.2 * u), ocean, push_v, grad_y, zonal)
         slope = slope_x(zonal, shift_refs[2:])
         spread = each(jnp.add, slope, slope_y(merid))
         height = each(lambda h, d, p: h - d + 0.5 * p, height, spread, push_h)

time: 26.2 us -> 25.7 us (0.981)
  waiting for transfers between devices: 6.76 us -> 6.38 us
    ppermute x1, waiting for transfers between devices: 0.67 us -> 0.24 us  [per_device(): lax.ppermute(jnp.concatenate([corners[0], up, corners[1]]), 'row', back)]
where the time goes in v6:
time: 25.7 us; the launch traced here: 25.5 us
  starting transfers between devices  12.8 us (50%)
  waiting for transfers between devices  6.38 us (25%)
  Pallas kernels  3.66 us (14%)
  local copies, waits for them, and re-layouts  1.29 us (5%)
  between operations  0.73 us (3%)
  other arithmetic  0.67 us (3%)
    ppermute x1, starting transfers between devices, per_device(): lax.ppermute(jnp.concatenate([corners[0], up, corners[1]]), 'row', back)  3.8 us
    ppermute x1, starting transfers between devices, per_device(): following = lax.ppermute(part, 'row', back)  3.1 us
    ppermute x1, starting transfers between devices, per_device(): previous = lax.ppermute(part, 'row', onward)  3.02 us
    ppermute x1, waiting for transfers between devices, per_device(): previous = lax.ppermute(part, 'row', onward)  2.09 us
    pallas_call x1, Pallas kernels, per_device(): pl.pallas_call(ocean_kernel, out_shape=f32(3, high, wide), in_specs=[vmem...  1.49 us
    ppermute x1, starting transfers between devices, per_device(): from2 = lax.ppermute(edge2, 'col', col_far)  1.31 us
    ppermute x1, waiting for transfers between devices, per_device(): from2 = lax.ppermute(edge2, 'col', col_far)  1.27 us
    slice x1, local copies, waits for them, and re-layouts, per_device(): atmo_states[fields // 2:]  1.24 us
  transfers between devices with their start and end apart: 9, of which 7 were waited for; matrix products, arithmetic and copies ran while one was open for 3% of the time, Pallas kernels for 5%

profile of v6, /device:TPU:0, one launch (start us, length us, event | category | flops | bytes accessed | tf_op | source)
XLA Modules:
  0.0 25.5 jit_solution(9914495581852361368)
XLA Ops:
  0.6 1.2 %fusion = (f32[5,12,16,128]{3,2,1,0:T(8,128)S(1)}, f32[5,12,16,128]{3,2,1,0:T(8,128)S(1)}) fusion(f32[10,12,16,128]{3,2,1,0:T(8,128)} %param.5), kind=kLoop, calls=%fused_computation.4 | loop fusion | bytes 1966080 | tf_op jit(solution)/shard_map/slice | solution.py:260
  1.9 0.0 copy-start
  1.9 0.0 copy-start.3
  1.9 0.1 shard_map.68
  2.0 0.0 copy-start.1
  2.0 0.0 copy-start.2
  2.0 3.0 %collective-permute-start.2 = (f32[200,128]{1,0:T(8,128)S(1)}, f32[200,128]{1,0:T(8,128)S(1)}, u32[]{:S(2)}, u32[]{:S(2)}) collective-permute-start(f32[200,128]{1,0:T(8,128)S(1)} %get-tuple-element.16), channel_id=1, source_target_pairs={{0,4},{4,8},{8,12},{12,16},{16,20},{20,24},{24,28},{28,0},{1,5},{5... | collective-permute-start | bytes 307208 | tf_op jit(solution)/shard_map/ppermute | solution.py:261
  5.0 3.1 %collective-permute-start = (f32[200,128]{1,0:T(8,128)S(1)}, f32[200,128]{1,0:T(8,128)S(1)}, u32[]{:S(2)}, u32[]{:S(2)}) collective-permute-start(f32[200,128]{1,0:T(8,128)S(1)} %get-tuple-element.16), channel_id=1, source_target_pairs={{4,0},{8,4},{12,8},{16,12},{20,16},{24,20},{28,24},{0,28},{5,1},{9... | collective-permute-start | bytes 307208 | tf_op jit(solution)/shard_map/ppermute | solution.py:262
  8.2 0.0 copy-done
  8.2 0.0 copy-done.3
  8.2 0.8 %shard_map.69 = (f32[32,16,128]{2,1,0:T(8,128)S(1)}, bf16[16,256,256]{2,1,0:T(8,128)(2,1)S(1)}) custom-call(s32[4,16]{1,0:T(4,128)S(1)} %bitcast.2, f32[400,128]{1,0:T(8,128)S(1)} %get-tuple-element.17.own_ref, f32[16,4,128,128]{3,2,1,0:T(8,128)S(1)} %copy-done), custom_call_target="tpu_custom_call" | custom-call | flops 1000000000 | bytes 4194304 | tf_op jit(solution)/shard_map/pallas_call | solution.py:264
  9.0 2.1 %collective-permute-done.2.near_ref = f32[200,128]{1,0:T(8,128)S(1)} collective-permute-done((f32[200,128]{1,0:T(8,128)S(1)}, f32[200,128]{1,0:T(8,128)S(1)}, u32[]{:S(2)}, u32[]{:S(2)}) %collective-permute-start.2) | collective-permute-done | bytes 102432 | tf_op jit(solution)/shard_map/ppermute | solution.py:261
  11.1 0.0 collective-permute-start.3
  11.1 0.8 %collective-permute-done.near_ref = f32[200,128]{1,0:T(8,128)S(1)} collective-permute-done((f32[200,128]{1,0:T(8,128)S(1)}, f32[200,128]{1,0:T(8,128)S(1)}, u32[]{:S(2)}, u32[]{:S(2)}) %collective-permute-start) | collective-permute-done | bytes 102432 | tf_op jit(solution)/shard_map/ppermute | solution.py:262
  11.9 0.0 collective-permute-start.1
  11.9 0.5 %collective-permute-done.3.far_ref = f32[200,128]{1,0:T(8,128)S(1)} collective-permute-done((f32[200,128]{1,0:T(8,128)S(1)}, f32[200,128]{1,0:T(8,128)S(1)}, u32[]{:S(2)}, u32[]{:S(2)}) %collective-permute-start.3) | collective-permute-done | bytes 102432 | tf_op jit(solution)/shard_map/ppermute | solution.py:275
  12.4 0.5 %shard_map.70.add_ref = f32[32,16,128]{2,1,0:T(8,128)S(1)} custom-call(s32[4,16]{1,0:T(4,128)S(1)} %bitcast.3, f32[200,128]{1,0:T(8,128)S(1)} %collective-permute-done.2.near_ref, f32[200,128]{1,0:T(8,128)S(1)} %collective-permute-done.3.far_ref, bf16[16,256,256]{2,1,0:T(8,128)(2,1)S(1)} %get-tuple-element.20.rest_ref, ...), custom_call_target="tpu_custom_call" | custom-call | flops 1000000000 | bytes 2097152 | tf_op jit(solution)/shard_map/pallas_call | solution.py:277
  12.9 0.3 %collective-permute-done.1.far_ref = f32[200,128]{1,0:T(8,128)S(1)} collective-permute-done((f32[200,128]{1,0:T(8,128)S(1)}, f32[200,128]{1,0:T(8,128)S(1)}, u32[]{:S(2)}, u32[]{:S(2)}) %collective-permute-start.1) | collective-permute-done | bytes 102432 | tf_op jit(solution)/shard_map/ppermute | solution.py:276
  13.2 0.0 copy-done.1
  13.2 0.7 %shard_map.71 = (f32[32,16,128]{2,1,0:T(8,128)S(1)}, f32[128,128]{1,0:T(8,128)S(1)}, f32[128,128]{1,0:T(8,128)S(1)}, f32[32,128]{1,0:T(8,128)S(1)}, f32[32,128]{1,0:T(8,128)S(1)}) custom-call(s32[4,16]{1,0:T(4,128)S(1)} %bitcast.4, f32[200,128]{1,0:T(8,128)S(1)} %collective-permute-done.near_ref, f32[200,128]{1,0:T(8,128)S(1)} %collective-permute-done.1.far_ref, ...), custom_call_target="tpu_custom_call" | custom-call | flops 1000000000 | bytes 4194304 | tf_op jit(solution)/shard_map/pallas_call | solution.py:287
  14.0 1.3 %collective-permute-start.4 = (f32[32,128]{1,0:T(8,128)S(1)}, f32[32,128]{1,0:T(8,128)S(1)}, u32[]{:S(2)}, u32[]{:S(2)}) collective-permute-start(f32[32,128]{1,0:T(8,128)S(1)} %get-tuple-element.24), channel_id=1, source_target_pairs={{0,3},{1,2},{2,1},{3,0},{4,7},{5,6},{6,5},{7,4},{8,11},{9,10},{10,... | collective-permute-start | bytes 49160 | tf_op jit(solution)/shard_map/ppermute | solution.py:300
  15.3 0.4 %collective-permute-start.5 = (f32[32,128]{1,0:T(8,128)S(1)}, f32[32,128]{1,0:T(8,128)S(1)}, u32[]{:S(2)}, u32[]{:S(2)}) collective-permute-start(f32[32,128]{1,0:T(8,128)S(1)} %get-tuple-element.25), channel_id=1, source_target_pairs={{0,1},{1,0},{2,3},{3,2},{4,5},{5,4},{6,7},{7,6},{8,9},{9,8},{10,11... | collective-permute-start | bytes 49160 | tf_op jit(solution)/shard_map/ppermute | solution.py:299
  15.6 0.2 collective-permute-start.8
  15.9 1.3 %collective-permute-done.4.edge2_ref = f32[32,128]{1,0:T(8,128)S(1)} collective-permute-done((f32[32,128]{1,0:T(8,128)S(1)}, f32[32,128]{1,0:T(8,128)S(1)}, u32[]{:S(2)}, u32[]{:S(2)}) %collective-permute-start.4) | collective-permute-done | bytes 16416 | tf_op jit(solution)/shard_map/ppermute | solution.py:300
  17.2 0.0 collective-permute-done.5.edge1_ref
  17.2 1.0 %collective-permute-start.7 = (f32[32,128]{1,0:T(8,128)S(1)}, f32[32,128]{1,0:T(8,128)S(1)}, u32[]{:S(2)}, u32[]{:S(2)}) collective-permute-start(f32[32,128]{1,0:T(8,128)S(1)} %pad_maximum_fusion.2), channel_id=1, source_target_pairs={{0,4},{4,8},{8,12},{12,16},{16,20},{20,24},{24,28},{28,0},{1,5},{5... | collective-permute-start | bytes 49160 | tf_op jit(solution)/shard_map/ppermute | solution.py:304
  18.2 3.8 %collective-permute-start.6 = (f32[160,128]{1,0:T(8,128)S(1)}, f32[160,128]{1,0:T(8,128)S(1)}, u32[]{:S(2)}, u32[]{:S(2)}) collective-permute-start(f32[160,128]{1,0:T(8,128)S(1)} %pad_maximum_fusion.1), channel_id=1, source_target_pairs={{4,0},{8,4},{12,8},{16,12},{20,16},{24,20},{28,24},{0,28},{5,1},{9... | collective-permute-start | bytes 245768 | tf_op jit(solution)/shard_map/ppermute | solution.py:305
  22.0 0.6 %pad_maximum_fusion = f32[10,16,128]{2,1,0:T(8,128)} fusion(f32[7,16,128]{2,1,0:T(8,128)S(1)} %slice.21, f32[3,16,128]{2,1,0:T(8,128)S(1)} %broadcast_multiply_fusion), kind=kLoop, calls=%fused_computation | loop fusion | flops 20480 | bytes 163840 | tf_op jit(solution)/shard_map/concatenate | solution.py:297
  22.6 1.2 %collective-permute-done.7.corner_ref = f32[32,128]{1,0:T(8,128)S(1)} collective-permute-done((f32[32,128]{1,0:T(8,128)S(1)}, f32[32,128]{1,0:T(8,128)S(1)}, u32[]{:S(2)}, u32[]{:S(2)}) %collective-permute-start.7) | collective-permute-done | bytes 16416 | tf_op jit(solution)/shard_map/ppermute | solution.py:304
  23.8 0.0 collective-permute-done.8.top_ref
  23.8 0.2 collective-permute-done.6.low_ref
  24.0 1.5 %shard_map.72 = f32[3,16,128]{2,1,0:T(8,128)} custom-call(f32[32,16,128]{2,1,0:T(8,128)S(1)} %get-tuple-element.23.force_ref, f32[3,16,128]{2,1,0:T(8,128)S(1)} %copy-done.1, s32[16,128]{1,0:T(8,128)S(1)} %copy-done.2, f32[32,128]{1,0:T(8,128)S(1)} %collective-permute-done.5.edge1_ref, f32[32,128]{1,0:T(8,128)S(1)} %collective-permute-done.4.edge2_ref, ...), custom_call_target="tpu_custom_call" | custom-call | tf_op jit(solution)/shard_map/pallas_call | solution.py:307
  (9 shorter events, 0.1 us)
Async XLA Ops:
  1.9 6.3 %copy-start = (f32[16,4,128,128]{3,2,1,0:T(8,128)S(1)}, f32[16,4,128,128]{3,2,1,0:T(8,128)}, u32[]{:S(2)}) copy-start(f32[16,4,128,128]{3,2,1,0:T(8,128)} %weight_ref.1) | copy-start | bytes 12582916
  1.9 6.3 %copy-start.3 = (s32[16,4]{0,1:T(4,128)S(1)}, s32[16,4]{0,1:T(4,128)}, u32[]{:S(2)}) copy-start(s32[16,4]{0,1:T(4,128)} %param.7) | copy-start | bytes 772
  2.0 11.2 %copy-start.1 = (f32[3,16,128]{2,1,0:T(8,128)S(1)}, f32[3,16,128]{2,1,0:T(8,128)}, u32[]{:S(2)}) copy-start(f32[3,16,128]{2,1,0:T(8,128)} %state_ref.3) | copy-start | bytes 73732
  2.0 11.2 %copy-start.2 = (s32[16,128]{1,0:T(8,128)S(1)}, s32[16,128]{1,0:T(8,128)}, u32[]{:S(2)}) copy-start(s32[16,128]{1,0:T(8,128)} %mask_ref.3) | copy-start | bytes 24580
  2.0 9.0 %collective-permute-start.2 = (f32[200,128]{1,0:T(8,128)S(1)}, f32[200,128]{1,0:T(8,128)S(1)}, u32[]{:S(2)}, u32[]{:S(2)}) collective-permute-start(f32[200,128]{1,0:T(8,128)S(1)} %get-tuple-element.16), channel_id=1, source_target_pairs={{0,4},{4,8},{8,12},{12,16},{16,20},{20,24},{24,28},{28,0},{1,5},{5... | collective-permute-start | bytes 307208 | tf_op jit(solution)/shard_map/ppermute | solution.py:261
  5.0 6.9 %collective-permute-start = (f32[200,128]{1,0:T(8,128)S(1)}, f32[200,128]{1,0:T(8,128)S(1)}, u32[]{:S(2)}, u32[]{:S(2)}) collective-permute-start(f32[200,128]{1,0:T(8,128)S(1)} %get-tuple-element.16), channel_id=1, source_target_pairs={{4,0},{8,4},{12,8},{16,12},{20,16},{24,20},{28,24},{0,28},{5,1},{9... | collective-permute-start | bytes 307208 | tf_op jit(solution)/shard_map/ppermute | solution.py:262
  11.1 1.3 %collective-permute-start.3 = (f32[200,128]{1,0:T(8,128)S(1)}, f32[200,128]{1,0:T(8,128)S(1)}, u32[]{:S(2)}, u32[]{:S(2)}) collective-permute-start(f32[200,128]{1,0:T(8,128)S(1)} %collective-permute-done.2.near_ref), channel_id=1, source_target_pairs={{0,1},{1,0},{2,3},{3,2},{4,5},{5,4},{6,7},{7,6},{8,9},{9,8},{10,11... | collective-permute-start | bytes 307208 | tf_op jit(solution)/shard_map/ppermute | solution.py:275
  11.9 1.3 %collective-permute-start.1 = (f32[200,128]{1,0:T(8,128)S(1)}, f32[200,128]{1,0:T(8,128)S(1)}, u32[]{:S(2)}, u32[]{:S(2)}) collective-permute-start(f32[200,128]{1,0:T(8,128)S(1)} %collective-permute-done.near_ref), channel_id=1, source_target_pairs={{0,1},{1,0},{2,3},{3,2},{4,5},{5,4},{6,7},{7,6},{8,9},{9,8},{10,11... | collective-permute-start | bytes 307208 | tf_op jit(solution)/shard_map/ppermute | solution.py:276
  14.0 3.2 %collective-permute-start.4 = (f32[32,128]{1,0:T(8,128)S(1)}, f32[32,128]{1,0:T(8,128)S(1)}, u32[]{:S(2)}, u32[]{:S(2)}) collective-permute-start(f32[32,128]{1,0:T(8,128)S(1)} %get-tuple-element.24), channel_id=1, source_target_pairs={{0,3},{1,2},{2,1},{3,0},{4,7},{5,6},{6,5},{7,4},{8,11},{9,10},{10,... | collective-permute-start | bytes 49160 | tf_op jit(solution)/shard_map/ppermute | solution.py:300
  15.3 1.9 %collective-permute-start.5 = (f32[32,128]{1,0:T(8,128)S(1)}, f32[32,128]{1,0:T(8,128)S(1)}, u32[]{:S(2)}, u32[]{:S(2)}) collective-permute-start(f32[32,128]{1,0:T(8,128)S(1)} %get-tuple-element.25), channel_id=1, source_target_pairs={{0,1},{1,0},{2,3},{3,2},{4,5},{5,4},{6,7},{7,6},{8,9},{9,8},{10,11... | collective-permute-start | bytes 49160 | tf_op jit(solution)/shard_map/ppermute | solution.py:299
  15.6 8.2 %collective-permute-start.8 = (f32[128,128]{1,0:T(8,128)S(1)}, f32[128,128]{1,0:T(8,128)S(1)}, u32[]{:S(2)}, u32[]{:S(2)}) collective-permute-start(f32[128,128]{1,0:T(8,128)S(1)} %get-tuple-element.29), channel_id=1, source_target_pairs={{0,4},{4,8},{8,12},{12,16},{16,20},{20,24},{24,28},{28,0},{1,5},{5... | collective-permute-start | bytes 196616 | tf_op jit(solution)/shard_map/ppermute | solution.py:303
  17.2 6.6 %collective-permute-start.7 = (f32[32,128]{1,0:T(8,128)S(1)}, f32[32,128]{1,0:T(8,128)S(1)}, u32[]{:S(2)}, u32[]{:S(2)}) collective-permute-start(f32[32,128]{1,0:T(8,128)S(1)} %pad_maximum_fusion.2), channel_id=1, source_target_pairs={{0,4},{4,8},{8,12},{12,16},{16,20},{20,24},{24,28},{28,0},{1,5},{5... | collective-permute-start | bytes 49160 | tf_op jit(solution)/shard_map/ppermute | solution.py:304
  18.2 5.9 %collective-permute-start.6 = (f32[160,128]{1,0:T(8,128)S(1)}, f32[160,128]{1,0:T(8,128)S(1)}, u32[]{:S(2)}, u32[]{:S(2)}) collective-permute-start(f32[160,128]{1,0:T(8,128)S(1)} %pad_maximum_fusion.1), channel_id=1, source_target_pairs={{4,0},{8,4},{12,8},{16,12},{20,16},{24,20},{28,24},{0,28},{5,1},{9... | collective-permute-start | bytes 245768 | tf_op jit(solution)/shard_map/ppermute | solution.py:305

commit v7 on v6

--- a/solution.py
+++ b/solution.py
@@ -44,10 +44,7 @@
 ITEMS = len(WIDTHS)
 ROW_AT = np.concatenate([[0], np.cumsum(WIDTHS)]).tolist()
 LANE_AT = ROW_AT[:ITEMS]
-CORNERS = [max(w - 1, 0) for w in WIDTHS]
-CORNER_AT = np.concatenate([[0], np.cumsum(CORNERS)]).tolist()
 MAIN = -(-ROW_AT[-1] // 8) * 8
-GROUPS = 2
 
 
 def interp_kernel(table, mean, rows, first_ref, second_ref, out_ref, half_ref):
@@ -137,17 +134,14 @@
         ref[ROW_AT[-1] :, :] = jnp.zeros((MAIN - ROW_AT[-1], wide), jnp.float32)
 
     lane = lax.broadcasted_iota(jnp.int32, (high, wide), 1)
-    own = [(i, WIDTHS[i], WIDTHS[i], LANE_AT[i]) for i in range(ITEMS)]
-    out = [(i, CORNERS[i], CORNERS[i], CORNER_AT[i]) for i in range(ITEMS)]
-    for g, group in enumerate((own, out)):
-        last = jnp.zeros((high, wide), jnp.float32)
-        head = jnp.zeros((high, wide), jnp.float32)
-        for i, count, w, at in group:
-            if count:
-                last = jnp.where(lane >= at, pltpu.roll(items[i], (at + w) % wide, 1), last)
-                head = jnp.where(lane >= at, pltpu.roll(items[i], (at + count - w) % wide, 1), head)
-        edge1_ref[g * high : (g + 1) * high, :] = jnp.where(col_even, last, head)
-        edge2_ref[g * high : (g + 1) * high, :] = jnp.where(col_even, head, last)
+    last = jnp.zeros((high, wide), jnp.float32)
+    head = jnp.zeros((high, wide), jnp.float32)
+    for value, w, at in zip(items, WIDTHS, LANE_AT):
+        if w:
+            last = jnp.where(lane >= at, pltpu.roll(value, (at + w) % wide, 1), last)
+            head = jnp.where(lane >= at, pltpu.roll(value, at, 1), head)
+    edge1_ref[...] = jnp.where(col_even, last, head)
+    edge2_ref[...] = jnp.where(col_even, head, last)
 
 
 def ocean_kernel(force_ref, state_ref, mask_ref, edge1_ref, edge2_ref, low_ref, corner_ref, top_ref, out_ref, *shift_refs):
@@ -159,7 +153,7 @@
     def sides(a, b):
         return jnp.where(col_even, b, a), jnp.where(col_even, a, b)
 
-    beside = sides(edge1_ref[:high], edge2_ref[:high])
+    beside = sides(edge1_ref[...], edge2_ref[...])
     above = sides(corner_ref[:high], corner_ref[high:])
     below = sides(low_ref[:high], low_ref[second:])
 
@@ -175,9 +169,9 @@
         main = [jnp.zeros((room, wide), jnp.float32)] if room else []
         main += [top_ref[at + w - rim + room : at + w, :], own, low_ref[high + at : high + at + rim, :]]
         rest = [
-            edge(above, CORNERS[i], CORNER_AT[i])[high - rim :],
+            edge(above, w, LANE_AT[i])[high - rim :],
             edge(beside, w, LANE_AT[i]),
-            edge(below, CORNERS[i], CORNER_AT[i])[:rim],
+            edge(below, w, LANE_AT[i])[:rim],
         ]
         return [jnp.concatenate(main, axis=0), jnp.concatenate(rest, axis=0)]
 
@@ -286,7 +280,7 @@
 
     total, down, up, edge1, edge2 = pl.pallas_call(
         functools.partial(rim_kernel, rows),
-        out_shape=(f32(32, high, wide), f32(MAIN, wide), f32(MAIN, wide), f32(GROUPS * high, wide), f32(GROUPS * high, wide)),
+        out_shape=(f32(32, high, wide), f32(MAIN, wide), f32(MAIN, wide), f32(high, wide), f32(high, wide)),
         in_specs=[vmem] * 7,
         out_specs=(vmem,) * 5,
         scratch_shapes=[pltpu.VMEM((tiles, 64, cells), jnp.bfloat16)],
@@ -299,7 +293,7 @@
     from1 = lax.ppermute(edge1, "col", col_near)
     from2 = lax.ppermute(edge2, "col", col_far)
     from2, from1 = lax.optimization_barrier((from2, from1))
-    corners = from1[high:], from2[high:]
+    corners = from1, from2
     top = lax.ppermute(down, "row", onward)
     corner = lax.ppermute(jnp.concatenate(corners), "row", onward)
     low = lax.ppermute(jnp.concatenate([corners[0], up, corners[1]]), "row", back)

time: 25.7 us -> 25.5 us (level)
  no operation moved by 1% of the time
where the time goes in v7:
time: 25.5 us; the launch traced here: 25.3 us
  starting transfers between devices  12.8 us (50%)
  waiting for transfers between devices  6.29 us (25%)
  Pallas kernels  3.59 us (14%)
  local copies, waits for them, and re-layouts  1.29 us (5%)
  between operations  0.73 us (3%)
  other arithmetic  0.67 us (3%)
    ppermute x1, starting transfers between devices, per_device(): lax.ppermute(jnp.concatenate([corners[0], up, corners[1]]), 'row', back)  3.66 us
    ppermute x1, starting transfers between devices, per_device(): following = lax.ppermute(part, 'row', back)  3.1 us
    ppermute x1, starting transfers between devices, per_device(): previous = lax.ppermute(part, 'row', onward)  3.02 us
    ppermute x1, waiting for transfers between devices, per_device(): previous = lax.ppermute(part, 'row', onward)  2.09 us
    pallas_call x1, Pallas kernels, per_device(): pl.pallas_call(ocean_kernel, out_shape=f32(3, high, wide), in_specs=[vmem...  1.49 us
    ppermute x1, starting transfers between devices, per_device(): from2 = lax.ppermute(edge2, 'col', col_far)  1.32 us
    slice x1, local copies, waits for them, and re-layouts, per_device(): atmo_states[fields // 2:]  1.24 us
    ppermute x1, waiting for transfers between devices, per_device(): from2 = lax.ppermute(edge2, 'col', col_far)  1.18 us
  transfers between devices with their start and end apart: 9, of which 7 were waited for; matrix products, arithmetic and copies ran while one was open for 3% of the time, Pallas kernels for 5%

profile of v7, /device:TPU:0, one launch (start us, length us, event | category | flops | bytes accessed | tf_op | source)
XLA Modules:
  0.0 25.3 jit_solution(3519195638671146195)
XLA Ops:
  0.6 1.2 %fusion = (f32[5,12,16,128]{3,2,1,0:T(8,128)S(1)}, f32[5,12,16,128]{3,2,1,0:T(8,128)S(1)}) fusion(f32[10,12,16,128]{3,2,1,0:T(8,128)} %param.5), kind=kLoop, calls=%fused_computation.4 | loop fusion | bytes 1966080 | tf_op jit(solution)/shard_map/slice | solution.py:254
  1.9 0.0 copy-start
  1.9 0.0 copy-start.3
  1.9 0.1 shard_map.68
  2.0 0.0 copy-start.1
  2.0 0.0 copy-start.2
  2.0 3.0 %collective-permute-start.2 = (f32[200,128]{1,0:T(8,128)S(1)}, f32[200,128]{1,0:T(8,128)S(1)}, u32[]{:S(2)}, u32[]{:S(2)}) collective-permute-start(f32[200,128]{1,0:T(8,128)S(1)} %get-tuple-element.16), channel_id=1, source_target_pairs={{0,4},{4,8},{8,12},{12,16},{16,20},{20,24},{24,28},{28,0},{1,5},{5... | collective-permute-start | bytes 307208 | tf_op jit(solution)/shard_map/ppermute | solution.py:255
  5.0 3.1 %collective-permute-start = (f32[200,128]{1,0:T(8,128)S(1)}, f32[200,128]{1,0:T(8,128)S(1)}, u32[]{:S(2)}, u32[]{:S(2)}) collective-permute-start(f32[200,128]{1,0:T(8,128)S(1)} %get-tuple-element.16), channel_id=1, source_target_pairs={{4,0},{8,4},{12,8},{16,12},{20,16},{24,20},{28,24},{0,28},{5,1},{9... | collective-permute-start | bytes 307208 | tf_op jit(solution)/shard_map/ppermute | solution.py:256
  8.2 0.0 copy-done
  8.2 0.0 copy-done.3
  8.2 0.8 %shard_map.69 = (f32[32,16,128]{2,1,0:T(8,128)S(1)}, bf16[16,256,256]{2,1,0:T(8,128)(2,1)S(1)}) custom-call(s32[4,16]{1,0:T(4,128)S(1)} %bitcast.2, f32[400,128]{1,0:T(8,128)S(1)} %get-tuple-element.17.own_ref, f32[16,4,128,128]{3,2,1,0:T(8,128)S(1)} %copy-done), custom_call_target="tpu_custom_call" | custom-call | flops 1000000000 | bytes 4194304 | tf_op jit(solution)/shard_map/pallas_call | solution.py:258
  9.0 2.1 %collective-permute-done.2.near_ref = f32[200,128]{1,0:T(8,128)S(1)} collective-permute-done((f32[200,128]{1,0:T(8,128)S(1)}, f32[200,128]{1,0:T(8,128)S(1)}, u32[]{:S(2)}, u32[]{:S(2)}) %collective-permute-start.2) | collective-permute-done | bytes 102432 | tf_op jit(solution)/shard_map/ppermute | solution.py:255
  11.1 0.0 collective-permute-start.3
  11.1 0.8 %collective-permute-done.near_ref = f32[200,128]{1,0:T(8,128)S(1)} collective-permute-done((f32[200,128]{1,0:T(8,128)S(1)}, f32[200,128]{1,0:T(8,128)S(1)}, u32[]{:S(2)}, u32[]{:S(2)}) %collective-permute-start) | collective-permute-done | bytes 102432 | tf_op jit(solution)/shard_map/ppermute | solution.py:256
  11.9 0.0 collective-permute-start.1
  11.9 0.5 %collective-permute-done.3.far_ref = f32[200,128]{1,0:T(8,128)S(1)} collective-permute-done((f32[200,128]{1,0:T(8,128)S(1)}, f32[200,128]{1,0:T(8,128)S(1)}, u32[]{:S(2)}, u32[]{:S(2)}) %collective-permute-start.3) | collective-permute-done | bytes 102432 | tf_op jit(solution)/shard_map/ppermute | solution.py:269
  12.4 0.5 %shard_map.70.add_ref = f32[32,16,128]{2,1,0:T(8,128)S(1)} custom-call(s32[4,16]{1,0:T(4,128)S(1)} %bitcast.3, f32[200,128]{1,0:T(8,128)S(1)} %collective-permute-done.2.near_ref, f32[200,128]{1,0:T(8,128)S(1)} %collective-permute-done.3.far_ref, bf16[16,256,256]{2,1,0:T(8,128)(2,1)S(1)} %get-tuple-element.20.rest_ref, ...), custom_call_target="tpu_custom_call" | custom-call | flops 1000000000 | bytes 2097152 | tf_op jit(solution)/shard_map/pallas_call | solution.py:271
  12.9 0.3 %collective-permute-done.1.far_ref = f32[200,128]{1,0:T(8,128)S(1)} collective-permute-done((f32[200,128]{1,0:T(8,128)S(1)}, f32[200,128]{1,0:T(8,128)S(1)}, u32[]{:S(2)}, u32[]{:S(2)}) %collective-permute-start.1) | collective-permute-done | bytes 102432 | tf_op jit(solution)/shard_map/ppermute | solution.py:270
  13.2 0.0 copy-done.1
  13.2 0.7 %shard_map.71 = (f32[32,16,128]{2,1,0:T(8,128)S(1)}, f32[128,128]{1,0:T(8,128)S(1)}, f32[128,128]{1,0:T(8,128)S(1)}, f32[16,128]{1,0:T(8,128)S(1)}, f32[16,128]{1,0:T(8,128)S(1)}) custom-call(s32[4,16]{1,0:T(4,128)S(1)} %bitcast.4, f32[200,128]{1,0:T(8,128)S(1)} %collective-permute-done.near_ref, f32[200,128]{1,0:T(8,128)S(1)} %collective-permute-done.1.far_ref, ...), custom_call_target="tpu_custom_call" | custom-call | flops 1000000000 | bytes 4194304 | tf_op jit(solution)/shard_map/pallas_call | solution.py:281
  13.9 1.3 %collective-permute-start.4 = (f32[16,128]{1,0:T(8,128)S(1)}, f32[16,128]{1,0:T(8,128)S(1)}, u32[]{:S(2)}, u32[]{:S(2)}) collective-permute-start(f32[16,128]{1,0:T(8,128)S(1)} %get-tuple-element.24), channel_id=1, source_target_pairs={{0,3},{1,2},{2,1},{3,0},{4,7},{5,6},{6,5},{7,4},{8,11},{9,10},{10,... | collective-permute-start | bytes 24584 | tf_op jit(solution)/shard_map/ppermute | solution.py:294
  15.2 0.3 %collective-permute-start.5 = (f32[16,128]{1,0:T(8,128)S(1)}, f32[16,128]{1,0:T(8,128)S(1)}, u32[]{:S(2)}, u32[]{:S(2)}) collective-permute-start(f32[16,128]{1,0:T(8,128)S(1)} %get-tuple-element.25), channel_id=1, source_target_pairs={{0,1},{1,0},{2,3},{3,2},{4,5},{5,4},{6,7},{7,6},{8,9},{9,8},{10,11... | collective-permute-start | bytes 24584 | tf_op jit(solution)/shard_map/ppermute | solution.py:293
  15.6 0.2 collective-permute-start.8
  15.9 1.2 %collective-permute-done.4.edge2_ref = f32[16,128]{1,0:T(8,128)S(1)} collective-permute-done((f32[16,128]{1,0:T(8,128)S(1)}, f32[16,128]{1,0:T(8,128)S(1)}, u32[]{:S(2)}, u32[]{:S(2)}) %collective-permute-start.4) | collective-permute-done | bytes 8224 | tf_op jit(solution)/shard_map/ppermute | solution.py:294
  17.0 0.0 collective-permute-done.5.edge1_ref
  17.0 1.1 %collective-permute-start.7 = (f32[32,128]{1,0:T(8,128)S(1)}, f32[32,128]{1,0:T(8,128)S(1)}, u32[]{:S(2)}, u32[]{:S(2)}) collective-permute-start(f32[32,128]{1,0:T(8,128)S(1)} %pad_maximum_fusion.2), channel_id=1, source_target_pairs={{0,4},{4,8},{8,12},{12,16},{16,20},{20,24},{24,28},{28,0},{1,5},{5... | collective-permute-start | bytes 49160 | tf_op jit(solution)/shard_map/ppermute | solution.py:298
  18.1 3.7 %collective-permute-start.6 = (f32[160,128]{1,0:T(8,128)S(1)}, f32[160,128]{1,0:T(8,128)S(1)}, u32[]{:S(2)}, u32[]{:S(2)}) collective-permute-start(f32[160,128]{1,0:T(8,128)S(1)} %pad_maximum_fusion.1), channel_id=1, source_target_pairs={{4,0},{8,4},{12,8},{16,12},{20,16},{24,20},{28,24},{0,28},{5,1},{9... | collective-permute-start | bytes 245768 | tf_op jit(solution)/shard_map/ppermute | solution.py:299
  21.8 0.6 %pad_maximum_fusion = f32[10,16,128]{2,1,0:T(8,128)} fusion(f32[7,16,128]{2,1,0:T(8,128)S(1)} %slice.15, f32[3,16,128]{2,1,0:T(8,128)S(1)} %broadcast_multiply_fusion), kind=kLoop, calls=%fused_computation | loop fusion | flops 20480 | bytes 163840 | tf_op jit(solution)/shard_map/concatenate | solution.py:291
  22.4 1.2 %collective-permute-done.7.corner_ref = f32[32,128]{1,0:T(8,128)S(1)} collective-permute-done((f32[32,128]{1,0:T(8,128)S(1)}, f32[32,128]{1,0:T(8,128)S(1)}, u32[]{:S(2)}, u32[]{:S(2)}) %collective-permute-start.7) | collective-permute-done | bytes 16416 | tf_op jit(solution)/shard_map/ppermute | solution.py:298
  23.6 0.0 collective-permute-done.8.top_ref
  23.6 0.2 collective-permute-done.6.low_ref
  23.8 1.5 %shard_map.72 = f32[3,16,128]{2,1,0:T(8,128)} custom-call(f32[32,16,128]{2,1,0:T(8,128)S(1)} %get-tuple-element.23.force_ref, f32[3,16,128]{2,1,0:T(8,128)S(1)} %copy-done.1, s32[16,128]{1,0:T(8,128)S(1)} %copy-done.2, f32[16,128]{1,0:T(8,128)S(1)} %collective-permute-done.5.edge1_ref, f32[16,128]{1,0:T(8,128)S(1)} %collective-permute-done.4.edge2_ref, ...), custom_call_target="tpu_custom_call" | custom-call | tf_op jit(solution)/shard_map/pallas_call | solution.py:301
  (7 shorter events, 0.0 us)
Async XLA Ops:
  1.9 6.3 %copy-start = (f32[16,4,128,128]{3,2,1,0:T(8,128)S(1)}, f32[16,4,128,128]{3,2,1,0:T(8,128)}, u32[]{:S(2)}) copy-start(f32[16,4,128,128]{3,2,1,0:T(8,128)} %weight_ref.1) | copy-start | bytes 12582916
  1.9 6.3 %copy-start.3 = (s32[16,4]{0,1:T(4,128)S(1)}, s32[16,4]{0,1:T(4,128)}, u32[]{:S(2)}) copy-start(s32[16,4]{0,1:T(4,128)} %param.7) | copy-start | bytes 772
  2.0 11.2 %copy-start.1 = (f32[3,16,128]{2,1,0:T(8,128)S(1)}, f32[3,16,128]{2,1,0:T(8,128)}, u32[]{:S(2)}) copy-start(f32[3,16,128]{2,1,0:T(8,128)} %state_ref.3) | copy-start | bytes 73732
  2.0 11.2 %copy-start.2 = (s32[16,128]{1,0:T(8,128)S(1)}, s32[16,128]{1,0:T(8,128)}, u32[]{:S(2)}) copy-start(s32[16,128]{1,0:T(8,128)} %mask_ref.3) | copy-start | bytes 24580
  2.0 9.0 %collective-permute-start.2 = (f32[200,128]{1,0:T(8,128)S(1)}, f32[200,128]{1,0:T(8,128)S(1)}, u32[]{:S(2)}, u32[]{:S(2)}) collective-permute-start(f32[200,128]{1,0:T(8,128)S(1)} %get-tuple-element.16), channel_id=1, source_target_pairs={{0,4},{4,8},{8,12},{12,16},{16,20},{20,24},{24,28},{28,0},{1,5},{5... | collective-permute-start | bytes 307208 | tf_op jit(solution)/shard_map/ppermute | solution.py:255
  5.0 6.9 %collective-permute-start = (f32[200,128]{1,0:T(8,128)S(1)}, f32[200,128]{1,0:T(8,128)S(1)}, u32[]{:S(2)}, u32[]{:S(2)}) collective-permute-start(f32[200,128]{1,0:T(8,128)S(1)} %get-tuple-element.16), channel_id=1, source_target_pairs={{4,0},{8,4},{12,8},{16,12},{20,16},{24,20},{28,24},{0,28},{5,1},{9... | collective-permute-start | bytes 307208 | tf_op jit(solution)/shard_map/ppermute | solution.py:256
  11.1 1.3 %collective-permute-start.3 = (f32[200,128]{1,0:T(8,128)S(1)}, f32[200,128]{1,0:T(8,128)S(1)}, u32[]{:S(2)}, u32[]{:S(2)}) collective-permute-start(f32[200,128]{1,0:T(8,128)S(1)} %collective-permute-done.2.near_ref), channel_id=1, source_target_pairs={{0,1},{1,0},{2,3},{3,2},{4,5},{5,4},{6,7},{7,6},{8,9},{9,8},{10,11... | collective-permute-start | bytes 307208 | tf_op jit(solution)/shard_map/ppermute | solution.py:269
  11.9 1.3 %collective-permute-start.1 = (f32[200,128]{1,0:T(8,128)S(1)}, f32[200,128]{1,0:T(8,128)S(1)}, u32[]{:S(2)}, u32[]{:S(2)}) collective-permute-start(f32[200,128]{1,0:T(8,128)S(1)} %collective-permute-done.near_ref), channel_id=1, source_target_pairs={{0,1},{1,0},{2,3},{3,2},{4,5},{5,4},{6,7},{7,6},{8,9},{9,8},{10,11... | collective-permute-start | bytes 307208 | tf_op jit(solution)/shard_map/ppermute | solution.py:270
  13.9 3.1 %collective-permute-start.4 = (f32[16,128]{1,0:T(8,128)S(1)}, f32[16,128]{1,0:T(8,128)S(1)}, u32[]{:S(2)}, u32[]{:S(2)}) collective-permute-start(f32[16,128]{1,0:T(8,128)S(1)} %get-tuple-element.24), channel_id=1, source_target_pairs={{0,3},{1,2},{2,1},{3,0},{4,7},{5,6},{6,5},{7,4},{8,11},{9,10},{10,... | collective-permute-start | bytes 24584 | tf_op jit(solution)/shard_map/ppermute | solution.py:294
  15.2 1.8 %collective-permute-start.5 = (f32[16,128]{1,0:T(8,128)S(1)}, f32[16,128]{1,0:T(8,128)S(1)}, u32[]{:S(2)}, u32[]{:S(2)}) collective-permute-start(f32[16,128]{1,0:T(8,128)S(1)} %get-tuple-element.25), channel_id=1, source_target_pairs={{0,1},{1,0},{2,3},{3,2},{4,5},{5,4},{6,7},{7,6},{8,9},{9,8},{10,11... | collective-permute-start | bytes 24584 | tf_op jit(solution)/shard_map/ppermute | solution.py:293
  15.6 8.0 %collective-permute-start.8 = (f32[128,128]{1,0:T(8,128)S(1)}, f32[128,128]{1,0:T(8,128)S(1)}, u32[]{:S(2)}, u32[]{:S(2)}) collective-permute-start(f32[128,128]{1,0:T(8,128)S(1)} %get-tuple-element.29), channel_id=1, source_target_pairs={{0,4},{4,8},{8,12},{12,16},{16,20},{20,24},{24,28},{28,0},{1,5},{5... | collective-permute-start | bytes 196616 | tf_op jit(solution)/shard_map/ppermute | solution.py:297
  17.0 6.5 %collective-permute-start.7 = (f32[32,128]{1,0:T(8,128)S(1)}, f32[32,128]{1,0:T(8,128)S(1)}, u32[]{:S(2)}, u32[]{:S(2)}) collective-permute-start(f32[32,128]{1,0:T(8,128)S(1)} %pad_maximum_fusion.2), channel_id=1, source_target_pairs={{0,4},{4,8},{8,12},{12,16},{16,20},{20,24},{24,28},{28,0},{1,5},{5... | collective-permute-start | bytes 49160 | tf_op jit(solution)/shard_map/ppermute | solution.py:298
  18.1 5.7 %collective-permute-start.6 = (f32[160,128]{1,0:T(8,128)S(1)}, f32[160,128]{1,0:T(8,128)S(1)}, u32[]{:S(2)}, u32[]{:S(2)}) collective-permute-start(f32[160,128]{1,0:T(8,128)S(1)} %pad_maximum_fusion.1), channel_id=1, source_target_pairs={{4,0},{8,4},{12,8},{16,12},{20,16},{24,20},{28,24},{0,28},{5,1},{9... | collective-permute-start | bytes 245768 | tf_op jit(solution)/shard_map/ppermute | solution.py:299

commit v8 on v7

--- a/solution.py
+++ b/solution.py
@@ -89,12 +89,16 @@
 
 def own_kernel(rows, tiles_ref, own_ref, weight_ref, acc_ref, rest_ref, split_ref):
     index = tiles_ref[...] - split_ref.shape[0]
+    cells = weight_ref.shape[2]
     split_tiles(own_ref, split_ref, 0, rows)
     for x in range(weight_ref.shape[0]):
         first, second = index[1, x], index[2, x]
         weights = split_weights(weight_ref[x, 1], weight_ref[x, 2])
         acc_ref[:, x, :] = remap_row(jnp.concatenate([split_ref[first], split_ref[second]], axis=1), weights)
-        rest_ref[x] = split_weights(weight_ref[x, 0], weight_ref[x, 3])
+        for k, slot in enumerate((0, 3)):
+            high = weight_ref[x, slot].astype(jnp.bfloat16)
+            low = (weight_ref[x, slot] - high.astype(jnp.float32)).astype(jnp.bfloat16)
+            rest_ref[x, 2 * k * cells : 2 * (k + 1) * cells, :] = jnp.concatenate([high, low], axis=0)
 
 
 def add_slot(rows, slot, offset, tiles_ref, near_ref, far_ref, rest_ref, add_ref, total_ref, split_ref):
@@ -105,9 +109,14 @@
     name = tiles_ref[...] - offset * 2 * part
     index = name % part + part * ((name // part + col_odd) % 2)
     cells = split_ref.shape[2]
-    at = (slot > 0) * cells
+    at = (slot > 0) * 2 * cells
     for x in range(rest_ref.shape[0]):
-        total_ref[:, x, :] = remap_row(split_ref[index[slot, x]], rest_ref[x, at : at + cells, :]) + add_ref[:, x, :]
+        tile = split_ref[index[slot, x]]
+        upper = jnp.concatenate([tile[0:32], tile[0:32]], axis=1)
+        lower = jnp.concatenate([tile[32:64], jnp.zeros_like(tile[32:64])], axis=1)
+        left = jnp.concatenate([upper, lower], axis=0)
+        both = jnp.dot(left, rest_ref[x, at : at + 2 * cells, :], preferred_element_type=jnp.float32)
+        total_ref[:, x, :] = both[0:32] + both[32:64] + add_ref[:, x, :]
 
 
 def first_push(force_ref, state_ref):
@@ -144,7 +153,7 @@
     edge2_ref[...] = jnp.where(col_even, head, last)
 
 
-def ocean_kernel(force_ref, state_ref, mask_ref, edge1_ref, edge2_ref, low_ref, corner_ref, top_ref, out_ref, *shift_refs):
+def ocean_kernel(force_ref, state_ref, mask_ref, edge1_ref, edge2_ref, low_ref, corner_ref, top_ref, out_ref, held_ref, sems, *shift_refs):
     high, wide = mask_ref.shape
     col_even = lax.axis_index("col") % 2 == 0
     second = high + MAIN
@@ -217,14 +226,20 @@
         grad_x = slope_x(height, shift_refs[:2])
         zonal = each(lambda m, p, g: m * (p - g), ocean, push_u, grad_x)
         merid = each(lambda m, p, g, u: m * (p - g - 0.2 * u), ocean, push_v, grad_y, zonal)
+        if s == SUB - 1:
+            for k, value in ((1, zonal), (2, merid)):
+                held_ref[k] = value[0][rim : rim + high]
+                pltpu.make_async_copy(held_ref.at[k], out_ref.at[k], sems.at[k]).start()
         slope = slope_x(zonal, shift_refs[2:])
         spread = each(jnp.add, slope, slope_y(merid))
         height = each(lambda h, d, p: h - d + 0.5 * p, height, spread, push_h)
         if s < SUB - 1:
             rest = slope_y(each(lambda d, p: 0.5 * p - d, slope, push_h))
             grad_y = each(lambda g, r, b: g + r - b, grad_y, rest, slope_yy(merid))
-    for k, value in enumerate((height, zonal, merid)):
-        out_ref[k] = value[0][rim : rim + high]
+    held_ref[0] = height[0][rim : rim + high]
+    pltpu.make_async_copy(held_ref.at[0], out_ref.at[0], sems.at[0]).start()
+    for k in range(3):
+        pltpu.make_async_copy(held_ref.at[k], out_ref.at[k], sems.at[k]).wait()
 
 
 def per_device(size_row, size_col, atmo_states, remap_weights, intersection_tiles, land_mask, ocean_state):
@@ -257,7 +272,7 @@
 
     acc, rest = pl.pallas_call(
         functools.partial(own_kernel, rows),
-        out_shape=(f32(32, high, wide), jax.ShapeDtypeStruct((high, 2 * cells, 2 * wide), jnp.bfloat16)),
+        out_shape=(f32(32, high, wide), jax.ShapeDtypeStruct((high, 4 * cells, wide), jnp.bfloat16)),
         in_specs=[vmem] * 3,
         out_specs=(vmem, vmem),
         scratch_shapes=[pltpu.VMEM((tiles, 64, cells), jnp.bfloat16)],
@@ -302,8 +317,9 @@
         ocean_kernel,
         out_shape=f32(3, high, wide),
         in_specs=[vmem] * 8,
-        out_specs=vmem,
-        scratch_shapes=[pltpu.VMEM((3 * high + 16, wide), jnp.float32)] * 4,
+        out_specs=pl.BlockSpec(memory_space=pl.ANY),
+        scratch_shapes=[pltpu.VMEM((3, high, wide), jnp.float32), pltpu.SemaphoreType.DMA((3,))]
+        + [pltpu.VMEM((3 * high + 16, wide), jnp.float32)] * 4,
         compiler_params=params(),
     )(total, ocean_state, land_mask, from1, from2, low, corner, top)
     return flux_mean, final

time: 25.5 us -> 25.5 us (level)
  no operation moved by 1% of the time
where the time goes in v8:
time: 25.5 us; the launch traced here: 25.4 us
  starting transfers between devices  12.8 us (50%)
  waiting for transfers between devices  6.35 us (25%)
  Pallas kernels  3.57 us (14%)
  local copies, waits for them, and re-layouts  1.29 us (5%)
  between operations  0.73 us (3%)
  other arithmetic  0.67 us (3%)
    ppermute x1, starting transfers between devices, per_device(): lax.ppermute(jnp.concatenate([corners[0], up, corners[1]]), 'row', back)  3.67 us
    ppermute x1, starting transfers between devices, per_device(): following = lax.ppermute(part, 'row', back)  3.1 us
    ppermute x1, starting transfers between devices, per_device(): previous = lax.ppermute(part, 'row', onward)  3.02 us
    ppermute x1, waiting for transfers between devices, per_device(): previous = lax.ppermute(part, 'row', onward)  2.16 us
    pallas_call x1, Pallas kernels, per_device(): pl.pallas_call(ocean_kernel, out_shape=f32(3, high, wide), in_specs=[vmem...  1.51 us
    ppermute x1, starting transfers between devices, per_device(): from2 = lax.ppermute(edge2, 'col', col_far)  1.31 us
    slice x1, local copies, waits for them, and re-layouts, per_device(): atmo_states[fields // 2:]  1.24 us
    ppermute x1, waiting for transfers between devices, per_device(): from2 = lax.ppermute(edge2, 'col', col_far)  1.18 us
  transfers between devices with their start and end apart: 9, of which 7 were waited for; matrix products, arithmetic and copies ran while one was open for 3% of the time, Pallas kernels for 5%

profile of v8, /device:TPU:0, one launch (start us, length us, event | category | flops | bytes accessed | tf_op | source)
XLA Modules:
  0.0 25.4 jit_solution(10189170117902474997)
XLA Ops:
  0.6 1.2 %fusion = (f32[5,12,16,128]{3,2,1,0:T(8,128)S(1)}, f32[5,12,16,128]{3,2,1,0:T(8,128)S(1)}) fusion(f32[10,12,16,128]{3,2,1,0:T(8,128)} %param.5), kind=kLoop, calls=%fused_computation.4 | loop fusion | bytes 1966080 | tf_op jit(solution)/shard_map/slice | solution.py:269
  1.9 0.0 copy-start
  1.9 0.0 copy-start.3
  1.9 0.1 shard_map.68
  2.0 0.0 copy-start.1
  2.0 0.0 copy-start.2
  2.0 3.0 %collective-permute-start.2 = (f32[200,128]{1,0:T(8,128)S(1)}, f32[200,128]{1,0:T(8,128)S(1)}, u32[]{:S(2)}, u32[]{:S(2)}) collective-permute-start(f32[200,128]{1,0:T(8,128)S(1)} %get-tuple-element.16), channel_id=1, source_target_pairs={{0,4},{4,8},{8,12},{12,16},{16,20},{20,24},{24,28},{28,0},{1,5},{5... | collective-permute-start | bytes 307208 | tf_op jit(solution)/shard_map/ppermute | solution.py:270
  5.0 3.1 %collective-permute-start = (f32[200,128]{1,0:T(8,128)S(1)}, f32[200,128]{1,0:T(8,128)S(1)}, u32[]{:S(2)}, u32[]{:S(2)}) collective-permute-start(f32[200,128]{1,0:T(8,128)S(1)} %get-tuple-element.16), channel_id=1, source_target_pairs={{4,0},{8,4},{12,8},{16,12},{20,16},{24,20},{28,24},{0,28},{5,1},{9... | collective-permute-start | bytes 307208 | tf_op jit(solution)/shard_map/ppermute | solution.py:271
  8.2 0.0 copy-done
  8.2 0.0 copy-done.3
  8.2 0.8 %shard_map.69 = (f32[32,16,128]{2,1,0:T(8,128)S(1)}, bf16[16,512,128]{2,1,0:T(8,128)(2,1)S(1)}) custom-call(s32[4,16]{1,0:T(4,128)S(1)} %bitcast.2, f32[400,128]{1,0:T(8,128)S(1)} %get-tuple-element.17.own_ref, f32[16,4,128,128]{3,2,1,0:T(8,128)S(1)} %copy-done), custom_call_target="tpu_custom_call" | custom-call | flops 1000000000 | bytes 4194304 | tf_op jit(solution)/shard_map/pallas_call | solution.py:273
  8.9 2.2 %collective-permute-done.2.near_ref = f32[200,128]{1,0:T(8,128)S(1)} collective-permute-done((f32[200,128]{1,0:T(8,128)S(1)}, f32[200,128]{1,0:T(8,128)S(1)}, u32[]{:S(2)}, u32[]{:S(2)}) %collective-permute-start.2) | collective-permute-done | bytes 102432 | tf_op jit(solution)/shard_map/ppermute | solution.py:270
  11.1 0.0 collective-permute-start.3
  11.1 0.8 %collective-permute-done.near_ref = f32[200,128]{1,0:T(8,128)S(1)} collective-permute-done((f32[200,128]{1,0:T(8,128)S(1)}, f32[200,128]{1,0:T(8,128)S(1)}, u32[]{:S(2)}, u32[]{:S(2)}) %collective-permute-start) | collective-permute-done | bytes 102432 | tf_op jit(solution)/shard_map/ppermute | solution.py:271
  11.9 0.0 collective-permute-start.1
  11.9 0.5 %collective-permute-done.3.far_ref = f32[200,128]{1,0:T(8,128)S(1)} collective-permute-done((f32[200,128]{1,0:T(8,128)S(1)}, f32[200,128]{1,0:T(8,128)S(1)}, u32[]{:S(2)}, u32[]{:S(2)}) %collective-permute-start.3) | collective-permute-done | bytes 102432 | tf_op jit(solution)/shard_map/ppermute | solution.py:284
  12.4 0.5 %shard_map.70.add_ref = f32[32,16,128]{2,1,0:T(8,128)S(1)} custom-call(s32[4,16]{1,0:T(4,128)S(1)} %bitcast.3, f32[200,128]{1,0:T(8,128)S(1)} %collective-permute-done.2.near_ref, f32[200,128]{1,0:T(8,128)S(1)} %collective-permute-done.3.far_ref, bf16[16,512,128]{2,1,0:T(8,128)(2,1)S(1)} %get-tuple-element.20.rest_ref, ...), custom_call_target="tpu_custom_call" | custom-call | flops 1000000000 | bytes 2097152 | tf_op jit(solution)/shard_map/pallas_call | solution.py:286
  12.9 0.3 %collective-permute-done.1.far_ref = f32[200,128]{1,0:T(8,128)S(1)} collective-permute-done((f32[200,128]{1,0:T(8,128)S(1)}, f32[200,128]{1,0:T(8,128)S(1)}, u32[]{:S(2)}, u32[]{:S(2)}) %collective-permute-start.1) | collective-permute-done | bytes 102432 | tf_op jit(solution)/shard_map/ppermute | solution.py:285
  13.2 0.0 copy-done.1
  13.2 0.7 %shard_map.71 = (f32[32,16,128]{2,1,0:T(8,128)S(1)}, f32[128,128]{1,0:T(8,128)S(1)}, f32[128,128]{1,0:T(8,128)S(1)}, f32[16,128]{1,0:T(8,128)S(1)}, f32[16,128]{1,0:T(8,128)S(1)}) custom-call(s32[4,16]{1,0:T(4,128)S(1)} %bitcast.4, f32[200,128]{1,0:T(8,128)S(1)} %collective-permute-done.near_ref, f32[200,128]{1,0:T(8,128)S(1)} %collective-permute-done.1.far_ref, ...), custom_call_target="tpu_custom_call" | custom-call | flops 1000000000 | bytes 4194304 | tf_op jit(solution)/shard_map/pallas_call | solution.py:296
  13.9 1.3 %collective-permute-start.4 = (f32[16,128]{1,0:T(8,128)S(1)}, f32[16,128]{1,0:T(8,128)S(1)}, u32[]{:S(2)}, u32[]{:S(2)}) collective-permute-start(f32[16,128]{1,0:T(8,128)S(1)} %get-tuple-element.24), channel_id=1, source_target_pairs={{0,3},{1,2},{2,1},{3,0},{4,7},{5,6},{6,5},{7,4},{8,11},{9,10},{10,... | collective-permute-start | bytes 24584 | tf_op jit(solution)/shard_map/ppermute | solution.py:309
  15.2 0.4 %collective-permute-start.5 = (f32[16,128]{1,0:T(8,128)S(1)}, f32[16,128]{1,0:T(8,128)S(1)}, u32[]{:S(2)}, u32[]{:S(2)}) collective-permute-start(f32[16,128]{1,0:T(8,128)S(1)} %get-tuple-element.25), channel_id=1, source_target_pairs={{0,1},{1,0},{2,3},{3,2},{4,5},{5,4},{6,7},{7,6},{8,9},{9,8},{10,11... | collective-permute-start | bytes 24584 | tf_op jit(solution)/shard_map/ppermute | solution.py:308
  15.6 0.2 collective-permute-start.8
  15.9 1.2 %collective-permute-done.4.edge2_ref = f32[16,128]{1,0:T(8,128)S(1)} collective-permute-done((f32[16,128]{1,0:T(8,128)S(1)}, f32[16,128]{1,0:T(8,128)S(1)}, u32[]{:S(2)}, u32[]{:S(2)}) %collective-permute-start.4) | collective-permute-done | bytes 8224 | tf_op jit(solution)/shard_map/ppermute | solution.py:309
  17.1 0.0 collective-permute-done.5.edge1_ref
  17.1 1.1 %collective-permute-start.7 = (f32[32,128]{1,0:T(8,128)S(1)}, f32[32,128]{1,0:T(8,128)S(1)}, u32[]{:S(2)}, u32[]{:S(2)}) collective-permute-start(f32[32,128]{1,0:T(8,128)S(1)} %pad_maximum_fusion.2), channel_id=1, source_target_pairs={{0,4},{4,8},{8,12},{12,16},{16,20},{20,24},{24,28},{28,0},{1,5},{5... | collective-permute-start | bytes 49160 | tf_op jit(solution)/shard_map/ppermute | solution.py:313
  18.1 3.7 %collective-permute-start.6 = (f32[160,128]{1,0:T(8,128)S(1)}, f32[160,128]{1,0:T(8,128)S(1)}, u32[]{:S(2)}, u32[]{:S(2)}) collective-permute-start(f32[160,128]{1,0:T(8,128)S(1)} %pad_maximum_fusion.1), channel_id=1, source_target_pairs={{4,0},{8,4},{12,8},{16,12},{20,16},{24,20},{28,24},{0,28},{5,1},{9... | collective-permute-start | bytes 245768 | tf_op jit(solution)/shard_map/ppermute | solution.py:314
  21.8 0.6 %pad_maximum_fusion = f32[10,16,128]{2,1,0:T(8,128)} fusion(f32[7,16,128]{2,1,0:T(8,128)S(1)} %slice.15, f32[3,16,128]{2,1,0:T(8,128)S(1)} %broadcast_multiply_fusion), kind=kLoop, calls=%fused_computation | loop fusion | flops 20480 | bytes 163840 | tf_op jit(solution)/shard_map/concatenate | solution.py:306
  22.4 1.2 %collective-permute-done.7.corner_ref = f32[32,128]{1,0:T(8,128)S(1)} collective-permute-done((f32[32,128]{1,0:T(8,128)S(1)}, f32[32,128]{1,0:T(8,128)S(1)}, u32[]{:S(2)}, u32[]{:S(2)}) %collective-permute-start.7) | collective-permute-done | bytes 16416 | tf_op jit(solution)/shard_map/ppermute | solution.py:313
  23.6 0.0 collective-permute-done.8.top_ref
  23.6 0.2 collective-permute-done.6.low_ref
  23.9 1.5 %shard_map.72 = f32[3,16,128]{2,1,0:T(8,128)} custom-call(f32[32,16,128]{2,1,0:T(8,128)S(1)} %get-tuple-element.23.force_ref, f32[3,16,128]{2,1,0:T(8,128)S(1)} %copy-done.1, s32[16,128]{1,0:T(8,128)S(1)} %copy-done.2, f32[16,128]{1,0:T(8,128)S(1)} %collective-permute-done.5.edge1_ref, f32[16,128]{1,0:T(8,128)S(1)} %collective-permute-done.4.edge2_ref, ...), custom_call_target="tpu_custom_call" | custom-call | tf_op jit(solution)/shard_map/pallas_call | solution.py:316
  (7 shorter events, 0.0 us)
Async XLA Ops:
  1.9 6.3 %copy-start = (f32[16,4,128,128]{3,2,1,0:T(8,128)S(1)}, f32[16,4,128,128]{3,2,1,0:T(8,128)}, u32[]{:S(2)}) copy-start(f32[16,4,128,128]{3,2,1,0:T(8,128)} %weight_ref.1) | copy-start | bytes 12582916
  1.9 6.3 %copy-start.3 = (s32[16,4]{0,1:T(4,128)S(1)}, s32[16,4]{0,1:T(4,128)}, u32[]{:S(2)}) copy-start(s32[16,4]{0,1:T(4,128)} %param.7) | copy-start | bytes 772
  2.0 11.2 %copy-start.1 = (f32[3,16,128]{2,1,0:T(8,128)S(1)}, f32[3,16,128]{2,1,0:T(8,128)}, u32[]{:S(2)}) copy-start(f32[3,16,128]{2,1,0:T(8,128)} %state_ref.3) | copy-start | bytes 73732
  2.0 11.2 %copy-start.2 = (s32[16,128]{1,0:T(8,128)S(1)}, s32[16,128]{1,0:T(8,128)}, u32[]{:S(2)}) copy-start(s32[16,128]{1,0:T(8,128)} %mask_ref.3) | copy-start | bytes 24580
  2.0 9.0 %collective-permute-start.2 = (f32[200,128]{1,0:T(8,128)S(1)}, f32[200,128]{1,0:T(8,128)S(1)}, u32[]{:S(2)}, u32[]{:S(2)}) collective-permute-start(f32[200,128]{1,0:T(8,128)S(1)} %get-tuple-element.16), channel_id=1, source_target_pairs={{0,4},{4,8},{8,12},{12,16},{16,20},{20,24},{24,28},{28,0},{1,5},{5... | collective-permute-start | bytes 307208 | tf_op jit(solution)/shard_map/ppermute | solution.py:270
  5.0 6.9 %collective-permute-start = (f32[200,128]{1,0:T(8,128)S(1)}, f32[200,128]{1,0:T(8,128)S(1)}, u32[]{:S(2)}, u32[]{:S(2)}) collective-permute-start(f32[200,128]{1,0:T(8,128)S(1)} %get-tuple-element.16), channel_id=1, source_target_pairs={{4,0},{8,4},{12,8},{16,12},{20,16},{24,20},{28,24},{0,28},{5,1},{9... | collective-permute-start | bytes 307208 | tf_op jit(solution)/shard_map/ppermute | solution.py:271
  11.1 1.3 %collective-permute-start.3 = (f32[200,128]{1,0:T(8,128)S(1)}, f32[200,128]{1,0:T(8,128)S(1)}, u32[]{:S(2)}, u32[]{:S(2)}) collective-permute-start(f32[200,128]{1,0:T(8,128)S(1)} %collective-permute-done.2.near_ref), channel_id=1, source_target_pairs={{0,1},{1,0},{2,3},{3,2},{4,5},{5,4},{6,7},{7,6},{8,9},{9,8},{10,11... | collective-permute-start | bytes 307208 | tf_op jit(solution)/shard_map/ppermute | solution.py:284
  11.9 1.3 %collective-permute-start.1 = (f32[200,128]{1,0:T(8,128)S(1)}, f32[200,128]{1,0:T(8,128)S(1)}, u32[]{:S(2)}, u32[]{:S(2)}) collective-permute-start(f32[200,128]{1,0:T(8,128)S(1)} %collective-permute-done.near_ref), channel_id=1, source_target_pairs={{0,1},{1,0},{2,3},{3,2},{4,5},{5,4},{6,7},{7,6},{8,9},{9,8},{10,11... | collective-permute-start | bytes 307208 | tf_op jit(solution)/shard_map/ppermute | solution.py:285
  13.9 3.1 %collective-permute-start.4 = (f32[16,128]{1,0:T(8,128)S(1)}, f32[16,128]{1,0:T(8,128)S(1)}, u32[]{:S(2)}, u32[]{:S(2)}) collective-permute-start(f32[16,128]{1,0:T(8,128)S(1)} %get-tuple-element.24), channel_id=1, source_target_pairs={{0,3},{1,2},{2,1},{3,0},{4,7},{5,6},{6,5},{7,4},{8,11},{9,10},{10,... | collective-permute-start | bytes 24584 | tf_op jit(solution)/shard_map/ppermute | solution.py:309
  15.2 1.8 %collective-permute-start.5 = (f32[16,128]{1,0:T(8,128)S(1)}, f32[16,128]{1,0:T(8,128)S(1)}, u32[]{:S(2)}, u32[]{:S(2)}) collective-permute-start(f32[16,128]{1,0:T(8,128)S(1)} %get-tuple-element.25), channel_id=1, source_target_pairs={{0,1},{1,0},{2,3},{3,2},{4,5},{5,4},{6,7},{7,6},{8,9},{9,8},{10,11... | collective-permute-start | bytes 24584 | tf_op jit(solution)/shard_map/ppermute | solution.py:308
  15.6 8.0 %collective-permute-start.8 = (f32[128,128]{1,0:T(8,128)S(1)}, f32[128,128]{1,0:T(8,128)S(1)}, u32[]{:S(2)}, u32[]{:S(2)}) collective-permute-start(f32[128,128]{1,0:T(8,128)S(1)} %get-tuple-element.29), channel_id=1, source_target_pairs={{0,4},{4,8},{8,12},{12,16},{16,20},{20,24},{24,28},{28,0},{1,5},{5... | collective-permute-start | bytes 196616 | tf_op jit(solution)/shard_map/ppermute | solution.py:312
  17.1 6.5 %collective-permute-start.7 = (f32[32,128]{1,0:T(8,128)S(1)}, f32[32,128]{1,0:T(8,128)S(1)}, u32[]{:S(2)}, u32[]{:S(2)}) collective-permute-start(f32[32,128]{1,0:T(8,128)S(1)} %pad_maximum_fusion.2), channel_id=1, source_target_pairs={{0,4},{4,8},{8,12},{12,16},{16,20},{20,24},{24,28},{28,0},{1,5},{5... | collective-permute-start | bytes 49160 | tf_op jit(solution)/shard_map/ppermute | solution.py:313
  18.1 5.7 %collective-permute-start.6 = (f32[160,128]{1,0:T(8,128)S(1)}, f32[160,128]{1,0:T(8,128)S(1)}, u32[]{:S(2)}, u32[]{:S(2)}) collective-permute-start(f32[160,128]{1,0:T(8,128)S(1)} %pad_maximum_fusion.1), channel_id=1, source_target_pairs={{4,0},{8,4},{12,8},{16,12},{20,16},{24,20},{28,24},{0,28},{5,1},{9... | collective-permute-start | bytes 245768 | tf_op jit(solution)/shard_map/ppermute | solution.py:314
